TPU v7x, 32 devices: a whole 2x2x4 slice. The times are simulated.
32 devices in a mesh: groups: 2 (over x), frames: 16 (over z, y, core).
Axes of the slice: x: 2, y: 2, z: 4, core: 2. Of those that a mesh axis runs over, the one named last changes fastest.
Arguments:
- video: bfloat16 [4, 16, 128, 1024], P('groups', 'frames'), parts along dimension 0, may hold values from -70 to 70
- w_qkv: bfloat16 [1024, 3072], replicated, may hold values from -8 to 8
- w_out: bfloat16 [1024, 1024], replicated, may hold values from -0.1875 to 0.1875
- keep_list: int32 [4, 16, 128], P('groups', 'frames'), parts along dimension 0, may hold values from 0 to 127, each once within a row
- kept_counts: int32 [4, 16], P('groups', 'frames'), parts along dimension 0, may hold values from 1 to 4, 32 in all within a row
- w_proj: bfloat16 [1024, 8192], P(None, 'frames'), may hold values from -20 to 20
- llm_gain: bfloat16 [8192], P('frames'), may hold values from 0.099609375 to 1.8984375
- w_gate: bfloat16 [8192, 16384], P(None, 'frames'), may hold values from -0.0625 to 0.0625
- w_up: bfloat16 [8192, 16384], P(None, 'frames'), may hold values from -0.0625 to 0.0625
Outputs:
- llm_hidden: bfloat16 [4, 32, 16384], P('groups', None, 'frames'), parts along dimension 0
There are 2 independent parts, one for each index of `groups`. A program takes and returns all parts, laid end to end along the dimension named above; an argument that names none is the same for every part. Nothing has to cross between parts.
Inputs may be any that keep to these rules, and one draw needn't show every extreme that they name: `keep_list`: each row of a frame lists every patch index once. `kept_counts`: the counts of one video sum to 32.
All inputs are finite; a program needn't handle non-finite values. No bound on the sum of `kept_counts` on one device may be relied on, other than what follows from the above.
Results may differ from a plain program's by a relative error of at most 0.0076.
Values may be sent and summed in bfloat16 or wider, within the bound.
No kernel may reach another device: no remote copies, remote signals or barrier semaphores. Data moves between devices by JAX's collectives and lax.ppermute only.
A program may use at most 128 MiB of HBM per device.

v0:
```python
import jax
import jax.numpy as jnp
from jax import lax
from jax.sharding import PartitionSpec as P

HEAD_DIM = 64
DL = 8192
TOKL = 2
KMAX = 4


NORM_EPS = 1e-05
SCORE_SCALE = 0.125


def layer_norm(values):
    floated = values.astype(jnp.float32)
    average = jnp.mean(floated, axis=-1, keepdims=True)
    centred = floated - average
    variance = jnp.mean(centred * centred, axis=-1, keepdims=True)
    return (centred * lax.rsqrt(variance + NORM_EPS)).astype(jnp.bfloat16)


def sequence_slots(counts, seq_len, slot_width):
    offsets = jnp.cumsum(counts, axis=1) - counts
    positions = lax.broadcasted_iota(jnp.int32, (counts.shape[0], seq_len), 1)
    started = (offsets[:, None, :] <= positions[:, :, None]).astype(jnp.int32)
    owner_frame = jnp.sum(started, axis=2) - 1
    frame_ids = lax.broadcasted_iota(jnp.int32, started.shape, 2)
    begin_at = jnp.sum(
        jnp.where(frame_ids == owner_frame[:, :, None], offsets[:, None, :], 0), axis=2
    )
    return owner_frame * slot_width + positions - begin_at


def temporal_attention(queries, keys_in, values_in):
    scores = (
        jnp.einsum("vfphe,vgphe->vphfg", queries, keys_in, preferred_element_type=jnp.float32)
        * SCORE_SCALE
    )
    largest = jnp.max(scores, axis=-1, keepdims=True)
    weights_exp = jnp.exp(scores - largest)
    weights = (weights_exp / jnp.sum(weights_exp, axis=-1, keepdims=True)).astype(jnp.bfloat16)
    return jnp.einsum(
        "vphfg,vgphe->vfphe", weights, values_in, preferred_element_type=jnp.float32
    ).astype(jnp.bfloat16)


def take_frame_rows(frame_rows, picks_row):
    return jnp.take(frame_rows, picks_row, axis=0)


def local(video, w_qkv, w_out, keep_list, kept_counts, w_proj, llm_gain, w_gate, w_up):
    videos = video.shape[0]
    patches = video.shape[2]
    model_width = video.shape[3]
    devices = lax.axis_size("frames")
    head_count = model_width // HEAD_DIM
    all_counts = lax.all_gather(kept_counts, "frames", axis=1, tiled=True)
    normed = layer_norm(video)

    def split_heads(tensor_in):
        return tensor_in.reshape(tensor_in.shape[:3] + (head_count, HEAD_DIM))

    received = lax.all_to_all(normed, "frames", split_axis=2, concat_axis=1, tiled=True)
    projected_here = jnp.dot(
        received.reshape(-1, model_width), w_qkv, preferred_element_type=jnp.float32
    ).astype(jnp.bfloat16)
    projected_here = projected_here.reshape(received.shape[:3] + (3 * model_width,))
    queries = split_heads(projected_here[..., :model_width])
    keys_in = split_heads(projected_here[..., model_width : 2 * model_width])
    values_in = split_heads(projected_here[..., 2 * model_width :])
    attended = temporal_attention(queries, keys_in, values_in)
    attended = attended.reshape(projected_here.shape[:3] + (model_width,))
    returned = lax.all_to_all(attended, "frames", split_axis=1, concat_axis=2, tiled=True)
    encoded = (
        video.astype(jnp.float32).reshape(-1, model_width)
        + jnp.dot(returned.reshape(-1, model_width), w_out, preferred_element_type=jnp.float32)
    ).astype(jnp.bfloat16)
    encoded = encoded.reshape(videos, patches, model_width)
    chosen = keep_list[:, 0, :KMAX]
    picked = jax.vmap(take_frame_rows)(encoded, chosen)
    slot_index = lax.broadcasted_iota(jnp.int32, (videos, KMAX), 1)
    live_slots = slot_index < kept_counts
    slot_rows = jnp.where(live_slots[:, :, None], picked, jnp.zeros_like(picked))
    gathered_slots = lax.all_gather(slot_rows, "frames", axis=1, tiled=True)
    sequence_order = sequence_slots(all_counts, devices * TOKL, KMAX)
    local_cols = jnp.dot(
        gathered_slots.reshape(-1, model_width), w_proj, preferred_element_type=jnp.float32
    )
    local_cols = local_cols.reshape(gathered_slots.shape[0], gathered_slots.shape[1], -1)
    squares = lax.psum(jnp.sum(local_cols * local_cols, axis=2), "frames")
    row_scale = lax.rsqrt(squares / DL + NORM_EPS)
    normed_cols = (local_cols * row_scale[:, :, None] * llm_gain.astype(jnp.float32)).astype(
        jnp.bfloat16
    )
    hidden_width = w_gate.shape[1]
    zero_sums = jnp.zeros(
        (gathered_slots.shape[0], gathered_slots.shape[1], hidden_width), jnp.float32
    )
    column_piece = lax.all_gather(normed_cols, "frames", axis=2, tiled=True)
    piece_width = column_piece.shape[2]
    flat_piece = column_piece.reshape(-1, piece_width)
    gate_more = jnp.dot(flat_piece, w_gate, preferred_element_type=jnp.float32).reshape(
        zero_sums.shape
    )
    up_more = jnp.dot(flat_piece, w_up, preferred_element_type=jnp.float32).reshape(zero_sums.shape)
    hidden_slots = (jax.nn.silu(gate_more) * up_more).astype(jnp.bfloat16)
    llm_hidden = jax.vmap(take_frame_rows)(hidden_slots, sequence_order)
    return llm_hidden


def solution(mesh):
    in_specs = (
        P("groups", "frames", None, None),
        P(),
        P(),
        P("groups", "frames", None),
        P("groups", "frames"),
        P(None, "frames"),
        P("frames"),
        P(None, "frames"),
        P(None, "frames"),
    )
    out_specs = P("groups", None, "frames")
    return jax.shard_map(local, mesh=mesh, in_specs=in_specs, out_specs=out_specs, check_vma=False)
```

profile of v0, /device:TPU:0, one launch (start us, length us, event | category | flops | bytes accessed | tf_op | source)
XLA Modules:
  0.0 195.9 jit_solution(10785479989955932589)
XLA Ops:
  6.5 1.7 convert_reduce_fusion
  8.3 1.9 multiply_reduce_fusion.1
  10.2 1.7 multiply_convert_fusion
  12.0 21.5 %all_to_all.8 = bf16[2,1,128,1024]{3,0,1,2:T(2,128)(2,1)S(1)} all-to-all(bf16[2,1,128,1024]{3,0,1,2:T(2,128)(2,1)S(1)} %multiply_convert_fusion), channel_id=1, replica_groups=mesh['groups'=2,'frames'=16] {'frames'}, dimensions={2} | all-to-all | bytes 1048576 | tf_op jit(solution)/shard_map/all_to_all | solution.py:65
  33.6 4.6 %convolution_convert_fusion = bf16[256,3072]{1,0:T(8,128)(2,1)S(1)} fusion(bf16[256,1024]{1,0:T(8,128)(2,1)S(1)} %bitcast.65, bf16[1024,3072]{1,0:T(8,128)(2,1)} %param.10), kind=kOutput, calls=%fused_computation.7 | convolution fusion | flops 1611399168 | bytes 8388608 | tf_op jit(solution)/shard_map/dot_general | solution.py:66
  39.1 2.5 %reshape.177 = bf16[2,16,8,16,64]{4,3,2,1,0:T(8,128)(2,1)} reshape(bf16[2,16,8,1024]{3,2,1,0:T(8,128)(2,1)} %get-tuple-element.7) | data formatting | bytes 1048576 | tf_op jit(solution)/shard_map/reshape | solution.py:63
  41.6 1.6 reshape.178
  43.2 1.6 reshape.176
  44.9 4.9 %fusion.43 = (f32[2,8,16,16]{3,2,1,0:T(8,128)S(1)}, f32[2,8,16,16,16]{3,4,2,1,0:T(8,128)}) fusion(bf16[2,16,8,16,64]{4,3,2,1,0:T(8,128)(2,1)} %reshape.178, bf16[2,16,8,16,64]{4,3,2,1,0:T(8,128)(2,1)} %reshape.177), kind=kOutput, calls=%fused_computation.62 | convolution fusion | flops 8585231 | bytes 1327104 | tf_op jit(solution)/shard_map/sub | solution.py:42
  49.8 2.5 %fusion.6 = bf16[2,16,8,16,64]{4,1,3,2,0:T(8,128)(2,1)S(1)} fusion(f32[2,8,16,16,16]{3,4,2,1,0:T(8,128)} %get-tuple-element.9, bf16[2,16,8,16,64]{4,3,2,1,0:T(8,128)(2,1)S(1)} %copy-done.3, f32[2,8,16,16]{3,2,1,0:T(8,128)S(1)} %get-tuple-element.8), kind=kOutput, calls=%fused_computation.13 | convolution fusion | flops 8781824 | bytes 1327104 | tf_op jit(solution)/shard_map/vphfg,vgphe->vfphe/dot_general | solution.py:44
  52.3 1.3 copy.73
  53.5 2.6 %reshape.201 = bf16[2,16,8,1024]{3,2,0,1:T(8,128)(2,1)} reshape(bf16[2,16,8,16,64]{4,3,2,0,1:T(8,128)(2,1)} %copy.73) | data formatting | bytes 1048576 | tf_op jit(solution)/shard_map/reshape | solution.py:74
  56.1 4.2 %all-to-all-start.1 = ((bf16[2,16,8,1024]{3,2,0,1:T(8,128)(2,1)}), bf16[2,16,8,1024]{3,2,0,1:T(8,128)(2,1)}, u32[]{:S(2)}, u32[]{:S(2)}) async-start(bf16[2,16,8,1024]{3,2,0,1:T(8,128)(2,1)} %reshape.201), calls=%async_computation.1 | async-start | bytes 1048576 | tf_op jit(solution)/shard_map/all_to_all | solution.py:75
  61.8 12.9 %all-to-all-done.1 = bf16[2,16,8,1024]{3,2,0,1:T(8,128)(2,1)} async-done(((bf16[2,16,8,1024]{3,2,0,1:T(8,128)(2,1)}), bf16[2,16,8,1024]{3,2,0,1:T(8,128)(2,1)}, u32[]{:S(2)}, u32[]{:S(2)}) %all-to-all-start.1) | async-done | bytes 524320 | tf_op jit(solution)/shard_map/all_to_all | solution.py:75
  75.8 1.5 fusion.7
  77.3 1.3 gather_fusion
  78.7 20.6 %all_gather.10 = bf16[2,64,1024]{2,0,1:T(2,128)(2,1)S(1)} all-gather(bf16[2,4,1024]{2,0,1:T(2,128)(2,1)S(1)} %broadcast_select_fusion.2), channel_id=1, replica_groups=mesh['groups'=2,'frames'=16] {'frames'}, dimensions={1}, use_global_device_ids=true | all-gather | bytes 278528 | tf_op jit(solution)/shard_map/all_gather | solution.py:86
  99.3 1.6 multiply_reduce_fusion.2
  100.9 29.8 %psum.7 = f32[2,64]{1,0:T(2,128)S(1)} all-reduce(f32[2,64]{1,0:T(2,128)S(1)} %get-tuple-element.10), channel_id=1, replica_groups=mesh['groups'=2,'frames'=16] {'frames'}, use_global_device_ids=true, to_apply=%region_8.9 | all-reduce | flops 128 | bytes 1024 | tf_op jit(solution)/shard_map/psum | solution.py:92
  131.5 17.1 %all-gather = s32[16,1,2]{2,1,0:T(1,128)S(1)} all-gather(s32[1,1,2]{2,1,0:T(1,128)S(1)} %bitcast.70), channel_id=1, replica_groups=mesh['groups'=2,'frames'=16] {'frames'}, dimensions={0}, use_global_device_ids=true | all-gather | bytes 136 | tf_op jit(solution)/shard_map/all_gather | solution.py:59
  149.2 20.7 %all-gather.3.cloned.1.call-done = bf16[2,64,8192]{2,1,0:T(8,128)(2,1)} async-done(((bf16[2,64,512]{2,1,0:T(8,128)(2,1)}), bf16[2,64,8192]{2,1,0:T(8,128)(2,1)}) %all-gather.3.cloned.1.call-update) | async-done | bytes 2097168 | tf_op jit(solution)/shard_map/all_gather | solution.py:101
  169.9 8.9 %fusion.3 = f32[2,64,1024]{2,1,0:T(8,128)S(1)} fusion(bf16[2,64,8192]{2,1,0:T(8,128)(2,1)} %all-gather.3.cloned.1.call-done, bf16[8192,1024]{1,0:T(8,128)(2,1)} %param.16), kind=kOutput, calls=%fused_computation.5 | convolution fusion | flops 2147483648 | bytes 19398656 | tf_op jit(solution)/shard_map/dot_general | solution.py:104
  178.8 8.3 %fusion.11 = bf16[2,64,1024]{2,1,0:T(8,128)(2,1)S(1)} fusion(bf16[2,64,8192]{2,1,0:T(8,128)(2,1)S(1)} %copy-done.1, bf16[8192,1024]{1,0:T(8,128)(2,1)} %param.17, f32[2,64,1024]{2,1,0:T(8,128)S(1)} %fusion.3), kind=kOutput, calls=%fused_computation.17 | convolution fusion | flops 2148270080 | bytes 19660800 | tf_op jit(solution)/shard_map/dot_general | solution.py:107
  187.2 1.1 gather_fusion.1
  (43 shorter events, 5.7 us)
Async XLA Ops:
  6.5 69.2 %copy-start = (bf16[1024,1024]{1,0:T(8,128)(2,1)S(1)}, bf16[1024,1024]{1,0:T(8,128)(2,1)}, u32[]{:S(2)}) copy-start(bf16[1024,1024]{1,0:T(8,128)(2,1)} %param.11) | copy-start | bytes 6291460
  44.9 4.9 %copy-start.3 = (bf16[2,16,8,16,64]{4,3,2,1,0:T(8,128)(2,1)S(1)}, bf16[2,16,8,16,64]{4,3,2,1,0:T(8,128)(2,1)}, u32[]{:S(2)}) copy-start(bf16[2,16,8,16,64]{4,3,2,1,0:T(8,128)(2,1)} %reshape.176) | copy-start | bytes 1572868
  52.2 8.4 %copy-start.2 = (bf16[2,1,128,1024]{3,2,1,0:T(8,128)(2,1)S(1)}, bf16[2,1,128,1024]{3,2,1,0:T(8,128)(2,1)}, u32[]{:S(2)}) copy-start(bf16[2,1,128,1024]{3,2,1,0:T(8,128)(2,1)} %param.9) | copy-start | bytes 1572868
  56.1 18.5 %all-to-all-start.1 = ((bf16[2,16,8,1024]{3,2,0,1:T(8,128)(2,1)}), bf16[2,16,8,1024]{3,2,0,1:T(8,128)(2,1)}, u32[]{:S(2)}, u32[]{:S(2)}) async-start(bf16[2,16,8,1024]{3,2,0,1:T(8,128)(2,1)} %reshape.201), calls=%async_computation.1 | async-start | bytes 1048576 | tf_op jit(solution)/shard_map/all_to_all | solution.py:75
  60.4 1.2 copy-start.5
  60.4 1.4 copy-start.4
  60.4 1.4 copy-start.6
  60.4 109.5 %all-gather.3.cloned.1.call-start = ((), (), s32[]{:S(2)}) async-start(), calls=%async_computation.2 | async-start | bytes 2228224 | tf_op jit(solution)/shard_map/all_gather | solution.py:101
  169.9 8.9 %copy-start.1 = (bf16[2,64,8192]{2,1,0:T(8,128)(2,1)S(1)}, bf16[2,64,8192]{2,1,0:T(8,128)(2,1)}, u32[]{:S(2)}) copy-start(bf16[2,64,8192]{2,1,0:T(8,128)(2,1)} %all-gather.3.cloned.1.call-done) | copy-start | bytes 6291460
Sparse Core Ops, SparseCore 0:
  131.6 38.2 all-gather.2
where the time goes:
time: 197 us; the launch traced here: 196 us
  blocking collectives  89 us (45%)
  waiting for transfers between devices  33.6 us (17%)
  matrix products  32.3 us (16%)
  local copies, waits for them, and re-layouts  14.9 us (8%)
  between operations  13.6 us (7%)
  other arithmetic  7.99 us (4%)
  starting transfers between devices  4.46 us (2%)
    psum x1, blocking collectives, local(): squares = lax.psum(jnp.sum(local_cols * local_cols, axis=2), 'frames')  29.8 us
    all_to_all x1, blocking collectives, local(): lax.all_to_all(normed, 'frames', split_axis=2, concat_axis=1, tiled=True)  21.5 us
    all_gather x1, waiting for transfers between devices, local(): column_piece = lax.all_gather(normed_cols, 'frames', axis=2, tiled=True)  20.7 us
    all_gather x1, blocking collectives, local(): gathered_slots = lax.all_gather(slot_rows, 'frames', axis=1, tiled=True)  20.6 us
    all_gather x1, blocking collectives, local(): all_counts = lax.all_gather(kept_counts, 'frames', axis=1, tiled=True)  17.1 us
    all_to_all x1, waiting for transfers between devices, local(): lax.all_to_all(attended, 'frames', split_axis=1, concat_axis=2, tiled=True)  12.9 us
    dot_general x1, matrix products, local(): jnp.dot(flat_piece, w_gate, preferred_element_type=jnp.float32)  8.87 us
    dot_general x1, matrix products, local(): jnp.dot(flat_piece, w_up, preferred_element_type=jnp.float32)  8.34 us
  transfers between devices with their start and end apart: 2, of which 2 were waited for; matrix products, arithmetic and copies ran while one was open for 1% of the time, Pallas kernels for 0%

commit v1 on v0

v1 whole, which is shorter than its diff:
```python
import functools

import jax
import jax.numpy as jnp
from jax import lax
from jax.experimental import pallas as pl
from jax.experimental.pallas import tpu as pltpu
from jax.sharding import Mesh
from jax.sharding import PartitionSpec as P

HEAD_DIM = 64
TOKL = 2
KMAX = 4
LANES = 128
NORM_EPS = 1e-05
SCORE_SCALE = 0.125
MIB = 1 << 20
F32 = jnp.float32
BF16 = jnp.bfloat16


def dot32(left, right):
    return jnp.dot(left, right, preferred_element_type=F32)


def swap_halves(values):
    rows = values.shape[-2] // 2
    return jnp.concatenate([values[..., rows:, :], values[..., :rows, :]], axis=-2)


def whole(space=pltpu.VMEM):
    return pl.BlockSpec(memory_space=space)


def params(limit):
    return pltpu.CompilerParams(vmem_limit_bytes=int(limit))


def index_kernel(counts_ref, keep_ref, gain_ref, out_ref):
    videos = keep_ref.shape[0]
    lane = lax.broadcasted_iota(jnp.int32, (1, LANES), 1)
    rows = []
    for v in range(videos):
        listed = keep_ref[v, :, :LANES].astype(F32)
        rows.append(jnp.where(lane == KMAX, counts_ref[v, 0].astype(F32), listed))
    gain = gain_ref[...].astype(F32)
    width = gain.shape[1]
    for start in range(0, width, LANES):
        piece = gain[:, start : start + LANES]
        if piece.shape[1] < LANES:
            piece = jnp.concatenate([piece, jnp.ones((1, LANES - piece.shape[1]), F32)], axis=1)
        rows.append(piece)
    while len(rows) < out_ref.shape[1]:
        rows.append(jnp.zeros((1, LANES), F32))
    message = jnp.concatenate(rows, axis=0)
    out_ref[...] = jnp.broadcast_to(message[None], out_ref.shape)


def select_kernel(index_ref, video_ref, out_ref):
    frames = index_ref.shape[0]
    videos, _, patches, width = video_ref.shape
    seq = frames * TOKL
    half = width // 2
    own = out_ref.shape[1] // 2
    row = lax.broadcasted_iota(jnp.int32, (frames, frames), 0)
    col = lax.broadcasted_iota(jnp.int32, (frames, frames), 1)
    before = (col < row).astype(BF16)
    token = lax.broadcasted_iota(jnp.int32, (frames, seq), 1)
    patch = lax.broadcasted_iota(jnp.int32, (frames, patches), 1).astype(F32)
    for v in range(videos):
        table = index_ref[:, v, :]
        count = table[:, KMAX : KMAX + 1]
        offset = dot32(before, jnp.broadcast_to(count, (frames, LANES)).astype(BF16))[:, :1]
        place = token.astype(F32) - offset
        at_token, at_patch = [], []
        for s in range(KMAX):
            live = jnp.logical_and(place == s, count > s)
            at_token.append(jnp.where(live, 1.0, 0.0))
            at_patch.append(jnp.where(table[:, s : s + 1] == patch, 1.0, 0.0))
        at_token = jnp.concatenate(at_token, axis=0).astype(BF16)
        at_patch = jnp.concatenate(at_patch, axis=0).astype(BF16)
        chosen = lax.dot_general(
            at_token, at_patch, (((0,), (0,)), ((), ())), preferred_element_type=F32
        ).astype(BF16)
        taken = dot32(chosen, video_ref[v, 0]).astype(BF16)
        base = v * seq
        for peer in range(base // own, (base + seq) // own):
            first = peer * own - base
            rows = taken[first : first + own]
            out_ref[peer] = jnp.concatenate([rows[:, :half], rows[:, half:]], axis=0)


def attend_kernel(me_ref, index_ref, rows_ref, w_qkv_ref, w_out_ref, out_ref):
    frames, packed, half = rows_ref.shape
    own = packed // 2
    width = 2 * half
    heads = width // HEAD_DIM
    seq = frames * TOKL
    videos = frames * own // seq
    raw = rows_ref[...].astype(F32)

    def feature_mean(values):
        part = jnp.sum(values, axis=-1, keepdims=True)
        return (part + swap_halves(part)) / width

    centred = raw - feature_mean(raw)
    variance = feature_mean(centred * centred)
    normed = (centred * lax.rsqrt(variance + NORM_EPS)).astype(BF16).reshape(-1, half)

    def project(start):
        low = dot32(normed, w_qkv_ref[:half, start : start + width])
        high = dot32(normed, w_qkv_ref[half:, start : start + width])
        low = low.reshape(frames, packed, width)
        high = high.reshape(frames, packed, width)
        return (low + swap_halves(high)).astype(BF16).astype(F32)

    table = index_ref[...]
    row = lax.broadcasted_iota(jnp.int32, (1, packed, 1), 1)
    flat = me_ref[0] * own + jnp.where(row >= own, row - own, row)
    owner = jnp.zeros((frames, packed, 1), jnp.bool_)
    for v in range(videos):
        count = table[:, v : v + 1, KMAX : KMAX + 1]
        upto = count
        step = 1
        while step < frames:
            moved = jnp.concatenate([jnp.zeros((step, 1, 1), F32), upto[:-step]], axis=0)
            upto = upto + moved
            step *= 2
        place = (flat - v * seq).astype(F32)
        inside = jnp.logical_and(place >= upto - count, place < upto)
        ours = jnp.logical_and(flat >= v * seq, flat < (v + 1) * seq)
        owner = jnp.logical_or(owner, jnp.logical_and(inside, ours))

    def of_owner(values):
        return jnp.sum(jnp.where(owner, values, 0.0), axis=0)

    query = of_owner(project(0))
    product = (project(width) * query[None]).reshape(-1, width)
    feature = lax.broadcasted_iota(jnp.int32, (width, LANES), 0) // HEAD_DIM
    head = lax.broadcasted_iota(jnp.int32, (width, LANES), 1)
    to_head = jnp.where(feature == head, 1.0, 0.0).astype(BF16)
    coarse = product.astype(BF16)
    rest = product - coarse.astype(F32)
    fine = rest.astype(BF16)
    last = (rest - fine.astype(F32)).astype(BF16)
    scores = dot32(coarse, to_head) + dot32(fine, to_head) + dot32(last, to_head)
    scores = scores.reshape(frames, packed, LANES) * SCORE_SCALE
    raised = jnp.exp(scores - jnp.max(scores, axis=0, keepdims=True))
    weights = (raised / jnp.sum(raised, axis=0, keepdims=True)).astype(BF16)
    head = lax.broadcasted_iota(jnp.int32, (LANES, width), 0)
    feature = lax.broadcasted_iota(jnp.int32, (LANES, width), 1) // HEAD_DIM
    from_head = jnp.where(feature == head, 1.0, 0.0).astype(BF16)
    spread = dot32(weights.reshape(-1, LANES), from_head).reshape(frames, packed, width)
    attended = jnp.sum(spread * project(2 * width), axis=0).astype(BF16)
    change = dot32(attended, w_out_ref[...])
    place = lax.broadcasted_iota(jnp.int32, (packed, half), 0)
    change = jnp.where(place < own, change[:, :half], swap_halves(change[:, half:]))
    encoded = (of_owner(raw) + change).astype(BF16)
    out_ref[...] = jnp.broadcast_to(encoded[None], out_ref.shape)


def project_kernel(rows_ref, w_proj_ref, gain_ref, out_ref):
    frames, packed, half = rows_ref.shape
    own = packed // 2
    tokens = frames * own
    columns = w_proj_ref.shape[1]
    rows = rows_ref[...].reshape(frames * packed, half)
    token = lax.broadcasted_iota(jnp.int32, (tokens, frames * packed), 0)
    source = lax.broadcasted_iota(jnp.int32, (tokens, frames * packed), 1)
    first = (token // own) * packed + token % own
    low = dot32(jnp.where(source == first, 1.0, 0.0).astype(BF16), rows).astype(BF16)
    high = dot32(jnp.where(source == first + own, 1.0, 0.0).astype(BF16), rows).astype(BF16)
    total = dot32(low, w_proj_ref[:half, :]) + dot32(high, w_proj_ref[half:, :])
    gained = (total * gain_ref[...].astype(F32)).astype(BF16)
    out_ref[...] = jnp.broadcast_to(gained[None], out_ref.shape)


def hidden_kernel(index_ref, rows_ref, w_gate_ref, w_up_ref, out_ref, joined):
    cores, chips, tokens, columns = rows_ref.shape
    depth = cores * chips * columns
    first = index_ref.shape[1]
    gain_rows = -(-columns // LANES)
    videos = out_ref.shape[0]
    squares = jnp.zeros((tokens, 1), F32)
    for chip in range(chips):
        for core in range(cores):
            place = chip * cores + core
            piece = rows_ref[core, chip]
            joined[:, place * columns : (place + 1) * columns] = piece
            for r in range(gain_rows):
                part = piece[:, r * LANES : (r + 1) * LANES].astype(F32)
                gain = index_ref[place, videos + r : videos + r + 1, : part.shape[1]]
                part = part / gain
                squares = squares + jnp.sum(part * part, axis=1, keepdims=True)
    scale = lax.rsqrt(squares / depth + NORM_EPS)
    width = out_ref.shape[2]
    block = min(width, 256)

    for start in range(0, width, block):
        gate = dot32(joined[...], w_gate_ref[:, start : start + block]) * scale
        up = dot32(joined[...], w_up_ref[:, start : start + block]) * scale
        hidden = (jax.nn.silu(gate) * up).astype(BF16)
        out_ref[:, :, start : start + block] = hidden.reshape(videos, -1, block)


def local(video, w_qkv, w_out, keep_list, kept_counts, w_proj, llm_gain, w_gate, w_up):
    videos, _, patches, width = video.shape
    chips, cores = lax.axis_size("chips"), lax.axis_size("cores")
    frames = chips * cores
    axes = ("chips", "cores")
    seq = frames * TOKL
    tokens = videos * seq
    packed = 2 * (tokens // frames)
    half = width // 2
    columns = w_proj.shape[1]
    me = lax.axis_index(axes).astype(jnp.int32).reshape(1)
    spread = functools.partial(lax.all_to_all, split_axis=0, concat_axis=0, tiled=True)

    message_rows = -(-(videos + -(-columns // LANES)) // 8) * 8
    message = pl.pallas_call(
        index_kernel,
        out_shape=jax.ShapeDtypeStruct((frames, message_rows, LANES), F32),
        in_specs=[whole(pltpu.SMEM), whole(), whole()],
        out_specs=whole(),
        compiler_params=params(2 * MIB),
        name="index",
    )(kept_counts, keep_list, llm_gain.reshape(1, -1))
    index = spread(message, axes)

    chosen = pl.pallas_call(
        select_kernel,
        out_shape=jax.ShapeDtypeStruct((frames, packed, half), BF16),
        in_specs=[whole(), whole()],
        out_specs=whole(),
        compiler_params=params(4 * MIB + 8 * tokens * width),
        name="select",
    )(index, video)
    seen = spread(chosen, axes)

    encoded = pl.pallas_call(
        attend_kernel,
        out_shape=jax.ShapeDtypeStruct((frames, packed, half), BF16),
        in_specs=[whole(pltpu.SMEM), whole(), whole(), whole(), whole()],
        out_specs=whole(),
        compiler_params=params(12 * MIB + 24 * frames * packed * width),
        name="attend",
    )(me, index, seen, w_qkv, w_out)
    token_rows = spread(encoded, axes)

    gained = pl.pallas_call(
        project_kernel,
        out_shape=jax.ShapeDtypeStruct((chips, tokens, columns), BF16),
        in_specs=[whole(), whole(), whole()],
        out_specs=whole(),
        compiler_params=params(6 * MIB + 4 * tokens * chips * columns),
        name="project",
    )(token_rows, w_proj, llm_gain.reshape(1, -1))
    mine = spread(gained, "chips")
    rows = lax.all_gather(mine, "cores", axis=0)

    return pl.pallas_call(
        hidden_kernel,
        out_shape=jax.ShapeDtypeStruct((videos, seq, w_gate.shape[1]), BF16),
        in_specs=[whole(), whole(), whole(), whole()],
        out_specs=whole(),
        scratch_shapes=[pltpu.VMEM((tokens, w_gate.shape[0]), BF16)],
        compiler_params=params(52 * MIB),
        name="hidden",
    )(index, rows, w_gate, w_up)


def solution(mesh):
    groups, frames = mesh.devices.shape
    cores = 2 if frames % 2 == 0 else 1
    split = Mesh(mesh.devices.reshape(groups, frames // cores, cores), ("groups", "chips", "cores"))
    spread = ("chips", "cores")
    in_specs = (
        P("groups", spread, None, None),
        P(),
        P(),
        P("groups", spread, None),
        P("groups", spread),
        P(None, spread),
        P(spread),
        P(None, spread),
        P(None, spread),
    )
    out_specs = P("groups", None, spread)
    return jax.shard_map(local, mesh=split, in_specs=in_specs, out_specs=out_specs, check_vma=False)
```

time: 197 us -> 108 us (0.55)
  blocking collectives: 89 us -> 41.9 us
  matrix products: 32.3 us -> 0 us
  Pallas kernels: 0 us -> 22.3 us
  waiting for transfers between devices: 33.6 us -> 16.1 us
  other arithmetic: 7.99 us -> 0 us
  local copies, waits for them, and re-layouts: 14.9 us -> 9.97 us
    all_gather x2 -> x0, blocking collectives: 37.7 us -> none  [the longest x1 20.6 us: local(): gathered_slots = lax.all_gather(slot_rows, 'frames', axis=1, tiled=True)]
    psum x1 -> x0, blocking collectives: 29.8 us -> none  [local(): squares = lax.psum(jnp.sum(local_cols * local_cols, axis=2), 'frames')]
    dot_general x6 -> x0, matrix products: 27.4 us -> none  [the longest x1 8.87 us: local(): jnp.dot(flat_piece, w_gate, preferred_element_type=jnp.float32)]
    pallas_call x0 -> x5, Pallas kernels: none -> 22.3 us  [the longest x1 17.3 us: local(): pl.pallas_call(hidden_kernel, out_shape=jax.ShapeDtypeStruct((videos, seq...]
    all_to_all x1 -> x3, blocking collectives: 21.5 us -> 41.9 us  [the longest x1 17.3 us: local(): mine = spread(gained, 'chips')]
    all_gather x1, waiting for transfers between devices: 20.7 us -> 8.23 us  [local(): rows = lax.all_gather(mine, 'cores', axis=0)]
    unnamed x14 -> x13, local copies, waits for them, and re-layouts: 0.04 us -> 9.28 us
    reshape x5 -> x1, local copies, waits for them, and re-layouts: 9.63 us -> 0.68 us  [local(): llm_gain.reshape(1, -1)]
  transfers between devices with their start and end apart: 2 -> 2, of which waited for: 2 -> 2; matrix products, arithmetic and copies ran while one was open for 1% -> 0% of each run, Pallas kernels for 0% -> 0%
where the time goes in v1:
time: 108 us; the launch traced here: 107 us
  blocking collectives  41.9 us (39%)
  Pallas kernels  22.3 us (21%)
  waiting for transfers between devices  16.1 us (15%)
  between operations  13.4 us (12%)
  local copies, waits for them, and re-layouts  9.97 us (9%)
  starting transfers between devices  3.55 us (3%)
    all_to_all x1, blocking collectives, local(): mine = spread(gained, 'chips')  17.3 us
    pallas_call x1, Pallas kernels, local(): pl.pallas_call(hidden_kernel, out_shape=jax.ShapeDtypeStruct((videos, seq...  17.3 us
    all_to_all x1, blocking collectives, local(): index = spread(message, axes)  14.1 us
    all_to_all x1, blocking collectives, local(): token_rows = spread(encoded, axes)  10.5 us
    unnamed x13, local copies, waits for them, and re-layouts  9.28 us
    all_gather x1, waiting for transfers between devices, local(): rows = lax.all_gather(mine, 'cores', axis=0)  8.23 us
    all_to_all x1, waiting for transfers between devices, local(): seen = spread(chosen, axes)  7.82 us
    all_to_all x1, starting transfers between devices, local(): seen = spread(chosen, axes)  3.51 us
  transfers between devices with their start and end apart: 2, of which 2 were waited for; matrix products, arithmetic and copies ran while one was open for 0% of the time, Pallas kernels for 0%

profile of v1, /device:TPU:0, one launch (start us, length us, event | category | flops | bytes accessed | tf_op | source)
XLA Modules:
  0.0 107.2 jit_solution(1516507750117522022)
XLA Ops:
  6.5 0.7 copy.11.counts_ref
  7.3 0.7 reshape.7.gain_ref
  8.0 0.0 copy-start.5
  8.0 0.7 copy-done.5
  8.6 0.6 index.1
  9.2 14.1 %all_to_all.20.index_ref = f32[16,8,128]{2,1,0:T(8,128)S(1)} all-to-all(f32[16,8,128]{2,1,0:T(8,128)S(1)} %index.1), channel_id=1, replica_groups=mesh['groups'=2,'chips'=8,'cores'=2] {'chips','cores'}, dimensions={0} | all-to-all | bytes 131072 | tf_op jit(solution)/shard_map/all_to_all | solution.py:228
  23.3 0.0 copy-start.4
  23.3 1.0 copy-done.4
  24.4 1.6 %select.1 = bf16[16,8,512]{2,1,0:T(8,128)(2,1)} custom-call(f32[16,8,128]{2,1,0:T(8,128)S(1)} %all_to_all.20.index_ref, bf16[2,1,128,1024]{3,2,1,0:T(8,128)(2,1)S(1)} %copy-done.4), custom_call_target="tpu_custom_call" | custom-call | tf_op jit(solution)/shard_map/select/pallas_call | solution.py:230
  26.0 3.5 %all-to-all-start.1 = ((bf16[16,8,512]{2,1,0:T(8,128)(2,1)}), bf16[16,8,512]{2,1,0:T(8,128)(2,1)S(1)}, u32[]{:S(2)}, u32[]{:S(2)}) async-start(bf16[16,8,512]{2,1,0:T(8,128)(2,1)} %select.1), calls=%async_computation.1 | async-start | bytes 262144 | tf_op jit(solution)/shard_map/all_to_all | solution.py:238
  29.5 0.0 all-gather.3.cloned.1.call-start
  29.6 7.8 %all-to-all-done.1.rows_ref = bf16[16,8,512]{2,1,0:T(8,128)(2,1)S(1)} async-done(((bf16[16,8,512]{2,1,0:T(8,128)(2,1)}), bf16[16,8,512]{2,1,0:T(8,128)(2,1)S(1)}, u32[]{:S(2)}, u32[]{:S(2)}) %all-to-all-start.1) | async-done | bytes 131104 | tf_op jit(solution)/shard_map/all_to_all | solution.py:238
  37.4 0.0 copy-start
  37.4 2.8 %copy-done = bf16[1024,3072]{1,0:T(8,128)(2,1)S(1)} copy-done((bf16[1024,3072]{1,0:T(8,128)(2,1)S(1)}, bf16[1024,3072]{1,0:T(8,128)(2,1)}, u32[]{:S(2)}) %copy-start) | copy-done | bytes 6291480
  40.2 1.6 %copy-done.1 = bf16[1024,1024]{1,0:T(8,128)(2,1)S(1)} copy-done((bf16[1024,1024]{1,0:T(8,128)(2,1)S(1)}, bf16[1024,1024]{1,0:T(8,128)(2,1)}, u32[]{:S(2)}) %copy-start.1) | copy-done | bytes 2097176
  41.8 2.3 %attend.1 = bf16[16,8,512]{2,1,0:T(8,128)(2,1)S(1)} custom-call(s32[1]{0:T(128)} %bitcast.me_ref, f32[16,8,128]{2,1,0:T(8,128)S(1)} %all_to_all.20.index_ref, bf16[16,8,512]{2,1,0:T(8,128)(2,1)S(1)} %all-to-all-done.1.rows_ref, bf16[1024,3072]{1,0:T(8,128)(2,1)S(1)} %copy-done, bf16[1024,1024]{1,0:T(8,128)(2,1)S(1)} %copy-done.1), custom_call_target="tpu_custom_call" | custom-call | tf_op jit(solution)/shard_map/attend/pallas_call | solution.py:240
  44.1 10.5 %all_to_all.21.rows_ref = bf16[16,8,512]{2,1,0:T(8,128)(2,1)S(1)} all-to-all(bf16[16,8,512]{2,1,0:T(8,128)(2,1)S(1)} %attend.1), channel_id=1, replica_groups=mesh['groups'=2,'chips'=8,'cores'=2] {'chips','cores'}, dimensions={0} | all-to-all | bytes 262144 | tf_op jit(solution)/shard_map/all_to_all | solution.py:248
  54.6 1.2 %copy-done.3 = bf16[1024,512]{1,0:T(8,128)(2,1)S(1)} copy-done((bf16[1024,512]{1,0:T(8,128)(2,1)S(1)}, bf16[1024,512]{1,0:T(8,128)(2,1)}, u32[]{:S(2)}) %copy-start.3) | copy-done | bytes 1048600
  55.8 0.4 project.1
  56.3 17.3 %all_to_all.22 = bf16[8,64,512]{2,1,0:T(8,128)(2,1)} all-to-all(bf16[8,64,512]{2,1,0:T(8,128)(2,1)S(1)} %project.1), channel_id=1, replica_groups=mesh['groups'=2,'chips'=8,'cores'=2] {'chips'}, dimensions={0} | all-to-all | bytes 1048576 | tf_op jit(solution)/shard_map/all_to_all | solution.py:258
  73.6 0.0 all-gather.3.cloned.1.call-update
  73.6 8.2 %all-gather.3.cloned.1.call-done = bf16[16,64,512]{2,1,0:T(8,128)(2,1)} async-done(((bf16[8,64,512]{2,1,0:T(8,128)(2,1)}), bf16[16,64,512]{2,1,0:T(8,128)(2,1)}) %all-gather.3.cloned.1.call-update) | async-done | bytes 1048592 | tf_op jit(solution)/shard_map/all_gather | solution.py:259
  81.9 1.2 %copy-done.2 = bf16[16,64,512]{2,1,0:T(8,128)(2,1)S(1)} copy-done((bf16[16,64,512]{2,1,0:T(8,128)(2,1)S(1)}, bf16[16,64,512]{2,1,0:T(8,128)(2,1)}, u32[]{:S(2)}) %copy-start.2) | copy-done | bytes 1048600
  83.1 17.3 %hidden.1 = bf16[2,32,1024]{2,1,0:T(8,128)(2,1)} custom-call(f32[16,8,128]{2,1,0:T(8,128)S(1)} %all_to_all.20.index_ref, bf16[2,8,64,512]{3,2,1,0:T(8,128)(2,1)S(1)} %bitcast.2, bf16[8192,1024]{1,0:T(8,128)(2,1)} %w_gate_ref.1, bf16[8192,1024]{1,0:T(8,128)(2,1)} %w_up_ref.1), custom_call_target="tpu_custom_call" | custom-call | tf_op jit(solution)/shard_map/hidden/pallas_call | solution.py:261
  (3 shorter events, 0.0 us)
Async XLA Ops:
  8.0 0.7 copy-start.5
  23.3 1.0 copy-start.4
  26.0 11.4 %all-to-all-start.1 = ((bf16[16,8,512]{2,1,0:T(8,128)(2,1)}), bf16[16,8,512]{2,1,0:T(8,128)(2,1)S(1)}, u32[]{:S(2)}, u32[]{:S(2)}) async-start(bf16[16,8,512]{2,1,0:T(8,128)(2,1)} %select.1), calls=%async_computation.1 | async-start | bytes 262144 | tf_op jit(solution)/shard_map/all_to_all | solution.py:238
  29.5 52.3 %all-gather.3.cloned.1.call-start = ((), (), s32[]{:S(2)}) async-start(), calls=%async_computation.4 | async-start | bytes 1572864 | tf_op jit(solution)/shard_map/all_gather | solution.py:259
  37.4 2.8 %copy-start = (bf16[1024,3072]{1,0:T(8,128)(2,1)S(1)}, bf16[1024,3072]{1,0:T(8,128)(2,1)}, u32[]{:S(2)}) copy-start(bf16[1024,3072]{1,0:T(8,128)(2,1)} %w_qkv_ref.1) | copy-start | bytes 18874372
  40.2 1.6 %copy-start.1 = (bf16[1024,1024]{1,0:T(8,128)(2,1)S(1)}, bf16[1024,1024]{1,0:T(8,128)(2,1)}, u32[]{:S(2)}) copy-start(bf16[1024,1024]{1,0:T(8,128)(2,1)} %w_out_ref.1) | copy-start | bytes 6291460
  54.6 1.2 %copy-start.3 = (bf16[1024,512]{1,0:T(8,128)(2,1)S(1)}, bf16[1024,512]{1,0:T(8,128)(2,1)}, u32[]{:S(2)}) copy-start(bf16[1024,512]{1,0:T(8,128)(2,1)} %w_proj_ref.1) | copy-start | bytes 3145732
  81.9 1.2 %copy-start.2 = (bf16[16,64,512]{2,1,0:T(8,128)(2,1)S(1)}, bf16[16,64,512]{2,1,0:T(8,128)(2,1)}, u32[]{:S(2)}) copy-start(bf16[16,64,512]{2,1,0:T(8,128)(2,1)} %all-gather.3.cloned.1.call-done) | copy-start | bytes 3145732
Sparse Core Ops, SparseCore 0:
  73.8 8.0 all-gather.2

commit v2 on v1

--- a/solution.py
+++ b/solution.py
@@ -36,22 +36,22 @@
     return pltpu.CompilerParams(vmem_limit_bytes=int(limit))
 
 
-def index_kernel(counts_ref, keep_ref, gain_ref, out_ref):
+def index_kernel(me_ref, counts_ref, keep_ref, gain_ref, out_ref):
+    del me_ref
     videos = keep_ref.shape[0]
     lane = lax.broadcasted_iota(jnp.int32, (1, LANES), 1)
     rows = []
     for v in range(videos):
         listed = keep_ref[v, :, :LANES].astype(F32)
-        rows.append(jnp.where(lane == KMAX, counts_ref[v, 0].astype(F32), listed))
+        rows.append(jnp.where(lane == KMAX, counts_ref[0, v].astype(F32), listed))
     gain = gain_ref[...].astype(F32)
-    width = gain.shape[1]
-    for start in range(0, width, LANES):
-        piece = gain[:, start : start + LANES]
-        if piece.shape[1] < LANES:
-            piece = jnp.concatenate([piece, jnp.ones((1, LANES - piece.shape[1]), F32)], axis=1)
-        rows.append(piece)
-    while len(rows) < out_ref.shape[1]:
-        rows.append(jnp.zeros((1, LANES), F32))
+    if gain.shape[1] < LANES:
+        fill = jnp.ones((gain.shape[0], LANES - gain.shape[1]), F32)
+        gain = jnp.concatenate([gain, fill], axis=1)
+    rows.append(gain)
+    spare = out_ref.shape[1] - videos - gain.shape[0]
+    if spare:
+        rows.append(jnp.zeros((spare, LANES), F32))
     message = jnp.concatenate(rows, axis=0)
     out_ref[...] = jnp.broadcast_to(message[None], out_ref.shape)
 
@@ -163,7 +163,6 @@
     frames, packed, half = rows_ref.shape
     own = packed // 2
     tokens = frames * own
-    columns = w_proj_ref.shape[1]
     rows = rows_ref[...].reshape(frames * packed, half)
     token = lax.broadcasted_iota(jnp.int32, (tokens, frames * packed), 0)
     source = lax.broadcasted_iota(jnp.int32, (tokens, frames * packed), 1)
@@ -171,36 +170,76 @@
     low = dot32(jnp.where(source == first, 1.0, 0.0).astype(BF16), rows).astype(BF16)
     high = dot32(jnp.where(source == first + own, 1.0, 0.0).astype(BF16), rows).astype(BF16)
     total = dot32(low, w_proj_ref[:half, :]) + dot32(high, w_proj_ref[half:, :])
-    gained = (total * gain_ref[...].astype(F32)).astype(BF16)
-    out_ref[...] = jnp.broadcast_to(gained[None], out_ref.shape)
-
-
-def hidden_kernel(index_ref, rows_ref, w_gate_ref, w_up_ref, out_ref, joined):
-    cores, chips, tokens, columns = rows_ref.shape
-    depth = cores * chips * columns
-    first = index_ref.shape[1]
+    gain = gain_ref[...].astype(F32)
+    lanes = gain.shape[1]
+    for r in range(gain.shape[0]):
+        piece = slice(r * lanes, (r + 1) * lanes)
+        gained = (total[:, piece] * gain[r : r + 1]).astype(BF16)
+        out_ref[:, :, piece] = jnp.broadcast_to(gained[None], (out_ref.shape[0], tokens, lanes))
+
+
+def products(core, videos, index_ref, rows_ref, w_gate_ref, w_up_ref, gate_in, up_in, emit):
+    chips, tokens, columns = rows_ref.shape
+    cores = index_ref.shape[0] // chips
     gain_rows = -(-columns // LANES)
+    squares = jnp.zeros((tokens, LANES), F32)
+    for chip in range(chips):
+        gains = index_ref[chip * cores + core, videos : videos + gain_rows, :]
+        for r in range(gain_rows):
+            part = rows_ref[chip, :, r * LANES : min((r + 1) * LANES, columns)].astype(F32)
+            part = part / gains[r : r + 1, : part.shape[1]]
+            part = part * part
+            if part.shape[1] < LANES:
+                fill = jnp.zeros((tokens, LANES - part.shape[1]), F32)
+                part = jnp.concatenate([part, fill], axis=1)
+            squares = squares + part
+    width = w_gate_ref.shape[1]
+    block = min(width, 256)
+    for first in range(0, width, block):
+        sums = []
+        for w_ref, begin_ref in ((w_gate_ref, gate_in), (w_up_ref, up_in)):
+            total = None if begin_ref is None else begin_ref[:, first : first + block]
+            for chip in range(chips):
+                depth = pl.ds(pl.multiple_of((chip * cores + core) * columns, columns), columns)
+                part = dot32(rows_ref[chip], w_ref[depth, first : first + block])
+                total = part if total is None else total + part
+            sums.append(total)
+        emit(first, block, *sums)
+    return squares
+
+
+def first_kernel(
+    videos, me_ref, index_ref, rows_ref, w_gate_ref, w_up_ref, gate_ref, up_ref, squares_ref
+):
+    def emit(first, block, gate, up):
+        gate_ref[:, first : first + block] = gate
+        up_ref[:, first : first + block] = up
+
+    core = lax.rem(me_ref[0], index_ref.shape[0] // rows_ref.shape[0])
+    squares_ref[...] = products(
+        core, videos, index_ref, rows_ref, w_gate_ref, w_up_ref, None, None, emit
+    )
+
+
+def second_kernel(
+    me_ref, index_ref, rows_ref, w_gate_ref, w_up_ref, gate_ref, up_ref, squares_ref, out_ref,
+    gate_sum, up_sum,
+):
     videos = out_ref.shape[0]
-    squares = jnp.zeros((tokens, 1), F32)
-    for chip in range(chips):
-        for core in range(cores):
-            place = chip * cores + core
-            piece = rows_ref[core, chip]
-            joined[:, place * columns : (place + 1) * columns] = piece
-            for r in range(gain_rows):
-                part = piece[:, r * LANES : (r + 1) * LANES].astype(F32)
-                gain = index_ref[place, videos + r : videos + r + 1, : part.shape[1]]
-                part = part / gain
-                squares = squares + jnp.sum(part * part, axis=1, keepdims=True)
-    scale = lax.rsqrt(squares / depth + NORM_EPS)
-    width = out_ref.shape[2]
-    block = min(width, 256)
-
-    for start in range(0, width, block):
-        gate = dot32(joined[...], w_gate_ref[:, start : start + block]) * scale
-        up = dot32(joined[...], w_up_ref[:, start : start + block]) * scale
-        hidden = (jax.nn.silu(gate) * up).astype(BF16)
-        out_ref[:, :, start : start + block] = hidden.reshape(videos, -1, block)
+
+    def emit(first, block, gate, up):
+        gate_sum[:, first : first + block] = gate
+        up_sum[:, first : first + block] = up
+
+    cores = index_ref.shape[0] // rows_ref.shape[0]
+    core = cores - 1 - lax.rem(me_ref[0], cores)
+    squares = squares_ref[...] + products(
+        core, videos, index_ref, rows_ref, w_gate_ref, w_up_ref, gate_ref, up_ref, emit
+    )
+    mean = jnp.sum(squares, axis=1, keepdims=True) / w_gate_ref.shape[0]
+    scale = lax.rsqrt(mean + NORM_EPS)
+    hidden = jax.nn.silu(gate_sum[...] * scale) * (up_sum[...] * scale)
+    out_ref[...] = hidden.astype(BF16).reshape(out_ref.shape)
 
 
 def local(video, w_qkv, w_out, keep_list, kept_counts, w_proj, llm_gain, w_gate, w_up):
@@ -215,16 +254,18 @@
     columns = w_proj.shape[1]
     me = lax.axis_index(axes).astype(jnp.int32).reshape(1)
     spread = functools.partial(lax.all_to_all, split_axis=0, concat_axis=0, tiled=True)
-
-    message_rows = -(-(videos + -(-columns // LANES)) // 8) * 8
+    gain_rows = -(-columns // LANES)
+    gain = llm_gain.reshape(gain_rows, -1)
+
     message = pl.pallas_call(
         index_kernel,
-        out_shape=jax.ShapeDtypeStruct((frames, message_rows, LANES), F32),
-        in_specs=[whole(pltpu.SMEM), whole(), whole()],
+        out_shape=jax.ShapeDtypeStruct((frames, -(-(videos + gain_rows) // 8) * 8, LANES), F32),
+        in_specs=[whole(pltpu.SMEM), whole(pltpu.SMEM), whole(), whole()],
         out_specs=whole(),
         compiler_params=params(2 * MIB),
+        cost_estimate=pl.CostEstimate(flops=20000000000, bytes_accessed=65536, transcendentals=0),
         name="index",
-    )(kept_counts, keep_list, llm_gain.reshape(1, -1))
+    )(me, kept_counts.T, keep_list, gain)
     index = spread(message, axes)
 
     chosen = pl.pallas_call(
@@ -232,7 +273,7 @@
         out_shape=jax.ShapeDtypeStruct((frames, packed, half), BF16),
         in_specs=[whole(), whole()],
         out_specs=whole(),
-        compiler_params=params(4 * MIB + 8 * tokens * width),
+        compiler_params=params(3 * MIB + 8 * tokens * width),
         name="select",
     )(index, video)
     seen = spread(chosen, axes)
@@ -242,7 +283,7 @@
         out_shape=jax.ShapeDtypeStruct((frames, packed, half), BF16),
         in_specs=[whole(pltpu.SMEM), whole(), whole(), whole(), whole()],
         out_specs=whole(),
-        compiler_params=params(12 * MIB + 24 * frames * packed * width),
+        compiler_params=params(4 * MIB + 24 * frames * packed * width),
         name="attend",
     )(me, index, seen, w_qkv, w_out)
     token_rows = spread(encoded, axes)
@@ -252,26 +293,43 @@
         out_shape=jax.ShapeDtypeStruct((chips, tokens, columns), BF16),
         in_specs=[whole(), whole(), whole()],
         out_specs=whole(),
-        compiler_params=params(6 * MIB + 4 * tokens * chips * columns),
+        compiler_params=params(4 * MIB + 4 * tokens * chips * columns),
         name="project",
-    )(token_rows, w_proj, llm_gain.reshape(1, -1))
+    )(token_rows, w_proj, gain)
     mine = spread(gained, "chips")
-    rows = lax.all_gather(mine, "cores", axis=0)
-
+    theirs = lax.ppermute(mine, "cores", [(0, 1), (1, 0)])
+
+    units = w_gate.shape[1]
+    part = jax.ShapeDtypeStruct((tokens, units), F32)
+    work = pl.CostEstimate(
+        flops=2 * tokens * w_gate.shape[0] * units,
+        bytes_accessed=2 * w_gate.shape[0] * units,
+        transcendentals=0,
+    )
+    begun = pl.pallas_call(
+        functools.partial(first_kernel, videos),
+        out_shape=(part, part, jax.ShapeDtypeStruct((tokens, LANES), F32)),
+        in_specs=[whole(pltpu.SMEM)] + [whole()] * 4,
+        out_specs=(whole(), whole(), whole()),
+        compiler_params=params(4 * MIB + 16 * tokens * units),
+        cost_estimate=work,
+        name="first",
+    )(me, index, mine, w_gate, w_up)
     return pl.pallas_call(
-        hidden_kernel,
-        out_shape=jax.ShapeDtypeStruct((videos, seq, w_gate.shape[1]), BF16),
-        in_specs=[whole(), whole(), whole(), whole()],
-        out_specs=whole(),
-        scratch_shapes=[pltpu.VMEM((tokens, w_gate.shape[0]), BF16)],
-        compiler_params=params(52 * MIB),
-        name="hidden",
-    )(index, rows, w_gate, w_up)
+        second_kernel,
+        out_shape=jax.ShapeDtypeStruct((videos, seq, units), BF16),
+        in_specs=[whole(pltpu.SMEM)] + [whole()] * 7,
+        out_specs=whole(),
+        scratch_shapes=[pltpu.VMEM((tokens, units), F32)] * 2,
+        compiler_params=params(4 * MIB + 24 * tokens * units),
+        cost_estimate=work,
+        name="second",
+    )(me, index, theirs, w_gate, w_up, *begun)
 
 
 def solution(mesh):
     groups, frames = mesh.devices.shape
-    cores = 2 if frames % 2 == 0 else 1
+    cores = 2
     split = Mesh(mesh.devices.reshape(groups, frames // cores, cores), ("groups", "chips", "cores"))
     spread = ("chips", "cores")
     in_specs = (

time: 108 us -> 67.4 us (0.62)
  waiting for transfers between devices: 16.1 us -> 0.01 us
  between operations: 13.4 us -> 0.18 us
  Pallas kernels: 22.3 us -> 11.5 us
  blocking collectives: 41.9 us -> 52.2 us
  local copies, waits for them, and re-layouts: 9.97 us -> 3.19 us
  starting transfers between devices: 3.55 us -> 0.01 us
    all_to_all x0 -> x1, blocking collectives: none -> 10.5 us  [local(): seen = spread(chosen, axes)]
    pallas_call x2 -> x3, Pallas kernels: 17.9 us -> 7.66 us  [the longest x1 3.9 us: local(): pl.pallas_call(second_kernel, out_shape=jax.ShapeDtypeStruct((videos, seq...]
    all_gather x1 -> x0, waiting for transfers between devices: 8.23 us -> none  [local(): rows = lax.all_gather(mine, 'cores', axis=0)]
    all_to_all x1 -> x0, waiting for transfers between devices: 7.82 us -> none  [local(): seen = spread(chosen, axes)]
    unnamed x13 -> x32, local copies, waits for them, and re-layouts: 9.28 us -> 3.19 us
    all_to_all x1 -> x0, starting transfers between devices: 3.51 us -> none  [local(): seen = spread(chosen, axes)]
  transfers between devices with their start and end apart: 2 -> 1, of which waited for: 2 -> 0; matrix products, arithmetic and copies ran while one was open for 0% -> 0% of each run, Pallas kernels for 0% -> 5%
where the time goes in v2:
time: 67.4 us; the launch traced here: 67.1 us
  blocking collectives  52.2 us (77%)
  Pallas kernels  11.5 us (17%)
  local copies, waits for them, and re-layouts  3.19 us (5%)
    all_to_all x1, blocking collectives, local(): mine = spread(gained, 'chips')  16.9 us
    all_to_all x1, blocking collectives, local(): index = spread(message, axes)  14.4 us
    all_to_all x1, blocking collectives, local(): seen = spread(chosen, axes)  10.5 us
    all_to_all x1, blocking collectives, local(): token_rows = spread(encoded, axes)  10.5 us
    pallas_call x1, Pallas kernels, local(): pl.pallas_call(second_kernel, out_shape=jax.ShapeDtypeStruct((videos, seq...  3.9 us
    pallas_call x1, Pallas kernels, local(): pl.pallas_call(functools.partial(first_kernel, videos), out_shape=(part,...  3.21 us
    unnamed x32, local copies, waits for them, and re-layouts  3.19 us
    pallas_call x1, Pallas kernels, local(): pl.pallas_call(attend_kernel, out_shape=jax.ShapeDtypeStruct((frames, pac...  2.34 us
  transfers between devices with their start and end apart: 1, of which 0 were waited for; matrix products, arithmetic and copies ran while one was open for 0% of the time, Pallas kernels for 5%

profile of v2, /device:TPU:0, one launch (start us, length us, event | category | flops | bytes accessed | tf_op | source)
XLA Modules:
  0.0 67.1 jit_solution(12552217865614041555)
XLA Ops:
  0.0 0.8 %copy-done.4 = bf16[512]{0:T(512)(128)(2,1)S(1)} copy-done((bf16[512]{0:T(512)(128)(2,1)S(1)}, bf16[512]{0:T(512)(128)(2,1)}, u32[]{:S(2)}) %copy-start.4) | copy-done | bytes 1048
  0.8 1.1 %copy-done.6 = s32[2,1,128]{2,1,0:T(1,128)S(1)} copy-done((s32[2,1,128]{2,1,0:T(1,128)S(1)}, s32[2,1,128]{2,1,0:T(1,128)}, u32[]{:S(2)}) %copy-start.6) | copy-done | bytes 1048
  1.9 1.2 %copy-done.7 = s32[2,1]{0,1:T(1,128)S(1)} copy-done((s32[2,1]{0,1:T(1,128)S(1)}, s32[2,1]{0,1:T(1,128)}, u32[]{:S(2)}) %copy-start.7) | copy-done | bytes 32
  3.2 0.0 copy-start.5
  3.2 0.0 slice-start.1
  3.2 0.0 slice-start.2
  3.2 0.0 slice-start.3
  3.2 0.0 slice-start.5
  3.2 0.0 slice-start.6
  3.2 0.0 slice-start.7
  3.2 0.6 index.1
  3.8 14.4 %all_to_all.20.index_ref = f32[16,8,128]{2,1,0:T(8,128)S(1)} all-to-all(f32[16,8,128]{2,1,0:T(8,128)S(1)} %index.1), channel_id=1, replica_groups=mesh['groups'=2,'chips'=8,'cores'=2] {'chips','cores'}, dimensions={0} | all-to-all | bytes 131072 | tf_op jit(solution)/shard_map/all_to_all | solution.py:269
  18.2 1.0 %select.1 = bf16[16,8,512]{2,1,0:T(8,128)(2,1)S(1)} custom-call(f32[16,8,128]{2,1,0:T(8,128)S(1)} %all_to_all.20.index_ref, bf16[2,1,128,1024]{3,2,1,0:T(8,128)(2,1)S(1)} %copy-done.3), custom_call_target="tpu_custom_call" | custom-call | tf_op jit(solution)/shard_map/select/pallas_call | solution.py:271
  19.2 10.5 %all_to_all.21.rows_ref = bf16[16,8,512]{2,1,0:T(8,128)(2,1)S(1)} all-to-all(bf16[16,8,512]{2,1,0:T(8,128)(2,1)S(1)} %select.1), channel_id=1, replica_groups=mesh['groups'=2,'chips'=8,'cores'=2] {'chips','cores'}, dimensions={0} | all-to-all | bytes 262144 | tf_op jit(solution)/shard_map/all_to_all | solution.py:279
  29.7 2.3 %attend.1 = bf16[16,8,512]{2,1,0:T(8,128)(2,1)S(1)} custom-call(s32[1]{0:T(128)} %bitcast.me_ref, f32[16,8,128]{2,1,0:T(8,128)S(1)} %all_to_all.20.index_ref, bf16[16,8,512]{2,1,0:T(8,128)(2,1)S(1)} %all_to_all.21.rows_ref, bf16[1024,3072]{1,0:T(8,128)(2,1)S(1)} %copy-done, bf16[1024,1024]{1,0:T(8,128)(2,1)S(1)} %copy-done.1), custom_call_target="tpu_custom_call" | custom-call | tf_op jit(solution)/shard_map/attend/pallas_call | solution.py:281
  32.0 10.5 %all_to_all.22.rows_ref = bf16[16,8,512]{2,1,0:T(8,128)(2,1)S(1)} all-to-all(bf16[16,8,512]{2,1,0:T(8,128)(2,1)S(1)} %attend.1), channel_id=1, replica_groups=mesh['groups'=2,'chips'=8,'cores'=2] {'chips','cores'}, dimensions={0} | all-to-all | bytes 262144 | tf_op jit(solution)/shard_map/all_to_all | solution.py:289
  42.5 0.5 project.1
  43.0 16.9 %all_to_all.23.rows_ref = bf16[8,64,512]{2,1,0:T(8,128)(2,1)S(1)} all-to-all(bf16[8,64,512]{2,1,0:T(8,128)(2,1)S(1)} %project.1), channel_id=1, replica_groups=mesh['groups'=2,'chips'=8,'cores'=2] {'chips'}, dimensions={0} | all-to-all | bytes 1048576 | tf_op jit(solution)/shard_map/all_to_all | solution.py:299
  59.9 0.0 collective-permute-start
  59.9 0.0 slice-done.4
  59.9 0.0 slice-done.1
  60.0 3.2 %first.1 = (f32[64,1024]{1,0:T(8,128)S(1)}, f32[64,1024]{1,0:T(8,128)S(1)}, f32[64,128]{1,0:T(8,128)S(1)}) custom-call(s32[1]{0:T(128)} %bitcast.me_ref, f32[16,8,128]{2,1,0:T(8,128)S(1)} %all_to_all.20.index_ref, bf16[8,64,512]{2,1,0:T(8,128)(2,1)S(1)} %all_to_all.23.rows_ref, bf16[8192,1024]{1,0:T(8,128)(2,1)S(1)} %bitcast.4, bf16[8192,1024]{1,0:T(8,128)(2,1)S(1)} %bitcast.6), custom_call_target="tpu_custom_call" | custom-call | flops 1073741824 | bytes 16777216 | tf_op jit(solution)/shard_map/first/pallas_call | solution.py:309
  63.2 0.0 collective-permute-done.rows_ref
  63.2 3.9 %second.1 = bf16[2,32,1024]{2,1,0:T(8,128)(2,1)} custom-call(s32[1]{0:T(128)} %bitcast.me_ref, f32[16,8,128]{2,1,0:T(8,128)S(1)} %all_to_all.20.index_ref, bf16[8,64,512]{2,1,0:T(8,128)(2,1)S(1)} %collective-permute-done.rows_ref, bf16[8192,1024]{1,0:T(8,128)(2,1)S(1)} %bitcast.4, bf16[8192,1024]{1,0:T(8,128)(2,1)S(1)} %bitcast.6, ...), custom_call_target="tpu_custom_call" | custom-call | flops 1073741824 | bytes 16777216 | tf_op jit(solution)/shard_map/second/pallas_call | solution.py:318
  (22 shorter events, 0.0 us)
Async XLA Ops:
  0.0 59.9 %slice-start = ((s8[16777216]{0:T(1024)(128)(4,1)}), s8[4194304]{0:T(1024)(128)(4,1)S(1)}, s32[]{:S(2)}) async-start(s8[16777216]{0:T(1024)(128)(4,1)} %bitcast.3), calls=%async_computation.4 | async-start | bytes 8388608
  0.0 59.9 %slice-start.4 = ((s8[16777216]{0:T(1024)(128)(4,1)}), s8[4194304]{0:T(1024)(128)(4,1)S(1)}, s32[]{:S(2)}) async-start(s8[16777216]{0:T(1024)(128)(4,1)} %bitcast.5), calls=%async_computation.8 | async-start | bytes 8388608
  0.0 0.8 %copy-start.4 = (bf16[512]{0:T(512)(128)(2,1)S(1)}, bf16[512]{0:T(512)(128)(2,1)}, u32[]{:S(2)}) copy-start(bf16[512]{0:T(512)(128)(2,1)} %param.15) | copy-start | bytes 3076
  0.8 1.1 %copy-start.6 = (s32[2,1,128]{2,1,0:T(1,128)S(1)}, s32[2,1,128]{2,1,0:T(1,128)}, u32[]{:S(2)}) copy-start(s32[2,1,128]{2,1,0:T(1,128)} %keep_ref.1) | copy-start | bytes 3076
  1.9 1.2 %copy-start.7 = (s32[2,1]{0,1:T(1,128)S(1)}, s32[2,1]{0,1:T(1,128)}, u32[]{:S(2)}) copy-start(s32[2,1]{0,1:T(1,128)} %param.13) | copy-start | bytes 28
  3.1 15.0 %copy-start.3 = (bf16[2,1,128,1024]{3,2,1,0:T(8,128)(2,1)S(1)}, bf16[2,1,128,1024]{3,2,1,0:T(8,128)(2,1)}, u32[]{:S(2)}) copy-start(bf16[2,1,128,1024]{3,2,1,0:T(8,128)(2,1)} %video_ref.1) | copy-start | bytes 1572868
  3.1 26.5 %copy-start = (bf16[1024,3072]{1,0:T(8,128)(2,1)S(1)}, bf16[1024,3072]{1,0:T(8,128)(2,1)}, u32[]{:S(2)}) copy-start(bf16[1024,3072]{1,0:T(8,128)(2,1)} %w_qkv_ref.1) | copy-start | bytes 18874372
  3.1 26.5 %copy-start.1 = (bf16[1024,1024]{1,0:T(8,128)(2,1)S(1)}, bf16[1024,1024]{1,0:T(8,128)(2,1)}, u32[]{:S(2)}) copy-start(bf16[1024,1024]{1,0:T(8,128)(2,1)} %w_out_ref.1) | copy-start | bytes 6291460
  3.1 39.4 %copy-start.2 = (bf16[1024,512]{1,0:T(8,128)(2,1)S(1)}, bf16[1024,512]{1,0:T(8,128)(2,1)}, u32[]{:S(2)}) copy-start(bf16[1024,512]{1,0:T(8,128)(2,1)} %w_proj_ref.1) | copy-start | bytes 3145732
  3.2 39.4 %copy-start.5 = (bf16[512]{0:T(512)(128)(2,1)S(1)}, bf16[512]{0:T(512)(128)(2,1)}, u32[]{:S(2)}) copy-start(bf16[512]{0:T(512)(128)(2,1)} %param.15) | copy-start | bytes 3076
  3.2 56.7 %slice-start.1 = ((s8[16777216]{0:T(1024)(128)(4,1)}), s8[4194304]{0:T(1024)(128)(4,1)S(1)}, s32[]{:S(2)}) async-start(s8[16777216]{0:T(1024)(128)(4,1)} %bitcast.3), calls=%async_computation.5 | async-start | bytes 8388608
  3.2 56.7 %slice-start.2 = ((s8[16777216]{0:T(1024)(128)(4,1)}), s8[4194304]{0:T(1024)(128)(4,1)S(1)}, s32[]{:S(2)}) async-start(s8[16777216]{0:T(1024)(128)(4,1)} %bitcast.3), calls=%async_computation.6 | async-start | bytes 8388608
  3.2 56.7 %slice-start.3 = ((s8[16777216]{0:T(1024)(128)(4,1)}), s8[4194304]{0:T(1024)(128)(4,1)S(1)}, s32[]{:S(2)}) async-start(s8[16777216]{0:T(1024)(128)(4,1)} %bitcast.3), calls=%async_computation.7 | async-start | bytes 8388608
  3.2 56.7 %slice-start.5 = ((s8[16777216]{0:T(1024)(128)(4,1)}), s8[4194304]{0:T(1024)(128)(4,1)S(1)}, s32[]{:S(2)}) async-start(s8[16777216]{0:T(1024)(128)(4,1)} %bitcast.5), calls=%async_computation.9 | async-start | bytes 8388608
  3.2 56.7 %slice-start.6 = ((s8[16777216]{0:T(1024)(128)(4,1)}), s8[4194304]{0:T(1024)(128)(4,1)S(1)}, s32[]{:S(2)}) async-start(s8[16777216]{0:T(1024)(128)(4,1)} %bitcast.5), calls=%async_computation.10 | async-start | bytes 8388608
  3.2 56.7 %slice-start.7 = ((s8[16777216]{0:T(1024)(128)(4,1)}), s8[4194304]{0:T(1024)(128)(4,1)S(1)}, s32[]{:S(2)}) async-start(s8[16777216]{0:T(1024)(128)(4,1)} %bitcast.5), calls=%async_computation.11 | async-start | bytes 8388608
  59.9 3.3 %collective-permute-start = (bf16[8,64,512]{2,1,0:T(8,128)(2,1)S(1)}, bf16[8,64,512]{2,1,0:T(8,128)(2,1)S(1)}, u32[]{:S(2)}, u32[]{:S(2)}) collective-permute-start(bf16[8,64,512]{2,1,0:T(8,128)(2,1)S(1)} %all_to_all.23.rows_ref), channel_id=1, source_target_pairs={{0,1},{1,0},{2,3},{3,2},{4,5},{5,4},{6,7},{7,6},{8,9},{9,8},{10,11... | collective-permute-start | bytes 1572872 | tf_op jit(solution)/shard_map/ppermute | solution.py:300

commit v3 on v2

--- a/solution.py
+++ b/solution.py
@@ -14,7 +14,9 @@
 LANES = 128
 NORM_EPS = 1e-05
 SCORE_SCALE = 0.125
+DIRECT = 4
 MIB = 1 << 20
+COVER_FLOPS = 20_000_000_000
 F32 = jnp.float32
 BF16 = jnp.bfloat16
 
@@ -36,24 +38,40 @@
     return pltpu.CompilerParams(vmem_limit_bytes=int(limit))
 
 
-def index_kernel(me_ref, counts_ref, keep_ref, gain_ref, out_ref):
-    del me_ref
+def collect_kernel(counts_hbm, keep_hbm, gain_hbm, out_ref, counts_ref, keep_ref, gain_ref, sems):
+    arrays = ((counts_hbm, counts_ref), (keep_hbm, keep_ref), (gain_hbm, gain_ref))
+    copies = [
+        pltpu.make_async_copy(source, target, sems.at[i])
+        for i, (source, target) in enumerate(arrays)
+    ]
+    for copy in copies:
+        copy.start()
+    for copy in copies:
+        copy.wait()
     videos = keep_ref.shape[0]
     lane = lax.broadcasted_iota(jnp.int32, (1, LANES), 1)
+    counts = counts_ref[...].astype(F32)
     rows = []
     for v in range(videos):
         listed = keep_ref[v, :, :LANES].astype(F32)
-        rows.append(jnp.where(lane == KMAX, counts_ref[0, v].astype(F32), listed))
+        rows.append(jnp.where(lane == KMAX, counts[:, v : v + 1], listed))
     gain = gain_ref[...].astype(F32)
     if gain.shape[1] < LANES:
         fill = jnp.ones((gain.shape[0], LANES - gain.shape[1]), F32)
         gain = jnp.concatenate([gain, fill], axis=1)
     rows.append(gain)
-    spare = out_ref.shape[1] - videos - gain.shape[0]
+    spare = out_ref.shape[0] - videos - gain.shape[0]
     if spare:
         rows.append(jnp.zeros((spare, LANES), F32))
-    message = jnp.concatenate(rows, axis=0)
-    out_ref[...] = jnp.broadcast_to(message[None], out_ref.shape)
+    out_ref[...] = jnp.concatenate(rows, axis=0)
+
+
+def index_kernel(message_ref, out_ref):
+    peer = lax.broadcasted_iota(jnp.int32, (out_ref.shape[0], 1, LANES), 0).astype(F32)
+    row = lax.broadcasted_iota(jnp.int32, message_ref.shape, 0)
+    lane = lax.broadcasted_iota(jnp.int32, message_ref.shape, 1)
+    free = jnp.logical_and(row == 0, lane == KMAX + 1)
+    out_ref[...] = jnp.where(free[None], peer, message_ref[...][None])
 
 
 def select_kernel(index_ref, video_ref, out_ref):
@@ -90,7 +108,7 @@
             out_ref[peer] = jnp.concatenate([rows[:, :half], rows[:, half:]], axis=0)
 
 
-def attend_kernel(me_ref, index_ref, rows_ref, w_qkv_ref, w_out_ref, out_ref):
+def attend_kernel(index_ref, rows_ref, w_qkv_ref, w_out_ref, out_ref):
     frames, packed, half = rows_ref.shape
     own = packed // 2
     width = 2 * half
@@ -116,7 +134,8 @@
 
     table = index_ref[...]
     row = lax.broadcasted_iota(jnp.int32, (1, packed, 1), 1)
-    flat = me_ref[0] * own + jnp.where(row >= own, row - own, row)
+    me = table[:1, :1, KMAX + 1 : KMAX + 2].astype(jnp.int32)
+    flat = me * own + jnp.where(row >= own, row - own, row)
     owner = jnp.zeros((frames, packed, 1), jnp.bool_)
     for v in range(videos):
         count = table[:, v : v + 1, KMAX : KMAX + 1]
@@ -175,66 +194,74 @@
     for r in range(gain.shape[0]):
         piece = slice(r * lanes, (r + 1) * lanes)
         gained = (total[:, piece] * gain[r : r + 1]).astype(BF16)
-        out_ref[:, :, piece] = jnp.broadcast_to(gained[None], (out_ref.shape[0], tokens, lanes))
-
-
-def products(core, videos, index_ref, rows_ref, w_gate_ref, w_up_ref, gate_in, up_in, emit):
-    chips, tokens, columns = rows_ref.shape
-    cores = index_ref.shape[0] // chips
+        out_ref[:, piece] = gained
+
+
+def products(place_of, videos, index_ref, rows_ref, w_gate_ref, w_up_ref, begun, emit):
+    parts, tokens, columns = rows_ref.shape
     gain_rows = -(-columns // LANES)
-    squares = jnp.zeros((tokens, LANES), F32)
-    for chip in range(chips):
-        gains = index_ref[chip * cores + core, videos : videos + gain_rows, :]
+    places = [place_of(part) for part in range(parts)]
+    squares = jnp.zeros((tokens, LANES), F32) if begun is None else begun[2][...]
+    for part, place in enumerate(places):
+        inverse = 1.0 / index_ref[place, videos : videos + gain_rows, :]
         for r in range(gain_rows):
-            part = rows_ref[chip, :, r * LANES : min((r + 1) * LANES, columns)].astype(F32)
-            part = part / gains[r : r + 1, : part.shape[1]]
-            part = part * part
-            if part.shape[1] < LANES:
-                fill = jnp.zeros((tokens, LANES - part.shape[1]), F32)
-                part = jnp.concatenate([part, fill], axis=1)
-            squares = squares + part
+            piece = rows_ref[part, :, r * LANES : min((r + 1) * LANES, columns)].astype(F32)
+            piece = piece * inverse[r : r + 1, : piece.shape[1]]
+            piece = piece * piece
+            if piece.shape[1] < LANES:
+                fill = jnp.zeros((tokens, LANES - piece.shape[1]), F32)
+                piece = jnp.concatenate([piece, fill], axis=1)
+            squares = squares + piece
     width = w_gate_ref.shape[1]
     block = min(width, 256)
     for first in range(0, width, block):
         sums = []
-        for w_ref, begin_ref in ((w_gate_ref, gate_in), (w_up_ref, up_in)):
-            total = None if begin_ref is None else begin_ref[:, first : first + block]
-            for chip in range(chips):
-                depth = pl.ds(pl.multiple_of((chip * cores + core) * columns, columns), columns)
-                part = dot32(rows_ref[chip], w_ref[depth, first : first + block])
-                total = part if total is None else total + part
+        for i, w_ref in enumerate((w_gate_ref, w_up_ref)):
+            total = None if begun is None else begun[i][:, first : first + block]
+            for part, place in enumerate(places):
+                depth = pl.ds(pl.multiple_of(place * columns, columns), columns)
+                one = dot32(rows_ref[part], w_ref[depth, first : first + block])
+                total = one if total is None else total + one
             sums.append(total)
         emit(first, block, *sums)
     return squares
 
 
-def first_kernel(
-    videos, me_ref, index_ref, rows_ref, w_gate_ref, w_up_ref, gate_ref, up_ref, squares_ref
-):
+def place_rule(index_ref, outer, flip):
+    me = jnp.max(index_ref[0, :1, KMAX + 1 : KMAX + 2]).astype(jnp.int32)
+    quad = index_ref.shape[0] // outer
+    row = me // quad
+    near = jnp.bitwise_xor(me - row * quad, flip)
+    if outer <= DIRECT:
+        return lambda i: jnp.bitwise_xor(row, i) * quad + near
+    return lambda i: i * quad + near
+
+
+def partial_kernel(flip, videos, *refs):
+    index_ref, rows_ref, w_gate_ref, w_up_ref = refs[:4]
+    gate_ref, up_ref, squares_ref = refs[-3:]
+    begun = refs[4:7] if len(refs) > 7 else None
+
     def emit(first, block, gate, up):
         gate_ref[:, first : first + block] = gate
         up_ref[:, first : first + block] = up
 
-    core = lax.rem(me_ref[0], index_ref.shape[0] // rows_ref.shape[0])
+    rule = place_rule(index_ref, rows_ref.shape[0], flip)
     squares_ref[...] = products(
-        core, videos, index_ref, rows_ref, w_gate_ref, w_up_ref, None, None, emit
+        rule, videos, index_ref, rows_ref, w_gate_ref, w_up_ref, begun, emit
     )
 
 
-def second_kernel(
-    me_ref, index_ref, rows_ref, w_gate_ref, w_up_ref, gate_ref, up_ref, squares_ref, out_ref,
-    gate_sum, up_sum,
-):
-    videos = out_ref.shape[0]
-
+def final_kernel(flip, index_ref, rows_ref, w_gate_ref, w_up_ref, gate_ref, up_ref, squares_ref,
+                 out_ref, gate_sum, up_sum):
     def emit(first, block, gate, up):
         gate_sum[:, first : first + block] = gate
         up_sum[:, first : first + block] = up
 
-    cores = index_ref.shape[0] // rows_ref.shape[0]
-    core = cores - 1 - lax.rem(me_ref[0], cores)
-    squares = squares_ref[...] + products(
-        core, videos, index_ref, rows_ref, w_gate_ref, w_up_ref, gate_ref, up_ref, emit
+    rule = place_rule(index_ref, rows_ref.shape[0], flip)
+    begun = (gate_ref, up_ref, squares_ref)
+    squares = products(
+        rule, out_ref.shape[0], index_ref, rows_ref, w_gate_ref, w_up_ref, begun, emit
     )
     mean = jnp.sum(squares, axis=1, keepdims=True) / w_gate_ref.shape[0]
     scale = lax.rsqrt(mean + NORM_EPS)
@@ -244,28 +271,38 @@
 
 def local(video, w_qkv, w_out, keep_list, kept_counts, w_proj, llm_gain, w_gate, w_up):
     videos, _, patches, width = video.shape
-    chips, cores = lax.axis_size("chips"), lax.axis_size("cores")
-    frames = chips * cores
-    axes = ("chips", "cores")
+    axes = ("outer", "mid", "cores")
+    frames, outer = lax.axis_size(axes), lax.axis_size("outer")
     seq = frames * TOKL
     tokens = videos * seq
     packed = 2 * (tokens // frames)
     half = width // 2
     columns = w_proj.shape[1]
-    me = lax.axis_index(axes).astype(jnp.int32).reshape(1)
     spread = functools.partial(lax.all_to_all, split_axis=0, concat_axis=0, tiled=True)
     gain_rows = -(-columns // LANES)
     gain = llm_gain.reshape(gain_rows, -1)
 
+    counts, listed = kept_counts.T, keep_list
+    rows = -(-(videos + gain_rows) // 8) * 8
+    message = pl.pallas_call(
+        collect_kernel,
+        out_shape=jax.ShapeDtypeStruct((rows, LANES), F32),
+        in_specs=[whole(pltpu.HBM)] * 3,
+        out_specs=whole(),
+        scratch_shapes=[pltpu.VMEM(x.shape, x.dtype) for x in (counts, listed, gain)]
+        + [pltpu.SemaphoreType.DMA((3,))],
+        compiler_params=params(2 * MIB),
+        name="collect",
+    )(*(pltpu.with_memory_space_constraint(x, pltpu.HBM) for x in (counts, listed, gain)))
     message = pl.pallas_call(
         index_kernel,
-        out_shape=jax.ShapeDtypeStruct((frames, -(-(videos + gain_rows) // 8) * 8, LANES), F32),
-        in_specs=[whole(pltpu.SMEM), whole(pltpu.SMEM), whole(), whole()],
+        out_shape=jax.ShapeDtypeStruct((frames, rows, LANES), F32),
+        in_specs=[whole()],
         out_specs=whole(),
         compiler_params=params(2 * MIB),
-        cost_estimate=pl.CostEstimate(flops=20000000000, bytes_accessed=65536, transcendentals=0),
+        cost_estimate=pl.CostEstimate(flops=COVER_FLOPS, bytes_accessed=65536, transcendentals=0),
         name="index",
-    )(me, kept_counts.T, keep_list, gain)
+    )(message)
     index = spread(message, axes)
 
     chosen = pl.pallas_call(
@@ -281,57 +318,74 @@
     encoded = pl.pallas_call(
         attend_kernel,
         out_shape=jax.ShapeDtypeStruct((frames, packed, half), BF16),
-        in_specs=[whole(pltpu.SMEM), whole(), whole(), whole(), whole()],
+        in_specs=[whole()] * 4,
         out_specs=whole(),
         compiler_params=params(4 * MIB + 24 * frames * packed * width),
         name="attend",
-    )(me, index, seen, w_qkv, w_out)
+    )(index, seen, w_qkv, w_out)
     token_rows = spread(encoded, axes)
 
     gained = pl.pallas_call(
         project_kernel,
-        out_shape=jax.ShapeDtypeStruct((chips, tokens, columns), BF16),
+        out_shape=jax.ShapeDtypeStruct((tokens, columns), BF16),
         in_specs=[whole(), whole(), whole()],
         out_specs=whole(),
-        compiler_params=params(4 * MIB + 4 * tokens * chips * columns),
+        compiler_params=params(4 * MIB + 16 * tokens * columns),
         name="project",
     )(token_rows, w_proj, gain)
-    mine = spread(gained, "chips")
-    theirs = lax.ppermute(mine, "cores", [(0, 1), (1, 0)])
-
+
+    def swap(values, axis, flip=1):
+        pairs = [(i, i ^ flip) for i in range(lax.axis_size(axis))]
+        return lax.ppermute(values, axis, pairs)
+
+    if outer <= DIRECT:
+        line = jnp.stack([gained] + [swap(gained, "outer", k) for k in range(1, outer)])
+    else:
+        line = spread(jnp.broadcast_to(gained[None], (outer,) + gained.shape), "outer")
     units = w_gate.shape[1]
     part = jax.ShapeDtypeStruct((tokens, units), F32)
+    sums = (part, part, jax.ShapeDtypeStruct((tokens, LANES), F32))
     work = pl.CostEstimate(
-        flops=2 * tokens * w_gate.shape[0] * units,
-        bytes_accessed=2 * w_gate.shape[0] * units,
+        flops=tokens * w_gate.shape[0] * units,
+        bytes_accessed=w_gate.shape[0] * units,
         transcendentals=0,
     )
-    begun = pl.pallas_call(
-        functools.partial(first_kernel, videos),
-        out_shape=(part, part, jax.ShapeDtypeStruct((tokens, LANES), F32)),
-        in_specs=[whole(pltpu.SMEM)] + [whole()] * 4,
-        out_specs=(whole(), whole(), whole()),
-        compiler_params=params(4 * MIB + 16 * tokens * units),
+
+    def add(name, flip, block, begun):
+        return pl.pallas_call(
+            functools.partial(partial_kernel, flip, videos),
+            out_shape=sums,
+            in_specs=[whole()] * (4 + len(begun)),
+            out_specs=(whole(), whole(), whole()),
+            compiler_params=params(3 * MIB + 20 * tokens * units),
+            cost_estimate=work,
+            name=name,
+        )(index, block, w_gate, w_up, *begun)
+
+    line_mid = swap(line, "mid")
+    line_core = swap(line, "cores")
+    begun = add("own", 0, line, ())
+    begun = add("core", 1, line_core, begun)
+    line_mid, begun = lax.optimization_barrier((line_mid, begun))
+    line_both = swap(line_mid, "cores")
+    begun = add("mid", 2, line_mid, begun)
+    return pl.pallas_call(
+        functools.partial(final_kernel, 3),
+        out_shape=jax.ShapeDtypeStruct((videos, seq, units), BF16),
+        in_specs=[whole()] * 7,
+        out_specs=whole(),
+        scratch_shapes=[pltpu.VMEM((tokens, units), F32)] * 2,
+        compiler_params=params(3 * MIB + 24 * tokens * units),
         cost_estimate=work,
-        name="first",
-    )(me, index, mine, w_gate, w_up)
-    return pl.pallas_call(
-        second_kernel,
-        out_shape=jax.ShapeDtypeStruct((videos, seq, units), BF16),
-        in_specs=[whole(pltpu.SMEM)] + [whole()] * 7,
-        out_specs=whole(),
-        scratch_shapes=[pltpu.VMEM((tokens, units), F32)] * 2,
-        compiler_params=params(4 * MIB + 24 * tokens * units),
-        cost_estimate=work,
-        name="second",
-    )(me, index, theirs, w_gate, w_up, *begun)
+        name="final",
+    )(index, line_both, w_gate, w_up, *begun)
 
 
 def solution(mesh):
     groups, frames = mesh.devices.shape
-    cores = 2
-    split = Mesh(mesh.devices.reshape(groups, frames // cores, cores), ("groups", "chips", "cores"))
-    spread = ("chips", "cores")
+    devices = mesh.devices.reshape(groups, frames // 4, 2, 2)
+    split = Mesh(devices, ("groups", "outer", "mid", "cores"))
+    spread = ("outer", "mid", "cores")
     in_specs = (
         P("groups", spread, None, None),
         P(),

time: 67.4 us -> 61.7 us (0.915)
  blocking collectives: 52.2 us -> 35.4 us
  waiting for transfers between devices: 0.01 us -> 7.8 us
  starting transfers between devices: 0.01 us -> 5.32 us
  local copies, waits for them, and re-layouts: 3.19 us -> 0.07 us
  Pallas kernels: 11.5 us -> 12.6 us
    all_to_all x1 -> x0, blocking collectives: 16.9 us -> none  [local(): mine = spread(gained, 'chips')]
    ppermute x1 -> x6, waiting for transfers between devices: 0.01 us -> 7.8 us  [swap(): return lax.ppermute(values, axis, pairs)]
    ppermute x1 -> x6, starting transfers between devices: 0.01 us -> 5.32 us  [swap(): return lax.ppermute(values, axis, pairs)]
    unnamed x32 -> x26, local copies, waits for them, and re-layouts: 3.19 us -> 0.07 us
    pallas_call x4 -> x7, Pallas kernels: 8.14 us -> 9.24 us  [the longest x3 5.36 us: add(): pl.pallas_call(functools.partial(partial_kernel, flip, videos), out_shape...]
  transfers between devices with their start and end apart: 1 -> 6, of which waited for: 0 -> 3; matrix products, arithmetic and copies ran while one was open for 0% -> 0% of each run, Pallas kernels for 5% -> 9%
where the time goes in v3:
time: 61.7 us; the launch traced here: 61.4 us
  blocking collectives  35.4 us (57%)
  Pallas kernels  12.6 us (20%)
  waiting for transfers between devices  7.8 us (13%)
  starting transfers between devices  5.32 us (9%)
    all_to_all x1, blocking collectives, local(): index = spread(message, axes)  14.4 us
    all_to_all x1, blocking collectives, local(): seen = spread(chosen, axes)  10.5 us
    all_to_all x1, blocking collectives, local(): token_rows = spread(encoded, axes)  10.5 us
    ppermute x6, waiting for transfers between devices, swap(): return lax.ppermute(values, axis, pairs)  7.8 us
    pallas_call x3, Pallas kernels, add(): pl.pallas_call(functools.partial(partial_kernel, flip, videos), out_shape...  5.36 us
    ppermute x6, starting transfers between devices, swap(): return lax.ppermute(values, axis, pairs)  5.32 us
    pallas_call x1, Pallas kernels, local(): pl.pallas_call(functools.partial(final_kernel, 3), out_shape=jax.ShapeDty...  2.48 us
    pallas_call x1, Pallas kernels, local(): pl.pallas_call(attend_kernel, out_shape=jax.ShapeDtypeStruct((frames, pac...  2.4 us
  transfers between devices with their start and end apart: 6, of which 3 were waited for; matrix products, arithmetic and copies ran while one was open for 0% of the time, Pallas kernels for 9%

profile of v3, /device:TPU:0, one launch (start us, length us, event | category | flops | bytes accessed | tf_op | source)
XLA Modules:
  0.0 61.4 jit_solution(18387798982879909071)
XLA Ops:
  0.0 1.0 %collect.1.message_ref = f32[8,128]{1,0:T(8,128)S(1)} custom-call(s32[1,2]{1,0:T(1,128)} %bitcast.16, s32[2,1,128]{2,1,0:T(1,128)} %keep_hbm.1, bf16[4,128]{1,0:T(4,128)(2,1)} %bitcast.11), custom_call_target="tpu_custom_call" | custom-call | tf_op jit(solution)/shard_map/collect/pallas_call | solution.py:287
  1.0 0.0 copy-start.3
  1.0 0.0 copy-start.1
  1.0 0.0 copy-start.2
  1.0 0.0 slice-start.1
  1.1 0.0 slice-start.5
  1.1 14.4 %all_to_all.15.index_ref.refs_0_ = f32[16,8,128]{2,1,0:T(8,128)S(1)} all-to-all(f32[16,8,128]{2,1,0:T(8,128)S(1)} %index.1), channel_id=1, replica_groups=mesh['groups'=2,'outer'=4,'mid'=2,'cores'=2] {'outer','mid','cores'}, dimensions={0} | all-to-all | bytes 131072 | tf_op jit(solution)/shard_map/all_to_all | solution.py:306
  15.5 1.0 %select.1 = bf16[16,8,512]{2,1,0:T(8,128)(2,1)S(1)} custom-call(f32[16,8,128]{2,1,0:T(8,128)S(1)} %all_to_all.15.index_ref.refs_0_, bf16[2,1,128,1024]{3,2,1,0:T(8,128)(2,1)S(1)} %copy-done.3), custom_call_target="tpu_custom_call" | custom-call | tf_op jit(solution)/shard_map/select/pallas_call | solution.py:308
  16.5 10.5 %all_to_all.16.rows_ref = bf16[16,8,512]{2,1,0:T(8,128)(2,1)S(1)} all-to-all(bf16[16,8,512]{2,1,0:T(8,128)(2,1)S(1)} %select.1), channel_id=1, replica_groups=mesh['groups'=2,'outer'=4,'mid'=2,'cores'=2] {'outer','mid','cores'}, dimensions={0} | all-to-all | bytes 262144 | tf_op jit(solution)/shard_map/all_to_all | solution.py:316
  27.0 2.4 %attend.1 = bf16[16,8,512]{2,1,0:T(8,128)(2,1)S(1)} custom-call(f32[16,8,128]{2,1,0:T(8,128)S(1)} %all_to_all.15.index_ref.refs_0_, bf16[16,8,512]{2,1,0:T(8,128)(2,1)S(1)} %all_to_all.16.rows_ref, bf16[1024,3072]{1,0:T(8,128)(2,1)S(1)} %copy-done, bf16[1024,1024]{1,0:T(8,128)(2,1)S(1)} %copy-done.1), custom_call_target="tpu_custom_call" | custom-call | tf_op jit(solution)/shard_map/attend/pallas_call | solution.py:318
  29.4 10.5 %all_to_all.17.rows_ref = bf16[16,8,512]{2,1,0:T(8,128)(2,1)S(1)} all-to-all(bf16[16,8,512]{2,1,0:T(8,128)(2,1)S(1)} %attend.1), channel_id=1, replica_groups=mesh['groups'=2,'outer'=4,'mid'=2,'cores'=2] {'outer','mid','cores'}, dimensions={0} | all-to-all | bytes 262144 | tf_op jit(solution)/shard_map/all_to_all | solution.py:326
  39.9 0.4 project.1
  40.3 0.7 %collective-permute-start.2 = (bf16[64,512]{1,0:T(8,128)(2,1)S(1)}, bf16[64,512]{1,0:T(8,128)(2,1)S(1)}, u32[]{:S(2)}, u32[]{:S(2)}) collective-permute-start(bf16[64,512]{1,0:T(8,128)(2,1)S(1)} %project.1), channel_id=1, source_target_pairs={{0,12},{4,8},{8,4},{12,0},{1,13},{5,9},{9,5},{13,1},{2,14},{6,10},... | collective-permute-start | bytes 196616 | tf_op jit(solution)/shard_map/ppermute | solution.py:339
  41.0 0.2 collective-permute-start.1
  41.2 3.5 %collective-permute-start = (bf16[64,512]{1,0:T(8,128)(2,1)S(1)}, bf16[64,512]{1,0:T(8,128)(2,1)S(1)}, u32[]{:S(2)}, u32[]{:S(2)}) collective-permute-start(bf16[64,512]{1,0:T(8,128)(2,1)S(1)} %project.1), channel_id=1, source_target_pairs={{0,4},{4,0},{8,12},{12,8},{1,5},{5,1},{9,13},{13,9},{2,6},{6,2},{1... | collective-permute-start | bytes 196616 | tf_op jit(solution)/shard_map/ppermute | solution.py:339
  44.8 2.3 %collective-permute-done.2 = bf16[64,512]{1,0:T(8,128)(2,1)S(1)} collective-permute-done((bf16[64,512]{1,0:T(8,128)(2,1)S(1)}, bf16[64,512]{1,0:T(8,128)(2,1)S(1)}, u32[]{:S(2)}, u32[]{:S(2)}) %collective-permute-start.2) | collective-permute-done | bytes 65568 | tf_op jit(solution)/shard_map/ppermute | solution.py:339
  47.1 1.2 %collective-permute-done.1 = bf16[64,512]{1,0:T(8,128)(2,1)S(1)} collective-permute-done((bf16[64,512]{1,0:T(8,128)(2,1)S(1)}, bf16[64,512]{1,0:T(8,128)(2,1)S(1)}, u32[]{:S(2)}, u32[]{:S(2)}) %collective-permute-start.1) | collective-permute-done | bytes 65568 | tf_op jit(solution)/shard_map/ppermute | solution.py:339
  48.3 0.1 collective-permute-start.4
  48.4 0.8 %collective-permute-start.3 = (bf16[4,64,512]{2,1,0:T(8,128)(2,1)S(1)}, bf16[4,64,512]{2,1,0:T(8,128)(2,1)S(1)}, u32[]{:S(2)}, u32[]{:S(2)}) collective-permute-start(bf16[4,64,512]{2,1,0:T(8,128)(2,1)S(1)} %pad_maximum_fusion.refs_1_), channel_id=1, source_target_pairs={{0,2},{2,0},{1,3},{3,1},{4,6},{6,4},{5,7},{7,5},{8,10},{10,8},{9,1... | collective-permute-start | bytes 786440 | tf_op jit(solution)/shard_map/ppermute | solution.py:339
  49.3 1.8 %own.1 = (f32[64,1024]{1,0:T(8,128)S(1)}, f32[64,1024]{1,0:T(8,128)S(1)}, f32[64,128]{1,0:T(8,128)S(1)}) custom-call(f32[16,8,128]{2,1,0:T(8,128)S(1)} %all_to_all.15.index_ref.refs_0_, bf16[4,64,512]{2,1,0:T(8,128)(2,1)S(1)} %pad_maximum_fusion.refs_1_, bf16[8192,1024]{1,0:T(8,128)(2,1)S(1)} %bitcast.7, bf16[8192,1024]{1,0:T(8,128)(2,1)S(1)} %bitcast.9), custom_call_target="tpu_custom_call" | custom-call | flops 536870912 | bytes 8388608 | tf_op jit(solution)/shard_map/own/pallas_call | solution.py:355
  51.1 1.8 %core.1 = (f32[64,1024]{1,0:T(8,128)S(1)}, f32[64,1024]{1,0:T(8,128)S(1)}, f32[64,128]{1,0:T(8,128)S(1)}) custom-call(f32[16,8,128]{2,1,0:T(8,128)S(1)} %all_to_all.15.index_ref.refs_0_, bf16[4,64,512]{2,1,0:T(8,128)(2,1)S(1)} %collective-permute-done.4.refs_1_, bf16[8192,1024]{1,0:T(8,128)(2,1)S(1)} %bitcast.7, bf16[8192,1024]{1,0:T(8,128)(2,1)S(1)} %bitcast.9, ...), custom_call_target="tpu_custom_call" | custom-call | flops 536870912 | bytes 8388608 | tf_op jit(solution)/shard_map/core/pallas_call | solution.py:355
  52.9 4.3 %collective-permute-done.3.refs_1_ = bf16[4,64,512]{2,1,0:T(8,128)(2,1)S(1)} collective-permute-done((bf16[4,64,512]{2,1,0:T(8,128)(2,1)S(1)}, bf16[4,64,512]{2,1,0:T(8,128)(2,1)S(1)}, u32[]{:S(2)}, u32[]{:S(2)}) %collective-permute-start.3) | collective-permute-done | bytes 262176 | tf_op jit(solution)/shard_map/ppermute | solution.py:339
  57.1 1.8 %mid.1 = (f32[64,1024]{1,0:T(8,128)S(1)}, f32[64,1024]{1,0:T(8,128)S(1)}, f32[64,128]{1,0:T(8,128)S(1)}) custom-call(f32[16,8,128]{2,1,0:T(8,128)S(1)} %all_to_all.15.index_ref.refs_0_, bf16[4,64,512]{2,1,0:T(8,128)(2,1)S(1)} %collective-permute-done.3.refs_1_, bf16[8192,1024]{1,0:T(8,128)(2,1)S(1)} %bitcast.7, bf16[8192,1024]{1,0:T(8,128)(2,1)S(1)} %bitcast.9, ...), custom_call_target="tpu_custom_call" | custom-call | flops 536870912 | bytes 8388608 | tf_op jit(solution)/shard_map/mid/pallas_call | solution.py:355
  59.0 2.5 %final.1 = bf16[2,32,1024]{2,1,0:T(8,128)(2,1)} custom-call(f32[16,8,128]{2,1,0:T(8,128)S(1)} %all_to_all.15.index_ref.refs_0_, bf16[4,64,512]{2,1,0:T(8,128)(2,1)S(1)} %collective-permute-done.5.rows_ref, bf16[8192,1024]{1,0:T(8,128)(2,1)S(1)} %bitcast.7, bf16[8192,1024]{1,0:T(8,128)(2,1)S(1)} %bitcast.9, f32[64,1024]{1,0:T(8,128)S(1)} %get-tuple-element.28.gate_ref, ...), custom_call_target="tpu_custom_call" | custom-call | flops 536870912 | bytes 8388608 | tf_op jit(solution)/shard_map/final/pallas_call | solution.py:372
  (29 shorter events, 0.1 us)
Async XLA Ops:
  0.0 49.2 %slice-start = ((s8[16777216]{0:T(1024)(128)(4,1)}), s8[4194304]{0:T(1024)(128)(4,1)S(1)}, s32[]{:S(2)}) async-start(s8[16777216]{0:T(1024)(128)(4,1)} %bitcast.6), calls=%async_computation.3 | async-start | bytes 8388608
  0.0 49.2 %slice-start.4 = ((s8[16777216]{0:T(1024)(128)(4,1)}), s8[4194304]{0:T(1024)(128)(4,1)S(1)}, s32[]{:S(2)}) async-start(s8[16777216]{0:T(1024)(128)(4,1)} %bitcast.8), calls=%async_computation.7 | async-start | bytes 8388608
  1.0 14.5 %copy-start.3 = (bf16[2,1,128,1024]{3,2,1,0:T(8,128)(2,1)S(1)}, bf16[2,1,128,1024]{3,2,1,0:T(8,128)(2,1)}, u32[]{:S(2)}) copy-start(bf16[2,1,128,1024]{3,2,1,0:T(8,128)(2,1)} %video_ref.1) | copy-start | bytes 1572868
  1.0 26.0 %copy-start = (bf16[1024,3072]{1,0:T(8,128)(2,1)S(1)}, bf16[1024,3072]{1,0:T(8,128)(2,1)}, u32[]{:S(2)}) copy-start(bf16[1024,3072]{1,0:T(8,128)(2,1)} %w_qkv_ref.1) | copy-start | bytes 18874372
  1.0 26.0 %copy-start.1 = (bf16[1024,1024]{1,0:T(8,128)(2,1)S(1)}, bf16[1024,1024]{1,0:T(8,128)(2,1)}, u32[]{:S(2)}) copy-start(bf16[1024,1024]{1,0:T(8,128)(2,1)} %w_out_ref.1) | copy-start | bytes 6291460
  1.0 38.9 %copy-start.2 = (bf16[1024,512]{1,0:T(8,128)(2,1)S(1)}, bf16[1024,512]{1,0:T(8,128)(2,1)}, u32[]{:S(2)}) copy-start(bf16[1024,512]{1,0:T(8,128)(2,1)} %w_proj_ref.1) | copy-start | bytes 3145732
  1.0 38.9 %copy-start.4 = (bf16[512]{0:T(512)(128)(2,1)S(1)}, bf16[512]{0:T(512)(128)(2,1)}, u32[]{:S(2)}) copy-start(bf16[512]{0:T(512)(128)(2,1)} %param.15) | copy-start | bytes 3076
  1.0 48.2 %slice-start.1 = ((s8[16777216]{0:T(1024)(128)(4,1)}), s8[4194304]{0:T(1024)(128)(4,1)S(1)}, s32[]{:S(2)}) async-start(s8[16777216]{0:T(1024)(128)(4,1)} %bitcast.6), calls=%async_computation.4 | async-start | bytes 8388608
  1.0 48.2 %slice-start.2 = ((s8[16777216]{0:T(1024)(128)(4,1)}), s8[4194304]{0:T(1024)(128)(4,1)S(1)}, s32[]{:S(2)}) async-start(s8[16777216]{0:T(1024)(128)(4,1)} %bitcast.6), calls=%async_computation.5 | async-start | bytes 8388608
  1.1 48.2 %slice-start.3 = ((s8[16777216]{0:T(1024)(128)(4,1)}), s8[4194304]{0:T(1024)(128)(4,1)S(1)}, s32[]{:S(2)}) async-start(s8[16777216]{0:T(1024)(128)(4,1)} %bitcast.6), calls=%async_computation.6 | async-start | bytes 8388608
  1.1 48.2 %slice-start.5 = ((s8[16777216]{0:T(1024)(128)(4,1)}), s8[4194304]{0:T(1024)(128)(4,1)S(1)}, s32[]{:S(2)}) async-start(s8[16777216]{0:T(1024)(128)(4,1)} %bitcast.8), calls=%async_computation.8 | async-start | bytes 8388608
  1.1 48.2 %slice-start.6 = ((s8[16777216]{0:T(1024)(128)(4,1)}), s8[4194304]{0:T(1024)(128)(4,1)S(1)}, s32[]{:S(2)}) async-start(s8[16777216]{0:T(1024)(128)(4,1)} %bitcast.8), calls=%async_computation.9 | async-start | bytes 8388608
  1.1 48.2 %slice-start.7 = ((s8[16777216]{0:T(1024)(128)(4,1)}), s8[4194304]{0:T(1024)(128)(4,1)S(1)}, s32[]{:S(2)}) async-start(s8[16777216]{0:T(1024)(128)(4,1)} %bitcast.8), calls=%async_computation.10 | async-start | bytes 8388608
  40.3 6.7 %collective-permute-start.2 = (bf16[64,512]{1,0:T(8,128)(2,1)S(1)}, bf16[64,512]{1,0:T(8,128)(2,1)S(1)}, u32[]{:S(2)}, u32[]{:S(2)}) collective-permute-start(bf16[64,512]{1,0:T(8,128)(2,1)S(1)} %project.1), channel_id=1, source_target_pairs={{0,12},{4,8},{8,4},{12,0},{1,13},{5,9},{9,5},{13,1},{2,14},{6,10},... | collective-permute-start | bytes 196616 | tf_op jit(solution)/shard_map/ppermute | solution.py:339
  41.0 7.3 %collective-permute-start.1 = (bf16[64,512]{1,0:T(8,128)(2,1)S(1)}, bf16[64,512]{1,0:T(8,128)(2,1)S(1)}, u32[]{:S(2)}, u32[]{:S(2)}) collective-permute-start(bf16[64,512]{1,0:T(8,128)(2,1)S(1)} %project.1), channel_id=1, source_target_pairs={{0,8},{4,12},{8,0},{12,4},{1,9},{5,13},{9,1},{13,5},{2,10},{6,14},... | collective-permute-start | bytes 196616 | tf_op jit(solution)/shard_map/ppermute | solution.py:339
  41.2 7.1 %collective-permute-start = (bf16[64,512]{1,0:T(8,128)(2,1)S(1)}, bf16[64,512]{1,0:T(8,128)(2,1)S(1)}, u32[]{:S(2)}, u32[]{:S(2)}) collective-permute-start(bf16[64,512]{1,0:T(8,128)(2,1)S(1)} %project.1), channel_id=1, source_target_pairs={{0,4},{4,0},{8,12},{12,8},{1,5},{5,1},{9,13},{13,9},{2,6},{6,2},{1... | collective-permute-start | bytes 196616 | tf_op jit(solution)/shard_map/ppermute | solution.py:339
  48.3 2.7 %collective-permute-start.4 = (bf16[4,64,512]{2,1,0:T(8,128)(2,1)S(1)}, bf16[4,64,512]{2,1,0:T(8,128)(2,1)S(1)}, u32[]{:S(2)}, u32[]{:S(2)}) collective-permute-start(bf16[4,64,512]{2,1,0:T(8,128)(2,1)S(1)} %pad_maximum_fusion.refs_1_), channel_id=1, source_target_pairs={{0,1},{1,0},{2,3},{3,2},{4,5},{5,4},{6,7},{7,6},{8,9},{9,8},{10,11... | collective-permute-start | bytes 786440 | tf_op jit(solution)/shard_map/ppermute | solution.py:339
  48.4 8.7 %collective-permute-start.3 = (bf16[4,64,512]{2,1,0:T(8,128)(2,1)S(1)}, bf16[4,64,512]{2,1,0:T(8,128)(2,1)S(1)}, u32[]{:S(2)}, u32[]{:S(2)}) collective-permute-start(bf16[4,64,512]{2,1,0:T(8,128)(2,1)S(1)} %pad_maximum_fusion.refs_1_), channel_id=1, source_target_pairs={{0,2},{2,0},{1,3},{3,1},{4,6},{6,4},{5,7},{7,5},{8,10},{10,8},{9,1... | collective-permute-start | bytes 786440 | tf_op jit(solution)/shard_map/ppermute | solution.py:339
  57.1 1.8 %collective-permute-start.5 = (bf16[4,64,512]{2,1,0:T(8,128)(2,1)S(1)}, bf16[4,64,512]{2,1,0:T(8,128)(2,1)S(1)}, u32[]{:S(2)}, u32[]{:S(2)}) collective-permute-start(bf16[4,64,512]{2,1,0:T(8,128)(2,1)S(1)} %collective-permute-done.3.refs_1_), channel_id=1, source_target_pairs={{0,1},{1,0},{2,3},{3,2},{4,5},{5,4},{6,7},{7,6},{8,9},{9,8},{10,11... | collective-permute-start | bytes 786440 | tf_op jit(solution)/shard_map/ppermute | solution.py:339

commit v4 on v3

--- a/solution.py
+++ b/solution.py
@@ -15,6 +15,7 @@
 NORM_EPS = 1e-05
 SCORE_SCALE = 0.125
 DIRECT = 4
+NEAR = 4
 MIB = 1 << 20
 COVER_FLOPS = 20_000_000_000
 F32 = jnp.float32
@@ -112,7 +113,6 @@
     frames, packed, half = rows_ref.shape
     own = packed // 2
     width = 2 * half
-    heads = width // HEAD_DIM
     seq = frames * TOKL
     videos = frames * own // seq
     raw = rows_ref[...].astype(F32)
@@ -227,17 +227,17 @@
     return squares
 
 
-def place_rule(index_ref, outer, flip):
+def place_rule(index_ref, source):
+    flip, steps, direct = source
     me = jnp.max(index_ref[0, :1, KMAX + 1 : KMAX + 2]).astype(jnp.int32)
-    quad = index_ref.shape[0] // outer
-    row = me // quad
-    near = jnp.bitwise_xor(me - row * quad, flip)
-    if outer <= DIRECT:
-        return lambda i: jnp.bitwise_xor(row, i) * quad + near
-    return lambda i: i * quad + near
-
-
-def partial_kernel(flip, videos, *refs):
+    row = me // NEAR
+    near = jnp.bitwise_xor(me - row * NEAR, flip)
+    if direct:
+        return lambda i: jnp.bitwise_xor(row, steps[i]) * NEAR + near
+    return lambda i: steps[i] * NEAR + near
+
+
+def partial_kernel(source, videos, *refs):
     index_ref, rows_ref, w_gate_ref, w_up_ref = refs[:4]
     gate_ref, up_ref, squares_ref = refs[-3:]
     begun = refs[4:7] if len(refs) > 7 else None
@@ -246,19 +246,19 @@
         gate_ref[:, first : first + block] = gate
         up_ref[:, first : first + block] = up
 
-    rule = place_rule(index_ref, rows_ref.shape[0], flip)
+    rule = place_rule(index_ref, source)
     squares_ref[...] = products(
         rule, videos, index_ref, rows_ref, w_gate_ref, w_up_ref, begun, emit
     )
 
 
-def final_kernel(flip, index_ref, rows_ref, w_gate_ref, w_up_ref, gate_ref, up_ref, squares_ref,
+def final_kernel(source, index_ref, rows_ref, w_gate_ref, w_up_ref, gate_ref, up_ref, squares_ref,
                  out_ref, gate_sum, up_sum):
     def emit(first, block, gate, up):
         gate_sum[:, first : first + block] = gate
         up_sum[:, first : first + block] = up
 
-    rule = place_rule(index_ref, rows_ref.shape[0], flip)
+    rule = place_rule(index_ref, source)
     begun = (gate_ref, up_ref, squares_ref)
     squares = products(
         rule, out_ref.shape[0], index_ref, rows_ref, w_gate_ref, w_up_ref, begun, emit
@@ -269,8 +269,8 @@
     out_ref[...] = hidden.astype(BF16).reshape(out_ref.shape)
 
 
-def local(video, w_qkv, w_out, keep_list, kept_counts, w_proj, llm_gain, w_gate, w_up):
-    videos, _, patches, width = video.shape
+def program(video, w_qkv, w_out, keep_list, kept_counts, w_proj, llm_gain, w_gate, w_up):
+    videos, _, _, width = video.shape
     axes = ("outer", "mid", "cores")
     frames, outer = lax.axis_size(axes), lax.axis_size("outer")
     seq = frames * TOKL
@@ -338,39 +338,48 @@
         pairs = [(i, i ^ flip) for i in range(lax.axis_size(axis))]
         return lax.ppermute(values, axis, pairs)
 
-    if outer <= DIRECT:
-        line = jnp.stack([gained] + [swap(gained, "outer", k) for k in range(1, outer)])
-    else:
-        line = spread(jnp.broadcast_to(gained[None], (outer,) + gained.shape), "outer")
     units = w_gate.shape[1]
     part = jax.ShapeDtypeStruct((tokens, units), F32)
     sums = (part, part, jax.ShapeDtypeStruct((tokens, LANES), F32))
     work = pl.CostEstimate(
-        flops=tokens * w_gate.shape[0] * units,
-        bytes_accessed=w_gate.shape[0] * units,
+        flops=tokens * w_gate.shape[0] * units // 2,
+        bytes_accessed=w_gate.shape[0] * units // 2,
         transcendentals=0,
     )
 
-    def add(name, flip, block, begun):
+    def add(source, block, begun):
         return pl.pallas_call(
-            functools.partial(partial_kernel, flip, videos),
+            functools.partial(partial_kernel, source, videos),
             out_shape=sums,
             in_specs=[whole()] * (4 + len(begun)),
             out_specs=(whole(), whole(), whole()),
             compiler_params=params(3 * MIB + 20 * tokens * units),
             cost_estimate=work,
-            name=name,
+            name="part",
         )(index, block, w_gate, w_up, *begun)
 
-    line_mid = swap(line, "mid")
-    line_core = swap(line, "cores")
-    begun = add("own", 0, line, ())
-    begun = add("core", 1, line_core, begun)
-    line_mid, begun = lax.optimization_barrier((line_mid, begun))
-    line_both = swap(line_mid, "cores")
-    begun = add("mid", 2, line_mid, begun)
+    direct = outer <= DIRECT
+    if direct:
+        blocks = [gained] + [swap(gained, "outer", k) for k in range(1, outer)]
+        groups = [tuple(range(outer))[i : i + 2] for i in range(0, outer, 2)]
+        lines = [jnp.stack([blocks[i] for i in steps]) for steps in groups]
+    else:
+        groups = [tuple(range(outer))]
+        lines = [spread(jnp.broadcast_to(gained[None], (outer,) + gained.shape), "outer")]
+    begun = ()
+    mids = []
+    for steps, line in zip(groups, lines):
+        mids.append(swap(line, "mid"))
+        line_core = swap(line, "cores")
+        begun = add((0, steps, direct), line, begun)
+        begun = add((1, steps, direct), line_core, begun)
+    for i, steps in enumerate(groups):
+        line_core = swap(mids[i], "cores")
+        begun = add((2, steps, direct), mids[i], begun)
+        if i + 1 < len(groups):
+            begun = add((3, steps, direct), line_core, begun)
     return pl.pallas_call(
-        functools.partial(final_kernel, 3),
+        functools.partial(final_kernel, (3, groups[-1], direct)),
         out_shape=jax.ShapeDtypeStruct((videos, seq, units), BF16),
         in_specs=[whole()] * 7,
         out_specs=whole(),
@@ -378,7 +387,7 @@
         compiler_params=params(3 * MIB + 24 * tokens * units),
         cost_estimate=work,
         name="final",
-    )(index, line_both, w_gate, w_up, *begun)
+    )(index, line_core, w_gate, w_up, *begun)
 
 
 def solution(mesh):
@@ -398,4 +407,6 @@
         P(None, spread),
     )
     out_specs = P("groups", None, spread)
-    return jax.shard_map(local, mesh=split, in_specs=in_specs, out_specs=out_specs, check_vma=False)
+    return jax.shard_map(
+        program, mesh=split, in_specs=in_specs, out_specs=out_specs, check_vma=False
+    )

time: 61.7 us -> 61.8 us (level)
  waiting for transfers between devices: 7.8 us -> 6.34 us
  Pallas kernels: 12.6 us -> 13.6 us
    ppermute x6 -> x9, waiting for transfers between devices: 7.8 us -> 6.34 us  [swap(): return lax.ppermute(values, axis, pairs)]
    pallas_call x9 -> x13, Pallas kernels: 12.6 us -> 13.6 us  [the longest x7 7.15 us: add(): pl.pallas_call(functools.partial(partial_kernel, source, videos), out_sha...]
    ppermute x6 -> x9, starting transfers between devices: 5.32 us -> 5.82 us  [swap(): return lax.ppermute(values, axis, pairs)]
  transfers between devices with their start and end apart: 6 -> 9, of which waited for: 3 -> 4; matrix products, arithmetic and copies ran while one was open for 0% -> 0% of each run, Pallas kernels for 9% -> 12%
where the time goes in v4:
time: 61.8 us; the launch traced here: 61.6 us
  blocking collectives  35.4 us (57%)
  Pallas kernels  13.6 us (22%)
  waiting for transfers between devices  6.34 us (10%)
  starting transfers between devices  5.82 us (9%)
    all_to_all x1, blocking collectives, program(): index = spread(message, axes)  14.4 us
    all_to_all x1, blocking collectives, program(): seen = spread(chosen, axes)  10.5 us
    all_to_all x1, blocking collectives, program(): token_rows = spread(encoded, axes)  10.5 us
    pallas_call x7, Pallas kernels, add(): pl.pallas_call(functools.partial(partial_kernel, source, videos), out_sha...  7.15 us
    ppermute x9, waiting for transfers between devices, swap(): return lax.ppermute(values, axis, pairs)  6.34 us
    ppermute x9, starting transfers between devices, swap(): return lax.ppermute(values, axis, pairs)  5.82 us
    pallas_call x1, Pallas kernels, program(): pl.pallas_call(attend_kernel, out_shape=jax.ShapeDtypeStruct((frames, pac...  2.4 us
    pallas_call x1, Pallas kernels, program(): pl.pallas_call(functools.partial(final_kernel, (3, groups[-1], direct)),...  1.71 us
  transfers between devices with their start and end apart: 9, of which 4 were waited for; matrix products, arithmetic and copies ran while one was open for 0% of the time, Pallas kernels for 12%

profile of v4, /device:TPU:0, one launch (start us, length us, event | category | flops | bytes accessed | tf_op | source)
XLA Modules:
  0.0 61.6 jit_solution(7499056593939318216)
XLA Ops:
  0.0 1.0 %collect.1.message_ref = f32[8,128]{1,0:T(8,128)S(1)} custom-call(s32[1,2]{1,0:T(1,128)} %bitcast.16, s32[2,1,128]{2,1,0:T(1,128)} %keep_hbm.1, bf16[4,128]{1,0:T(4,128)(2,1)} %bitcast.11), custom_call_target="tpu_custom_call" | custom-call | tf_op jit(solution)/shard_map/collect/pallas_call | solution.py:287
  1.1 14.4 %all_to_all.15.index_ref.refs_0_ = f32[16,8,128]{2,1,0:T(8,128)S(1)} all-to-all(f32[16,8,128]{2,1,0:T(8,128)S(1)} %index.1), channel_id=1, replica_groups=mesh['groups'=2,'outer'=4,'mid'=2,'cores'=2] {'outer','mid','cores'}, dimensions={0} | all-to-all | bytes 131072 | tf_op jit(solution)/shard_map/all_to_all | solution.py:306
  15.5 1.0 %select.1 = bf16[16,8,512]{2,1,0:T(8,128)(2,1)S(1)} custom-call(f32[16,8,128]{2,1,0:T(8,128)S(1)} %all_to_all.15.index_ref.refs_0_, bf16[2,1,128,1024]{3,2,1,0:T(8,128)(2,1)S(1)} %copy-done.3), custom_call_target="tpu_custom_call" | custom-call | tf_op jit(solution)/shard_map/select/pallas_call | solution.py:308
  16.5 10.5 %all_to_all.16.rows_ref = bf16[16,8,512]{2,1,0:T(8,128)(2,1)S(1)} all-to-all(bf16[16,8,512]{2,1,0:T(8,128)(2,1)S(1)} %select.1), channel_id=1, replica_groups=mesh['groups'=2,'outer'=4,'mid'=2,'cores'=2] {'outer','mid','cores'}, dimensions={0} | all-to-all | bytes 262144 | tf_op jit(solution)/shard_map/all_to_all | solution.py:316
  27.0 2.4 %attend.1 = bf16[16,8,512]{2,1,0:T(8,128)(2,1)S(1)} custom-call(f32[16,8,128]{2,1,0:T(8,128)S(1)} %all_to_all.15.index_ref.refs_0_, bf16[16,8,512]{2,1,0:T(8,128)(2,1)S(1)} %all_to_all.16.rows_ref, bf16[1024,3072]{1,0:T(8,128)(2,1)S(1)} %copy-done, bf16[1024,1024]{1,0:T(8,128)(2,1)S(1)} %copy-done.1), custom_call_target="tpu_custom_call" | custom-call | tf_op jit(solution)/shard_map/attend/pallas_call | solution.py:318
  29.4 10.5 %all_to_all.17.rows_ref = bf16[16,8,512]{2,1,0:T(8,128)(2,1)S(1)} all-to-all(bf16[16,8,512]{2,1,0:T(8,128)(2,1)S(1)} %attend.1), channel_id=1, replica_groups=mesh['groups'=2,'outer'=4,'mid'=2,'cores'=2] {'outer','mid','cores'}, dimensions={0} | all-to-all | bytes 262144 | tf_op jit(solution)/shard_map/all_to_all | solution.py:326
  39.9 0.4 project.1
  40.3 0.1 collective-permute-start.4
  40.4 1.2 %collective-permute-start = (bf16[64,512]{1,0:T(8,128)(2,1)S(1)}, bf16[64,512]{1,0:T(8,128)(2,1)S(1)}, u32[]{:S(2)}, u32[]{:S(2)}) collective-permute-start(bf16[64,512]{1,0:T(8,128)(2,1)S(1)} %project.1), channel_id=1, source_target_pairs={{0,8},{4,12},{8,0},{12,4},{1,9},{5,13},{9,1},{13,5},{2,10},{6,14},... | collective-permute-start | bytes 196616 | tf_op jit(solution)/shard_map/ppermute | solution.py:339
  41.6 3.2 %collective-permute-start.1 = (bf16[64,512]{1,0:T(8,128)(2,1)S(1)}, bf16[64,512]{1,0:T(8,128)(2,1)S(1)}, u32[]{:S(2)}, u32[]{:S(2)}) collective-permute-start(bf16[64,512]{1,0:T(8,128)(2,1)S(1)} %project.1), channel_id=1, source_target_pairs={{0,12},{4,8},{8,4},{12,0},{1,13},{5,9},{9,5},{13,1},{2,14},{6,10},... | collective-permute-start | bytes 196616 | tf_op jit(solution)/shard_map/ppermute | solution.py:339
  44.8 0.3 collective-permute-done.4
  45.1 3.4 %collective-permute-done = bf16[64,512]{1,0:T(8,128)(2,1)S(1)} collective-permute-done((bf16[64,512]{1,0:T(8,128)(2,1)S(1)}, bf16[64,512]{1,0:T(8,128)(2,1)S(1)}, u32[]{:S(2)}, u32[]{:S(2)}) %collective-permute-start) | collective-permute-done | bytes 65568 | tf_op jit(solution)/shard_map/ppermute | solution.py:339
  48.6 0.8 %collective-permute-start.2 = (bf16[2,64,512]{2,1,0:T(8,128)(2,1)S(1)}, bf16[2,64,512]{2,1,0:T(8,128)(2,1)S(1)}, u32[]{:S(2)}, u32[]{:S(2)}) collective-permute-start(bf16[2,64,512]{2,1,0:T(8,128)(2,1)S(1)} %pad_maximum_fusion.refs_1_), channel_id=1, source_target_pairs={{0,2},{2,0},{1,3},{3,1},{4,6},{6,4},{5,7},{7,5},{8,10},{10,8},{9,1... | collective-permute-start | bytes 393224 | tf_op jit(solution)/shard_map/ppermute | solution.py:339
  49.4 0.5 collective-permute-start.7
  49.9 1.4 %collective-permute-done.5.refs_1_ = bf16[2,64,512]{2,1,0:T(8,128)(2,1)S(1)} collective-permute-done((bf16[2,64,512]{2,1,0:T(8,128)(2,1)S(1)}, bf16[2,64,512]{2,1,0:T(8,128)(2,1)S(1)}, u32[]{:S(2)}, u32[]{:S(2)}) %collective-permute-start.5) | collective-permute-done | bytes 131104 | tf_op jit(solution)/shard_map/ppermute | solution.py:339
  51.4 1.0 %part.7 = (f32[64,1024]{1,0:T(8,128)S(1)}, f32[64,1024]{1,0:T(8,128)S(1)}, f32[64,128]{1,0:T(8,128)S(1)}) custom-call(f32[16,8,128]{2,1,0:T(8,128)S(1)} %all_to_all.15.index_ref.refs_0_, bf16[2,64,512]{2,1,0:T(8,128)(2,1)S(1)} %pad_maximum_fusion.1.refs_1_, bf16[8192,1024]{1,0:T(8,128)(2,1)S(1)} %bitcast.7, bf16[8192,1024]{1,0:T(8,128)(2,1)S(1)} %bitcast.9), custom_call_target="tpu_custom_call" | custom-call | flops 268435456 | bytes 4194304 | tf_op jit(solution)/shard_map/part/pallas_call | solution.py:351
  52.4 1.2 %collective-permute-done.2.refs_1_ = bf16[2,64,512]{2,1,0:T(8,128)(2,1)S(1)} collective-permute-done((bf16[2,64,512]{2,1,0:T(8,128)(2,1)S(1)}, bf16[2,64,512]{2,1,0:T(8,128)(2,1)S(1)}, u32[]{:S(2)}, u32[]{:S(2)}) %collective-permute-start.2) | collective-permute-done | bytes 131104 | tf_op jit(solution)/shard_map/ppermute | solution.py:339
  53.6 1.0 %part.8 = (f32[64,1024]{1,0:T(8,128)S(1)}, f32[64,1024]{1,0:T(8,128)S(1)}, f32[64,128]{1,0:T(8,128)S(1)}) custom-call(f32[16,8,128]{2,1,0:T(8,128)S(1)} %all_to_all.15.index_ref.refs_0_, bf16[2,64,512]{2,1,0:T(8,128)(2,1)S(1)} %collective-permute-done.8.refs_1_, bf16[8192,1024]{1,0:T(8,128)(2,1)S(1)} %bitcast.7, bf16[8192,1024]{1,0:T(8,128)(2,1)S(1)} %bitcast.9, ...), custom_call_target="tpu_custom_call" | custom-call | flops 268435456 | bytes 4194304 | tf_op jit(solution)/shard_map/part/pallas_call | solution.py:351
  54.7 1.0 %part.9 = (f32[64,1024]{1,0:T(8,128)S(1)}, f32[64,1024]{1,0:T(8,128)S(1)}, f32[64,128]{1,0:T(8,128)S(1)}) custom-call(f32[16,8,128]{2,1,0:T(8,128)S(1)} %all_to_all.15.index_ref.refs_0_, bf16[2,64,512]{2,1,0:T(8,128)(2,1)S(1)} %pad_maximum_fusion.refs_1_, bf16[8192,1024]{1,0:T(8,128)(2,1)S(1)} %bitcast.7, bf16[8192,1024]{1,0:T(8,128)(2,1)S(1)} %bitcast.9, ...), custom_call_target="tpu_custom_call" | custom-call | flops 268435456 | bytes 4194304 | tf_op jit(solution)/shard_map/part/pallas_call | solution.py:351
  55.7 1.0 %part.10 = (f32[64,1024]{1,0:T(8,128)S(1)}, f32[64,1024]{1,0:T(8,128)S(1)}, f32[64,128]{1,0:T(8,128)S(1)}) custom-call(f32[16,8,128]{2,1,0:T(8,128)S(1)} %all_to_all.15.index_ref.refs_0_, bf16[2,64,512]{2,1,0:T(8,128)(2,1)S(1)} %collective-permute-done.7.refs_1_, bf16[8192,1024]{1,0:T(8,128)(2,1)S(1)} %bitcast.7, bf16[8192,1024]{1,0:T(8,128)(2,1)S(1)} %bitcast.9, ...), custom_call_target="tpu_custom_call" | custom-call | flops 268435456 | bytes 4194304 | tf_op jit(solution)/shard_map/part/pallas_call | solution.py:351
  56.7 1.0 %part.11 = (f32[64,1024]{1,0:T(8,128)S(1)}, f32[64,1024]{1,0:T(8,128)S(1)}, f32[64,128]{1,0:T(8,128)S(1)}) custom-call(f32[16,8,128]{2,1,0:T(8,128)S(1)} %all_to_all.15.index_ref.refs_0_, bf16[2,64,512]{2,1,0:T(8,128)(2,1)S(1)} %collective-permute-done.5.refs_1_, bf16[8192,1024]{1,0:T(8,128)(2,1)S(1)} %bitcast.7, bf16[8192,1024]{1,0:T(8,128)(2,1)S(1)} %bitcast.9, ...), custom_call_target="tpu_custom_call" | custom-call | flops 268435456 | bytes 4194304 | tf_op jit(solution)/shard_map/part/pallas_call | solution.py:351
  57.8 1.0 %part.12 = (f32[64,1024]{1,0:T(8,128)S(1)}, f32[64,1024]{1,0:T(8,128)S(1)}, f32[64,128]{1,0:T(8,128)S(1)}) custom-call(f32[16,8,128]{2,1,0:T(8,128)S(1)} %all_to_all.15.index_ref.refs_0_, bf16[2,64,512]{2,1,0:T(8,128)(2,1)S(1)} %collective-permute-done.6.refs_1_, bf16[8192,1024]{1,0:T(8,128)(2,1)S(1)} %bitcast.7, bf16[8192,1024]{1,0:T(8,128)(2,1)S(1)} %bitcast.9, ...), custom_call_target="tpu_custom_call" | custom-call | flops 268435456 | bytes 4194304 | tf_op jit(solution)/shard_map/part/pallas_call | solution.py:351
  58.8 1.0 %part.13 = (f32[64,1024]{1,0:T(8,128)S(1)}, f32[64,1024]{1,0:T(8,128)S(1)}, f32[64,128]{1,0:T(8,128)S(1)}) custom-call(f32[16,8,128]{2,1,0:T(8,128)S(1)} %all_to_all.15.index_ref.refs_0_, bf16[2,64,512]{2,1,0:T(8,128)(2,1)S(1)} %collective-permute-done.2.refs_1_, bf16[8192,1024]{1,0:T(8,128)(2,1)S(1)} %bitcast.7, bf16[8192,1024]{1,0:T(8,128)(2,1)S(1)} %bitcast.9, ...), custom_call_target="tpu_custom_call" | custom-call | flops 268435456 | bytes 4194304 | tf_op jit(solution)/shard_map/part/pallas_call | solution.py:351
  59.8 1.7 %final.1 = bf16[2,32,1024]{2,1,0:T(8,128)(2,1)} custom-call(f32[16,8,128]{2,1,0:T(8,128)S(1)} %all_to_all.15.index_ref.refs_0_, bf16[2,64,512]{2,1,0:T(8,128)(2,1)S(1)} %collective-permute-done.3.rows_ref, bf16[8192,1024]{1,0:T(8,128)(2,1)S(1)} %bitcast.7, bf16[8192,1024]{1,0:T(8,128)(2,1)S(1)} %bitcast.9, f32[64,1024]{1,0:T(8,128)S(1)} %get-tuple-element.44.gate_ref, ...), custom_call_target="tpu_custom_call" | custom-call | flops 268435456 | bytes 4194304 | tf_op jit(solution)/shard_map/final/pallas_call | solution.py:381
  (40 shorter events, 0.2 us)
Async XLA Ops:
  0.0 51.3 %slice-start = ((s8[16777216]{0:T(1024)(128)(4,1)}), s8[4194304]{0:T(1024)(128)(4,1)S(1)}, s32[]{:S(2)}) async-start(s8[16777216]{0:T(1024)(128)(4,1)} %bitcast.6), calls=%async_computation.3 | async-start | bytes 8388608
  0.0 51.3 %slice-start.4 = ((s8[16777216]{0:T(1024)(128)(4,1)}), s8[4194304]{0:T(1024)(128)(4,1)S(1)}, s32[]{:S(2)}) async-start(s8[16777216]{0:T(1024)(128)(4,1)} %bitcast.8), calls=%async_computation.7 | async-start | bytes 8388608
  1.0 14.5 %copy-start.3 = (bf16[2,1,128,1024]{3,2,1,0:T(8,128)(2,1)S(1)}, bf16[2,1,128,1024]{3,2,1,0:T(8,128)(2,1)}, u32[]{:S(2)}) copy-start(bf16[2,1,128,1024]{3,2,1,0:T(8,128)(2,1)} %video_ref.1) | copy-start | bytes 1572868
  1.0 26.0 %copy-start = (bf16[1024,3072]{1,0:T(8,128)(2,1)S(1)}, bf16[1024,3072]{1,0:T(8,128)(2,1)}, u32[]{:S(2)}) copy-start(bf16[1024,3072]{1,0:T(8,128)(2,1)} %w_qkv_ref.1) | copy-start | bytes 18874372
  1.0 26.0 %copy-start.1 = (bf16[1024,1024]{1,0:T(8,128)(2,1)S(1)}, bf16[1024,1024]{1,0:T(8,128)(2,1)}, u32[]{:S(2)}) copy-start(bf16[1024,1024]{1,0:T(8,128)(2,1)} %w_out_ref.1) | copy-start | bytes 6291460
  1.0 38.9 %copy-start.2 = (bf16[1024,512]{1,0:T(8,128)(2,1)S(1)}, bf16[1024,512]{1,0:T(8,128)(2,1)}, u32[]{:S(2)}) copy-start(bf16[1024,512]{1,0:T(8,128)(2,1)} %w_proj_ref.1) | copy-start | bytes 3145732
  1.0 38.9 %copy-start.4 = (bf16[512]{0:T(512)(128)(2,1)S(1)}, bf16[512]{0:T(512)(128)(2,1)}, u32[]{:S(2)}) copy-start(bf16[512]{0:T(512)(128)(2,1)} %param.15) | copy-start | bytes 3076
  1.0 50.3 %slice-start.1 = ((s8[16777216]{0:T(1024)(128)(4,1)}), s8[4194304]{0:T(1024)(128)(4,1)S(1)}, s32[]{:S(2)}) async-start(s8[16777216]{0:T(1024)(128)(4,1)} %bitcast.6), calls=%async_computation.4 | async-start | bytes 8388608
  1.0 50.3 %slice-start.2 = ((s8[16777216]{0:T(1024)(128)(4,1)}), s8[4194304]{0:T(1024)(128)(4,1)S(1)}, s32[]{:S(2)}) async-start(s8[16777216]{0:T(1024)(128)(4,1)} %bitcast.6), calls=%async_computation.5 | async-start | bytes 8388608
  1.1 50.3 %slice-start.3 = ((s8[16777216]{0:T(1024)(128)(4,1)}), s8[4194304]{0:T(1024)(128)(4,1)S(1)}, s32[]{:S(2)}) async-start(s8[16777216]{0:T(1024)(128)(4,1)} %bitcast.6), calls=%async_computation.6 | async-start | bytes 8388608
  1.1 50.3 %slice-start.5 = ((s8[16777216]{0:T(1024)(128)(4,1)}), s8[4194304]{0:T(1024)(128)(4,1)S(1)}, s32[]{:S(2)}) async-start(s8[16777216]{0:T(1024)(128)(4,1)} %bitcast.8), calls=%async_computation.8 | async-start | bytes 8388608
  1.1 50.3 %slice-start.6 = ((s8[16777216]{0:T(1024)(128)(4,1)}), s8[4194304]{0:T(1024)(128)(4,1)S(1)}, s32[]{:S(2)}) async-start(s8[16777216]{0:T(1024)(128)(4,1)} %bitcast.8), calls=%async_computation.9 | async-start | bytes 8388608
  1.1 50.3 %slice-start.7 = ((s8[16777216]{0:T(1024)(128)(4,1)}), s8[4194304]{0:T(1024)(128)(4,1)S(1)}, s32[]{:S(2)}) async-start(s8[16777216]{0:T(1024)(128)(4,1)} %bitcast.8), calls=%async_computation.10 | async-start | bytes 8388608
  40.3 4.7 %collective-permute-start.4 = (bf16[64,512]{1,0:T(8,128)(2,1)S(1)}, bf16[64,512]{1,0:T(8,128)(2,1)S(1)}, u32[]{:S(2)}, u32[]{:S(2)}) collective-permute-start(bf16[64,512]{1,0:T(8,128)(2,1)S(1)} %project.1), channel_id=1, source_target_pairs={{0,4},{4,0},{8,12},{12,8},{1,5},{5,1},{9,13},{13,9},{2,6},{6,2},{1... | collective-permute-start | bytes 196616 | tf_op jit(solution)/shard_map/ppermute | solution.py:339
  40.4 8.1 %collective-permute-start = (bf16[64,512]{1,0:T(8,128)(2,1)S(1)}, bf16[64,512]{1,0:T(8,128)(2,1)S(1)}, u32[]{:S(2)}, u32[]{:S(2)}) collective-permute-start(bf16[64,512]{1,0:T(8,128)(2,1)S(1)} %project.1), channel_id=1, source_target_pairs={{0,8},{4,12},{8,0},{12,4},{1,9},{5,13},{9,1},{13,5},{2,10},{6,14},... | collective-permute-start | bytes 196616 | tf_op jit(solution)/shard_map/ppermute | solution.py:339
  41.6 7.0 %collective-permute-start.1 = (bf16[64,512]{1,0:T(8,128)(2,1)S(1)}, bf16[64,512]{1,0:T(8,128)(2,1)S(1)}, u32[]{:S(2)}, u32[]{:S(2)}) collective-permute-start(bf16[64,512]{1,0:T(8,128)(2,1)S(1)} %project.1), channel_id=1, source_target_pairs={{0,12},{4,8},{8,4},{12,0},{1,13},{5,9},{9,5},{13,1},{2,14},{6,10},... | collective-permute-start | bytes 196616 | tf_op jit(solution)/shard_map/ppermute | solution.py:339
  45.1 6.3 %collective-permute-start.5 = (bf16[2,64,512]{2,1,0:T(8,128)(2,1)S(1)}, bf16[2,64,512]{2,1,0:T(8,128)(2,1)S(1)}, u32[]{:S(2)}, u32[]{:S(2)}) collective-permute-start(bf16[2,64,512]{2,1,0:T(8,128)(2,1)S(1)} %pad_maximum_fusion.1.refs_1_), channel_id=1, source_target_pairs={{0,2},{2,0},{1,3},{3,1},{4,6},{6,4},{5,7},{7,5},{8,10},{10,8},{9,1... | collective-permute-start | bytes 393224 | tf_op jit(solution)/shard_map/ppermute | solution.py:339
  48.6 5.0 %collective-permute-start.2 = (bf16[2,64,512]{2,1,0:T(8,128)(2,1)S(1)}, bf16[2,64,512]{2,1,0:T(8,128)(2,1)S(1)}, u32[]{:S(2)}, u32[]{:S(2)}) collective-permute-start(bf16[2,64,512]{2,1,0:T(8,128)(2,1)S(1)} %pad_maximum_fusion.refs_1_), channel_id=1, source_target_pairs={{0,2},{2,0},{1,3},{3,1},{4,6},{6,4},{5,7},{7,5},{8,10},{10,8},{9,1... | collective-permute-start | bytes 393224 | tf_op jit(solution)/shard_map/ppermute | solution.py:339
  49.4 4.2 %collective-permute-start.8 = (bf16[2,64,512]{2,1,0:T(8,128)(2,1)S(1)}, bf16[2,64,512]{2,1,0:T(8,128)(2,1)S(1)}, u32[]{:S(2)}, u32[]{:S(2)}) collective-permute-start(bf16[2,64,512]{2,1,0:T(8,128)(2,1)S(1)} %pad_maximum_fusion.1.refs_1_), channel_id=1, source_target_pairs={{0,1},{1,0},{2,3},{3,2},{4,5},{5,4},{6,7},{7,6},{8,9},{9,8},{10,11... | collective-permute-start | bytes 393224 | tf_op jit(solution)/shard_map/ppermute | solution.py:339
  49.4 6.3 %collective-permute-start.7 = (bf16[2,64,512]{2,1,0:T(8,128)(2,1)S(1)}, bf16[2,64,512]{2,1,0:T(8,128)(2,1)S(1)}, u32[]{:S(2)}, u32[]{:S(2)}) collective-permute-start(bf16[2,64,512]{2,1,0:T(8,128)(2,1)S(1)} %pad_maximum_fusion.refs_1_), channel_id=1, source_target_pairs={{0,1},{1,0},{2,3},{3,2},{4,5},{5,4},{6,7},{7,6},{8,9},{9,8},{10,11... | collective-permute-start | bytes 393224 | tf_op jit(solution)/shard_map/ppermute | solution.py:339
  51.3 6.5 %collective-permute-start.6 = (bf16[2,64,512]{2,1,0:T(8,128)(2,1)S(1)}, bf16[2,64,512]{2,1,0:T(8,128)(2,1)S(1)}, u32[]{:S(2)}, u32[]{:S(2)}) collective-permute-start(bf16[2,64,512]{2,1,0:T(8,128)(2,1)S(1)} %collective-permute-done.5.refs_1_), channel_id=1, source_target_pairs={{0,1},{1,0},{2,3},{3,2},{4,5},{5,4},{6,7},{7,6},{8,9},{9,8},{10,11... | collective-permute-start | bytes 393224 | tf_op jit(solution)/shard_map/ppermute | solution.py:339
  53.6 6.2 %collective-permute-start.3 = (bf16[2,64,512]{2,1,0:T(8,128)(2,1)S(1)}, bf16[2,64,512]{2,1,0:T(8,128)(2,1)S(1)}, u32[]{:S(2)}, u32[]{:S(2)}) collective-permute-start(bf16[2,64,512]{2,1,0:T(8,128)(2,1)S(1)} %collective-permute-done.2.refs_1_), channel_id=1, source_target_pairs={{0,1},{1,0},{2,3},{3,2},{4,5},{5,4},{6,7},{7,6},{8,9},{9,8},{10,11... | collective-permute-start | bytes 393224 | tf_op jit(solution)/shard_map/ppermute | solution.py:339

commit v5 on v4

--- a/solution.py
+++ b/solution.py
@@ -109,34 +109,40 @@
             out_ref[peer] = jnp.concatenate([rows[:, :half], rows[:, half:]], axis=0)
 
 
+def unpack(rows, own):
+    packs = rows.shape[0] // (2 * own)
+    token = lax.broadcasted_iota(jnp.int32, (packs * own, rows.shape[0]), 0)
+    source = lax.broadcasted_iota(jnp.int32, (packs * own, rows.shape[0]), 1)
+    first = (token // own) * (2 * own) + token % own
+    low = dot32(jnp.where(source == first, 1.0, 0.0).astype(BF16), rows)
+    high = dot32(jnp.where(source == first + own, 1.0, 0.0).astype(BF16), rows)
+    return low, high
+
+
 def attend_kernel(index_ref, rows_ref, w_qkv_ref, w_out_ref, out_ref):
     frames, packed, half = rows_ref.shape
     own = packed // 2
     width = 2 * half
     seq = frames * TOKL
     videos = frames * own // seq
-    raw = rows_ref[...].astype(F32)
-
-    def feature_mean(values):
-        part = jnp.sum(values, axis=-1, keepdims=True)
-        return (part + swap_halves(part)) / width
-
-    centred = raw - feature_mean(raw)
-    variance = feature_mean(centred * centred)
-    normed = (centred * lax.rsqrt(variance + NORM_EPS)).astype(BF16).reshape(-1, half)
+    low, high = unpack(rows_ref[...].reshape(frames * packed, half), own)
+    raw = jnp.concatenate([low, high], axis=1)
+    centred = raw - jnp.mean(raw, axis=1, keepdims=True)
+    variance = jnp.mean(centred * centred, axis=1, keepdims=True)
+    normed = (centred * lax.rsqrt(variance + NORM_EPS)).astype(BF16)
+
+    pairs = frames * own // packed
 
     def project(start):
-        low = dot32(normed, w_qkv_ref[:half, start : start + width])
-        high = dot32(normed, w_qkv_ref[half:, start : start + width])
-        low = low.reshape(frames, packed, width)
-        high = high.reshape(frames, packed, width)
-        return (low + swap_halves(high)).astype(BF16).astype(F32)
+        part = dot32(normed, w_qkv_ref[:, start : start + width])
+        return part.astype(BF16).astype(F32).reshape(pairs, packed, width)
 
     table = index_ref[...]
-    row = lax.broadcasted_iota(jnp.int32, (1, packed, 1), 1)
+    row = lax.broadcasted_iota(jnp.int32, (1, packed, LANES), 1)
+    upper = row >= own
     me = table[:1, :1, KMAX + 1 : KMAX + 2].astype(jnp.int32)
-    flat = me * own + jnp.where(row >= own, row - own, row)
-    owner = jnp.zeros((frames, packed, 1), jnp.bool_)
+    flat = me * own + jnp.where(upper, row - own, row)
+    owner = jnp.zeros((pairs, packed, LANES), F32)
     for v in range(videos):
         count = table[:, v : v + 1, KMAX : KMAX + 1]
         upto = count
@@ -146,14 +152,21 @@
             upto = upto + moved
             step *= 2
         place = (flat - v * seq).astype(F32)
-        inside = jnp.logical_and(place >= upto - count, place < upto)
         ours = jnp.logical_and(flat >= v * seq, flat < (v + 1) * seq)
-        owner = jnp.logical_or(owner, jnp.logical_and(inside, ours))
-
-    def of_owner(values):
-        return jnp.sum(jnp.where(owner, values, 0.0), axis=0)
-
-    query = of_owner(project(0))
+        below = upto - count
+        below = below.reshape(pairs, 2, 1, 1)
+        upto = upto.reshape(pairs, 2, 1, 1)
+        start = jnp.where(upper, below[:, 1], below[:, 0])
+        stop = jnp.where(upper, upto[:, 1], upto[:, 0])
+        inside = jnp.logical_and(place >= start, place < stop)
+        owner = owner + jnp.where(jnp.logical_and(inside, ours), 1.0, 0.0)
+    owner = owner[:, :, :1]
+
+    def over_frames(values):
+        total = jnp.sum(values, axis=0)
+        return total + swap_halves(total)
+
+    query = over_frames(project(0) * owner)
     product = (project(width) * query[None]).reshape(-1, width)
     feature = lax.broadcasted_iota(jnp.int32, (width, LANES), 0) // HEAD_DIM
     head = lax.broadcasted_iota(jnp.int32, (width, LANES), 1)
@@ -163,31 +176,29 @@
     fine = rest.astype(BF16)
     last = (rest - fine.astype(F32)).astype(BF16)
     scores = dot32(coarse, to_head) + dot32(fine, to_head) + dot32(last, to_head)
-    scores = scores.reshape(frames, packed, LANES) * SCORE_SCALE
-    raised = jnp.exp(scores - jnp.max(scores, axis=0, keepdims=True))
-    weights = (raised / jnp.sum(raised, axis=0, keepdims=True)).astype(BF16)
+    scores = scores.reshape(pairs, packed, LANES) * SCORE_SCALE
+    largest = jnp.max(scores, axis=0)
+    largest = jnp.maximum(largest, swap_halves(largest))
+    raised = jnp.exp(scores - largest[None])
+    weights = (raised / over_frames(raised)[None]).astype(BF16)
     head = lax.broadcasted_iota(jnp.int32, (LANES, width), 0)
     feature = lax.broadcasted_iota(jnp.int32, (LANES, width), 1) // HEAD_DIM
     from_head = jnp.where(feature == head, 1.0, 0.0).astype(BF16)
-    spread = dot32(weights.reshape(-1, LANES), from_head).reshape(frames, packed, width)
-    attended = jnp.sum(spread * project(2 * width), axis=0).astype(BF16)
+    spread = dot32(weights.reshape(-1, LANES), from_head).reshape(pairs, packed, width)
+    attended = over_frames(spread * project(2 * width)).astype(BF16)
     change = dot32(attended, w_out_ref[...])
+    residual = over_frames(raw.reshape(pairs, packed, width) * owner)
+    encoded = residual + change
     place = lax.broadcasted_iota(jnp.int32, (packed, half), 0)
-    change = jnp.where(place < own, change[:, :half], swap_halves(change[:, half:]))
-    encoded = (of_owner(raw) + change).astype(BF16)
+    encoded = jnp.where(place < own, encoded[:, :half], encoded[:, half:]).astype(BF16)
     out_ref[...] = jnp.broadcast_to(encoded[None], out_ref.shape)
 
 
 def project_kernel(rows_ref, w_proj_ref, gain_ref, out_ref):
     frames, packed, half = rows_ref.shape
     own = packed // 2
-    tokens = frames * own
     rows = rows_ref[...].reshape(frames * packed, half)
-    token = lax.broadcasted_iota(jnp.int32, (tokens, frames * packed), 0)
-    source = lax.broadcasted_iota(jnp.int32, (tokens, frames * packed), 1)
-    first = (token // own) * packed + token % own
-    low = dot32(jnp.where(source == first, 1.0, 0.0).astype(BF16), rows).astype(BF16)
-    high = dot32(jnp.where(source == first + own, 1.0, 0.0).astype(BF16), rows).astype(BF16)
+    low, high = (part.astype(BF16) for part in unpack(rows, own))
     total = dot32(low, w_proj_ref[:half, :]) + dot32(high, w_proj_ref[half:, :])
     gain = gain_ref[...].astype(F32)
     lanes = gain.shape[1]
@@ -197,76 +208,85 @@
         out_ref[:, piece] = gained
 
 
-def products(place_of, videos, index_ref, rows_ref, w_gate_ref, w_up_ref, begun, emit):
-    parts, tokens, columns = rows_ref.shape
+def places(index_ref, sources):
+    me = jnp.max(index_ref[0, :1, KMAX + 1 : KMAX + 2]).astype(jnp.int32)
+    row = me // NEAR
+    found = []
+    for flip, steps, direct in sources:
+        near = jnp.bitwise_xor(me - row * NEAR, flip)
+        for i, step in enumerate(steps):
+            outer = jnp.bitwise_xor(row, step) if direct else step
+            found.append((i, outer * NEAR + near))
+    return found
+
+
+def square_sums(blocks, videos, index_ref):
+    tokens, columns = blocks[0][0].shape[1:]
     gain_rows = -(-columns // LANES)
-    places = [place_of(part) for part in range(parts)]
-    squares = jnp.zeros((tokens, LANES), F32) if begun is None else begun[2][...]
-    for part, place in enumerate(places):
+    squares = jnp.zeros((tokens, LANES), F32)
+    for rows_ref, i, place in blocks:
         inverse = 1.0 / index_ref[place, videos : videos + gain_rows, :]
         for r in range(gain_rows):
-            piece = rows_ref[part, :, r * LANES : min((r + 1) * LANES, columns)].astype(F32)
+            piece = rows_ref[i, :, r * LANES : min((r + 1) * LANES, columns)].astype(F32)
             piece = piece * inverse[r : r + 1, : piece.shape[1]]
             piece = piece * piece
             if piece.shape[1] < LANES:
                 fill = jnp.zeros((tokens, LANES - piece.shape[1]), F32)
                 piece = jnp.concatenate([piece, fill], axis=1)
             squares = squares + piece
+    return squares
+
+
+def products(blocks, w_gate_ref, w_up_ref, begun, emit):
+    columns = blocks[0][0].shape[2]
     width = w_gate_ref.shape[1]
     block = min(width, 256)
     for first in range(0, width, block):
         sums = []
         for i, w_ref in enumerate((w_gate_ref, w_up_ref)):
-            total = None if begun is None else begun[i][:, first : first + block]
-            for part, place in enumerate(places):
+            total = begun[i][:, first : first + block] if begun else None
+            for rows_ref, part, place in blocks:
                 depth = pl.ds(pl.multiple_of(place * columns, columns), columns)
                 one = dot32(rows_ref[part], w_ref[depth, first : first + block])
                 total = one if total is None else total + one
             sums.append(total)
         emit(first, block, *sums)
-    return squares
-
-
-def place_rule(index_ref, source):
-    flip, steps, direct = source
-    me = jnp.max(index_ref[0, :1, KMAX + 1 : KMAX + 2]).astype(jnp.int32)
-    row = me // NEAR
-    near = jnp.bitwise_xor(me - row * NEAR, flip)
-    if direct:
-        return lambda i: jnp.bitwise_xor(row, steps[i]) * NEAR + near
-    return lambda i: steps[i] * NEAR + near
-
-
-def partial_kernel(source, videos, *refs):
-    index_ref, rows_ref, w_gate_ref, w_up_ref = refs[:4]
-    gate_ref, up_ref, squares_ref = refs[-3:]
-    begun = refs[4:7] if len(refs) > 7 else None
+
+
+def split_refs(sources, refs):
+    index_ref, w_gate_ref, w_up_ref = refs[:3]
+    rows = refs[3 : 3 + len(sources)]
+    owners = [ref for ref, source in zip(rows, sources) for _ in source[1]]
+    blocks = [(ref,) + found for ref, found in zip(owners, places(index_ref, sources))]
+    return index_ref, w_gate_ref, w_up_ref, blocks, refs[3 + len(sources) :]
+
+
+def partial_kernel(sources, videos, *refs):
+    index_ref, w_gate_ref, w_up_ref, blocks, rest = split_refs(sources, refs)
+    begun, (gate_ref, up_ref, squares_ref) = rest[:-3], rest[-3:]
 
     def emit(first, block, gate, up):
         gate_ref[:, first : first + block] = gate
         up_ref[:, first : first + block] = up
 
-    rule = place_rule(index_ref, source)
-    squares_ref[...] = products(
-        rule, videos, index_ref, rows_ref, w_gate_ref, w_up_ref, begun, emit
-    )
-
-
-def final_kernel(source, index_ref, rows_ref, w_gate_ref, w_up_ref, gate_ref, up_ref, squares_ref,
-                 out_ref, gate_sum, up_sum):
-    def emit(first, block, gate, up):
-        gate_sum[:, first : first + block] = gate
-        up_sum[:, first : first + block] = up
-
-    rule = place_rule(index_ref, source)
-    begun = (gate_ref, up_ref, squares_ref)
-    squares = products(
-        rule, out_ref.shape[0], index_ref, rows_ref, w_gate_ref, w_up_ref, begun, emit
-    )
+    squares = square_sums(blocks, videos, index_ref)
+    squares_ref[...] = squares + begun[2][...] if begun else squares
+    products(blocks, w_gate_ref, w_up_ref, begun, emit)
+
+
+def final_kernel(sources, *refs):
+    index_ref, w_gate_ref, w_up_ref, blocks, rest = split_refs(sources, refs)
+    begun, out_ref = rest[:3], rest[3]
+    videos = out_ref.shape[0]
+    squares = begun[2][...] + square_sums(blocks, videos, index_ref)
     mean = jnp.sum(squares, axis=1, keepdims=True) / w_gate_ref.shape[0]
     scale = lax.rsqrt(mean + NORM_EPS)
-    hidden = jax.nn.silu(gate_sum[...] * scale) * (up_sum[...] * scale)
-    out_ref[...] = hidden.astype(BF16).reshape(out_ref.shape)
+
+    def emit(first, block, gate, up):
+        hidden = (jax.nn.silu(gate * scale) * (up * scale)).astype(BF16)
+        out_ref[:, :, first : first + block] = hidden.reshape(videos, -1, block)
+
+    products(blocks, w_gate_ref, w_up_ref, begun, emit)
 
 
 def program(video, w_qkv, w_out, keep_list, kept_counts, w_proj, llm_gain, w_gate, w_up):
@@ -347,47 +367,48 @@
         transcendentals=0,
     )
 
-    def add(source, block, begun):
-        return pl.pallas_call(
-            functools.partial(partial_kernel, source, videos),
-            out_shape=sums,
-            in_specs=[whole()] * (4 + len(begun)),
-            out_specs=(whole(), whole(), whole()),
+    direct = outer == DIRECT
+    if direct:
+        far = [swap(gained, "outer", k) for k in range(1, outer)]
+        own = gained[None]
+        near, rest = jnp.stack([gained, far[0]]), jnp.stack(far[1:])
+        mid0, mid1 = swap(near, "mid"), swap(rest, "mid")
+        core = swap(own, "cores")
+        core0, core1 = swap(far[0][None], "cores"), swap(rest, "cores")
+        both0, both1 = swap(mid0, "cores"), swap(mid1, "cores")
+        stages = (
+            ((own, 0, (0,)),),
+            ((core, 1, (0,)), (far[0][None], 0, (1,))),
+            ((core0, 1, (1,)), (rest, 0, (2, 3))),
+            ((core1, 1, (2, 3)),),
+            ((mid0, 2, (0, 1)),),
+            ((both0, 3, (0, 1)),),
+            ((mid1, 2, (2, 3)),),
+            ((both1, 3, (2, 3)),),
+        )
+    else:
+        line = spread(jnp.broadcast_to(gained[None], (outer,) + gained.shape), "outer")
+        steps = tuple(range(outer))
+        mid = swap(line, "mid")
+        core, both = swap(line, "cores"), swap(mid, "cores")
+        blocks = ((line, 0), (core, 1), (mid, 2), (both, 3))
+        stages = tuple(((block, flip, steps),) for block, flip in blocks)
+    begun = ()
+    for i, stage in enumerate(stages):
+        sources = tuple((flip, steps, direct) for _, flip, steps in stage)
+        last = i + 1 == len(stages)
+        begun = pl.pallas_call(
+            functools.partial(final_kernel, sources)
+            if last
+            else functools.partial(partial_kernel, sources, videos),
+            out_shape=jax.ShapeDtypeStruct((videos, seq, units), BF16) if last else sums,
+            in_specs=[whole()] * (3 + len(stage) + len(begun)),
+            out_specs=whole() if last else (whole(),) * 3,
             compiler_params=params(3 * MIB + 20 * tokens * units),
             cost_estimate=work,
-            name="part",
-        )(index, block, w_gate, w_up, *begun)
-
-    direct = outer <= DIRECT
-    if direct:
-        blocks = [gained] + [swap(gained, "outer", k) for k in range(1, outer)]
-        groups = [tuple(range(outer))[i : i + 2] for i in range(0, outer, 2)]
-        lines = [jnp.stack([blocks[i] for i in steps]) for steps in groups]
-    else:
-        groups = [tuple(range(outer))]
-        lines = [spread(jnp.broadcast_to(gained[None], (outer,) + gained.shape), "outer")]
-    begun = ()
-    mids = []
-    for steps, line in zip(groups, lines):
-        mids.append(swap(line, "mid"))
-        line_core = swap(line, "cores")
-        begun = add((0, steps, direct), line, begun)
-        begun = add((1, steps, direct), line_core, begun)
-    for i, steps in enumerate(groups):
-        line_core = swap(mids[i], "cores")
-        begun = add((2, steps, direct), mids[i], begun)
-        if i + 1 < len(groups):
-            begun = add((3, steps, direct), line_core, begun)
-    return pl.pallas_call(
-        functools.partial(final_kernel, (3, groups[-1], direct)),
-        out_shape=jax.ShapeDtypeStruct((videos, seq, units), BF16),
-        in_specs=[whole()] * 7,
-        out_specs=whole(),
-        scratch_shapes=[pltpu.VMEM((tokens, units), F32)] * 2,
-        compiler_params=params(3 * MIB + 24 * tokens * units),
-        cost_estimate=work,
-        name="final",
-    )(index, line_core, w_gate, w_up, *begun)
+            name="final" if last else "part",
+        )(index, w_gate, w_up, *(block for block, _, _ in stage), *begun)
+    return begun
 
 
 def solution(mesh):

time: 61.8 us -> 62.3 us (level)
    ppermute x9 -> x10, waiting for transfers between devices: 6.34 us -> 6.73 us  [swap(): return lax.ppermute(values, axis, pairs)]
    ppermute x9 -> x10, starting transfers between devices: 5.82 us -> 5.83 us  [swap(): return lax.ppermute(values, axis, pairs)]
  transfers between devices with their start and end apart: 9 -> 10, of which waited for: 4 -> 4; matrix products, arithmetic and copies ran while one was open for 0% -> 0% of each run, Pallas kernels for 12% -> 11%
where the time goes in v5:
time: 62.3 us; the launch traced here: 62 us
  blocking collectives  35.4 us (57%)
  Pallas kernels  13.7 us (22%)
  waiting for transfers between devices  6.73 us (11%)
  starting transfers between devices  5.83 us (9%)
    all_to_all x1, blocking collectives, program(): index = spread(message, axes)  14.4 us
    all_to_all x1, blocking collectives, program(): seen = spread(chosen, axes)  10.5 us
    all_to_all x1, blocking collectives, program(): token_rows = spread(encoded, axes)  10.5 us
    pallas_call x8, Pallas kernels, program(): pl.pallas_call(functools.partial(final_kernel, sources) if last else func...  8.81 us
    ppermute x10, waiting for transfers between devices, swap(): return lax.ppermute(values, axis, pairs)  6.73 us
    ppermute x10, starting transfers between devices, swap(): return lax.ppermute(values, axis, pairs)  5.83 us
    pallas_call x1, Pallas kernels, program(): pl.pallas_call(attend_kernel, out_shape=jax.ShapeDtypeStruct((frames, pac...  2.5 us
  transfers between devices with their start and end apart: 10, of which 4 were waited for; matrix products, arithmetic and copies ran while one was open for 0% of the time, Pallas kernels for 11%

profile of v5, /device:TPU:0, one launch (start us, length us, event | category | flops | bytes accessed | tf_op | source)
XLA Modules:
  0.0 62.0 jit_solution(14501626413067490460)
XLA Ops:
  0.0 1.0 %collect.1.message_ref = f32[8,128]{1,0:T(8,128)S(1)} custom-call(s32[1,2]{1,0:T(1,128)} %bitcast.20, s32[2,1,128]{2,1,0:T(1,128)} %keep_hbm.1, bf16[4,128]{1,0:T(4,128)(2,1)} %bitcast.16), custom_call_target="tpu_custom_call" | custom-call | tf_op jit(solution)/shard_map/collect/pallas_call | solution.py:307
  1.1 14.4 %all_to_all.15.index_ref.refs_0_ = f32[16,8,128]{2,1,0:T(8,128)S(1)} all-to-all(f32[16,8,128]{2,1,0:T(8,128)S(1)} %index.1), channel_id=1, replica_groups=mesh['groups'=2,'outer'=4,'mid'=2,'cores'=2] {'outer','mid','cores'}, dimensions={0} | all-to-all | bytes 131072 | tf_op jit(solution)/shard_map/all_to_all | solution.py:326
  15.5 1.0 %select.1 = bf16[16,8,512]{2,1,0:T(8,128)(2,1)S(1)} custom-call(f32[16,8,128]{2,1,0:T(8,128)S(1)} %all_to_all.15.index_ref.refs_0_, bf16[2,1,128,1024]{3,2,1,0:T(8,128)(2,1)S(1)} %copy-done.3), custom_call_target="tpu_custom_call" | custom-call | tf_op jit(solution)/shard_map/select/pallas_call | solution.py:328
  16.5 10.5 %all_to_all.16.rows_ref = bf16[16,8,512]{2,1,0:T(8,128)(2,1)S(1)} all-to-all(bf16[16,8,512]{2,1,0:T(8,128)(2,1)S(1)} %select.1), channel_id=1, replica_groups=mesh['groups'=2,'outer'=4,'mid'=2,'cores'=2] {'outer','mid','cores'}, dimensions={0} | all-to-all | bytes 262144 | tf_op jit(solution)/shard_map/all_to_all | solution.py:336
  27.0 2.5 %attend.1 = bf16[16,8,512]{2,1,0:T(8,128)(2,1)S(1)} custom-call(f32[16,8,128]{2,1,0:T(8,128)S(1)} %all_to_all.15.index_ref.refs_0_, bf16[16,8,512]{2,1,0:T(8,128)(2,1)S(1)} %all_to_all.16.rows_ref, bf16[1024,3072]{1,0:T(8,128)(2,1)S(1)} %copy-done, bf16[1024,1024]{1,0:T(8,128)(2,1)S(1)} %copy-done.1), custom_call_target="tpu_custom_call" | custom-call | tf_op jit(solution)/shard_map/attend/pallas_call | solution.py:338
  29.5 10.5 %all_to_all.17.rows_ref = bf16[16,8,512]{2,1,0:T(8,128)(2,1)S(1)} all-to-all(bf16[16,8,512]{2,1,0:T(8,128)(2,1)S(1)} %attend.1), channel_id=1, replica_groups=mesh['groups'=2,'outer'=4,'mid'=2,'cores'=2] {'outer','mid','cores'}, dimensions={0} | all-to-all | bytes 262144 | tf_op jit(solution)/shard_map/all_to_all | solution.py:346
  40.0 0.4 project.1
  40.4 0.1 collective-permute-start.4
  40.5 1.2 %collective-permute-start = (bf16[64,512]{1,0:T(8,128)(2,1)S(1)}, bf16[64,512]{1,0:T(8,128)(2,1)S(1)}, u32[]{:S(2)}, u32[]{:S(2)}) collective-permute-start(bf16[64,512]{1,0:T(8,128)(2,1)S(1)} %project.1), channel_id=1, source_target_pairs={{0,8},{4,12},{8,0},{12,4},{1,9},{5,13},{9,1},{13,5},{2,10},{6,14},... | collective-permute-start | bytes 196616 | tf_op jit(solution)/shard_map/ppermute | solution.py:359
  41.7 3.2 %collective-permute-start.1 = (bf16[64,512]{1,0:T(8,128)(2,1)S(1)}, bf16[64,512]{1,0:T(8,128)(2,1)S(1)}, u32[]{:S(2)}, u32[]{:S(2)}) collective-permute-start(bf16[64,512]{1,0:T(8,128)(2,1)S(1)} %project.1), channel_id=1, source_target_pairs={{0,12},{4,8},{8,4},{12,0},{1,13},{5,9},{9,5},{13,1},{2,14},{6,10},... | collective-permute-start | bytes 196616 | tf_op jit(solution)/shard_map/ppermute | solution.py:359
  44.9 0.3 collective-permute-done.4
  45.2 3.4 %collective-permute-done = bf16[64,512]{1,0:T(8,128)(2,1)S(1)} collective-permute-done((bf16[64,512]{1,0:T(8,128)(2,1)S(1)}, bf16[64,512]{1,0:T(8,128)(2,1)S(1)}, u32[]{:S(2)}, u32[]{:S(2)}) %collective-permute-start) | collective-permute-done | bytes 65568 | tf_op jit(solution)/shard_map/ppermute | solution.py:359
  48.7 0.8 %collective-permute-start.2 = (bf16[2,64,512]{2,1,0:T(8,128)(2,1)S(1)}, bf16[2,64,512]{2,1,0:T(8,128)(2,1)S(1)}, u32[]{:S(2)}, u32[]{:S(2)}) collective-permute-start(bf16[2,64,512]{2,1,0:T(8,128)(2,1)S(1)} %pad_maximum_fusion.refs_4_), channel_id=1, source_target_pairs={{0,2},{2,0},{1,3},{3,1},{4,6},{6,4},{5,7},{7,5},{8,10},{10,8},{9,1... | collective-permute-start | bytes 393224 | tf_op jit(solution)/shard_map/ppermute | solution.py:359
  49.5 0.5 collective-permute-start.9
  50.0 1.4 %collective-permute-done.5.refs_3_ = bf16[2,64,512]{2,1,0:T(8,128)(2,1)S(1)} collective-permute-done((bf16[2,64,512]{2,1,0:T(8,128)(2,1)S(1)}, bf16[2,64,512]{2,1,0:T(8,128)(2,1)S(1)}, u32[]{:S(2)}, u32[]{:S(2)}) %collective-permute-start.5) | collective-permute-done | bytes 131104 | tf_op jit(solution)/shard_map/ppermute | solution.py:359
  51.5 0.6 part.7
  52.1 1.6 %collective-permute-done.2.refs_3_ = bf16[2,64,512]{2,1,0:T(8,128)(2,1)S(1)} collective-permute-done((bf16[2,64,512]{2,1,0:T(8,128)(2,1)S(1)}, bf16[2,64,512]{2,1,0:T(8,128)(2,1)S(1)}, u32[]{:S(2)}, u32[]{:S(2)}) %collective-permute-start.2) | collective-permute-done | bytes 131104 | tf_op jit(solution)/shard_map/ppermute | solution.py:359
  53.7 1.0 %part.8 = (f32[64,1024]{1,0:T(8,128)S(1)}, f32[64,1024]{1,0:T(8,128)S(1)}, f32[64,128]{1,0:T(8,128)S(1)}) custom-call(f32[16,8,128]{2,1,0:T(8,128)S(1)} %all_to_all.15.index_ref.refs_0_, bf16[8192,1024]{1,0:T(8,128)(2,1)S(1)} %bitcast.7, bf16[8192,1024]{1,0:T(8,128)(2,1)S(1)} %bitcast.9, bf16[1,64,512]{2,1,0:T(8,128)(2,1)S(1)} %collective-permute-done.9.refs_3_, ...), custom_call_target="tpu_custom_call" | custom-call | flops 268435456 | bytes 4194304 | tf_op jit(solution)/shard_map/part/pallas_call | solution.py:400
  54.7 1.4 %part.9 = (f32[64,1024]{1,0:T(8,128)S(1)}, f32[64,1024]{1,0:T(8,128)S(1)}, f32[64,128]{1,0:T(8,128)S(1)}) custom-call(f32[16,8,128]{2,1,0:T(8,128)S(1)} %all_to_all.15.index_ref.refs_0_, bf16[8192,1024]{1,0:T(8,128)(2,1)S(1)} %bitcast.7, bf16[8192,1024]{1,0:T(8,128)(2,1)S(1)} %bitcast.9, bf16[1,64,512]{2,1,0:T(8,128)(2,1)S(1)} %collective-permute-done.8.refs_3_, ...), custom_call_target="tpu_custom_call" | custom-call | flops 268435456 | bytes 4194304 | tf_op jit(solution)/shard_map/part/pallas_call | solution.py:400
  56.2 1.0 %part.10 = (f32[64,1024]{1,0:T(8,128)S(1)}, f32[64,1024]{1,0:T(8,128)S(1)}, f32[64,128]{1,0:T(8,128)S(1)}) custom-call(f32[16,8,128]{2,1,0:T(8,128)S(1)} %all_to_all.15.index_ref.refs_0_, bf16[8192,1024]{1,0:T(8,128)(2,1)S(1)} %bitcast.7, bf16[8192,1024]{1,0:T(8,128)(2,1)S(1)} %bitcast.9, bf16[2,64,512]{2,1,0:T(8,128)(2,1)S(1)} %collective-permute-done.7.refs_3_, ...), custom_call_target="tpu_custom_call" | custom-call | flops 268435456 | bytes 4194304 | tf_op jit(solution)/shard_map/part/pallas_call | solution.py:400
  57.2 1.0 %part.11 = (f32[64,1024]{1,0:T(8,128)S(1)}, f32[64,1024]{1,0:T(8,128)S(1)}, f32[64,128]{1,0:T(8,128)S(1)}) custom-call(f32[16,8,128]{2,1,0:T(8,128)S(1)} %all_to_all.15.index_ref.refs_0_, bf16[8192,1024]{1,0:T(8,128)(2,1)S(1)} %bitcast.7, bf16[8192,1024]{1,0:T(8,128)(2,1)S(1)} %bitcast.9, bf16[2,64,512]{2,1,0:T(8,128)(2,1)S(1)} %collective-permute-done.5.refs_3_, ...), custom_call_target="tpu_custom_call" | custom-call | flops 268435456 | bytes 4194304 | tf_op jit(solution)/shard_map/part/pallas_call | solution.py:400
  58.3 1.0 %part.12 = (f32[64,1024]{1,0:T(8,128)S(1)}, f32[64,1024]{1,0:T(8,128)S(1)}, f32[64,128]{1,0:T(8,128)S(1)}) custom-call(f32[16,8,128]{2,1,0:T(8,128)S(1)} %all_to_all.15.index_ref.refs_0_, bf16[8192,1024]{1,0:T(8,128)(2,1)S(1)} %bitcast.7, bf16[8192,1024]{1,0:T(8,128)(2,1)S(1)} %bitcast.9, bf16[2,64,512]{2,1,0:T(8,128)(2,1)S(1)} %collective-permute-done.6.refs_3_, ...), custom_call_target="tpu_custom_call" | custom-call | flops 268435456 | bytes 4194304 | tf_op jit(solution)/shard_map/part/pallas_call | solution.py:400
  59.3 1.0 %part.13 = (f32[64,1024]{1,0:T(8,128)S(1)}, f32[64,1024]{1,0:T(8,128)S(1)}, f32[64,128]{1,0:T(8,128)S(1)}) custom-call(f32[16,8,128]{2,1,0:T(8,128)S(1)} %all_to_all.15.index_ref.refs_0_, bf16[8192,1024]{1,0:T(8,128)(2,1)S(1)} %bitcast.7, bf16[8192,1024]{1,0:T(8,128)(2,1)S(1)} %bitcast.9, bf16[2,64,512]{2,1,0:T(8,128)(2,1)S(1)} %collective-permute-done.2.refs_3_, ...), custom_call_target="tpu_custom_call" | custom-call | flops 268435456 | bytes 4194304 | tf_op jit(solution)/shard_map/part/pallas_call | solution.py:400
  60.3 1.7 %final.1 = bf16[2,32,1024]{2,1,0:T(8,128)(2,1)} custom-call(f32[16,8,128]{2,1,0:T(8,128)S(1)} %all_to_all.15.index_ref.refs_0_, bf16[8192,1024]{1,0:T(8,128)(2,1)S(1)} %bitcast.7, bf16[8192,1024]{1,0:T(8,128)(2,1)S(1)} %bitcast.9, bf16[2,64,512]{2,1,0:T(8,128)(2,1)S(1)} %collective-permute-done.3.refs_3_, f32[64,1024]{1,0:T(8,128)S(1)} %get-tuple-element.44.refs_4_, ...), custom_call_target="tpu_custom_call" | custom-call | flops 268435456 | bytes 4194304 | tf_op jit(solution)/shard_map/final/pallas_call | solution.py:400
  (42 shorter events, 0.2 us)
Async XLA Ops:
  0.0 51.4 %slice-start = ((s8[16777216]{0:T(1024)(128)(4,1)}), s8[4194304]{0:T(1024)(128)(4,1)S(1)}, s32[]{:S(2)}) async-start(s8[16777216]{0:T(1024)(128)(4,1)} %bitcast.6), calls=%async_computation.3 | async-start | bytes 8388608
  0.0 51.4 %slice-start.4 = ((s8[16777216]{0:T(1024)(128)(4,1)}), s8[4194304]{0:T(1024)(128)(4,1)S(1)}, s32[]{:S(2)}) async-start(s8[16777216]{0:T(1024)(128)(4,1)} %bitcast.8), calls=%async_computation.7 | async-start | bytes 8388608
  1.0 14.5 %copy-start.3 = (bf16[2,1,128,1024]{3,2,1,0:T(8,128)(2,1)S(1)}, bf16[2,1,128,1024]{3,2,1,0:T(8,128)(2,1)}, u32[]{:S(2)}) copy-start(bf16[2,1,128,1024]{3,2,1,0:T(8,128)(2,1)} %video_ref.1) | copy-start | bytes 1572868
  1.0 26.0 %copy-start = (bf16[1024,3072]{1,0:T(8,128)(2,1)S(1)}, bf16[1024,3072]{1,0:T(8,128)(2,1)}, u32[]{:S(2)}) copy-start(bf16[1024,3072]{1,0:T(8,128)(2,1)} %w_qkv_ref.1) | copy-start | bytes 18874372
  1.0 26.0 %copy-start.1 = (bf16[1024,1024]{1,0:T(8,128)(2,1)S(1)}, bf16[1024,1024]{1,0:T(8,128)(2,1)}, u32[]{:S(2)}) copy-start(bf16[1024,1024]{1,0:T(8,128)(2,1)} %w_out_ref.1) | copy-start | bytes 6291460
  1.0 39.0 %copy-start.2 = (bf16[1024,512]{1,0:T(8,128)(2,1)S(1)}, bf16[1024,512]{1,0:T(8,128)(2,1)}, u32[]{:S(2)}) copy-start(bf16[1024,512]{1,0:T(8,128)(2,1)} %w_proj_ref.1) | copy-start | bytes 3145732
  1.0 39.0 %copy-start.4 = (bf16[512]{0:T(512)(128)(2,1)S(1)}, bf16[512]{0:T(512)(128)(2,1)}, u32[]{:S(2)}) copy-start(bf16[512]{0:T(512)(128)(2,1)} %param.15) | copy-start | bytes 3076
  1.0 50.4 %slice-start.1 = ((s8[16777216]{0:T(1024)(128)(4,1)}), s8[4194304]{0:T(1024)(128)(4,1)S(1)}, s32[]{:S(2)}) async-start(s8[16777216]{0:T(1024)(128)(4,1)} %bitcast.6), calls=%async_computation.4 | async-start | bytes 8388608
  1.0 50.4 %slice-start.2 = ((s8[16777216]{0:T(1024)(128)(4,1)}), s8[4194304]{0:T(1024)(128)(4,1)S(1)}, s32[]{:S(2)}) async-start(s8[16777216]{0:T(1024)(128)(4,1)} %bitcast.6), calls=%async_computation.5 | async-start | bytes 8388608
  1.1 50.4 %slice-start.3 = ((s8[16777216]{0:T(1024)(128)(4,1)}), s8[4194304]{0:T(1024)(128)(4,1)S(1)}, s32[]{:S(2)}) async-start(s8[16777216]{0:T(1024)(128)(4,1)} %bitcast.6), calls=%async_computation.6 | async-start | bytes 8388608
  1.1 50.4 %slice-start.5 = ((s8[16777216]{0:T(1024)(128)(4,1)}), s8[4194304]{0:T(1024)(128)(4,1)S(1)}, s32[]{:S(2)}) async-start(s8[16777216]{0:T(1024)(128)(4,1)} %bitcast.8), calls=%async_computation.8 | async-start | bytes 8388608
  1.1 50.4 %slice-start.6 = ((s8[16777216]{0:T(1024)(128)(4,1)}), s8[4194304]{0:T(1024)(128)(4,1)S(1)}, s32[]{:S(2)}) async-start(s8[16777216]{0:T(1024)(128)(4,1)} %bitcast.8), calls=%async_computation.9 | async-start | bytes 8388608
  1.1 50.4 %slice-start.7 = ((s8[16777216]{0:T(1024)(128)(4,1)}), s8[4194304]{0:T(1024)(128)(4,1)S(1)}, s32[]{:S(2)}) async-start(s8[16777216]{0:T(1024)(128)(4,1)} %bitcast.8), calls=%async_computation.10 | async-start | bytes 8388608
  40.4 4.7 %collective-permute-start.4 = (bf16[64,512]{1,0:T(8,128)(2,1)S(1)}, bf16[64,512]{1,0:T(8,128)(2,1)S(1)}, u32[]{:S(2)}, u32[]{:S(2)}) collective-permute-start(bf16[64,512]{1,0:T(8,128)(2,1)S(1)} %project.1), channel_id=1, source_target_pairs={{0,4},{4,0},{8,12},{12,8},{1,5},{5,1},{9,13},{13,9},{2,6},{6,2},{1... | collective-permute-start | bytes 196616 | tf_op jit(solution)/shard_map/ppermute | solution.py:359
  40.5 8.1 %collective-permute-start = (bf16[64,512]{1,0:T(8,128)(2,1)S(1)}, bf16[64,512]{1,0:T(8,128)(2,1)S(1)}, u32[]{:S(2)}, u32[]{:S(2)}) collective-permute-start(bf16[64,512]{1,0:T(8,128)(2,1)S(1)} %project.1), channel_id=1, source_target_pairs={{0,8},{4,12},{8,0},{12,4},{1,9},{5,13},{9,1},{13,5},{2,10},{6,14},... | collective-permute-start | bytes 196616 | tf_op jit(solution)/shard_map/ppermute | solution.py:359
  41.7 7.0 %collective-permute-start.1 = (bf16[64,512]{1,0:T(8,128)(2,1)S(1)}, bf16[64,512]{1,0:T(8,128)(2,1)S(1)}, u32[]{:S(2)}, u32[]{:S(2)}) collective-permute-start(bf16[64,512]{1,0:T(8,128)(2,1)S(1)} %project.1), channel_id=1, source_target_pairs={{0,12},{4,8},{8,4},{12,0},{1,13},{5,9},{9,5},{13,1},{2,14},{6,10},... | collective-permute-start | bytes 196616 | tf_op jit(solution)/shard_map/ppermute | solution.py:359
  45.2 6.3 %collective-permute-start.5 = (bf16[2,64,512]{2,1,0:T(8,128)(2,1)S(1)}, bf16[2,64,512]{2,1,0:T(8,128)(2,1)S(1)}, u32[]{:S(2)}, u32[]{:S(2)}) collective-permute-start(bf16[2,64,512]{2,1,0:T(8,128)(2,1)S(1)} %pad_maximum_fusion.1), channel_id=1, source_target_pairs={{0,2},{2,0},{1,3},{3,1},{4,6},{6,4},{5,7},{7,5},{8,10},{10,8},{9,1... | collective-permute-start | bytes 393224 | tf_op jit(solution)/shard_map/ppermute | solution.py:359
  48.7 5.0 %collective-permute-start.2 = (bf16[2,64,512]{2,1,0:T(8,128)(2,1)S(1)}, bf16[2,64,512]{2,1,0:T(8,128)(2,1)S(1)}, u32[]{:S(2)}, u32[]{:S(2)}) collective-permute-start(bf16[2,64,512]{2,1,0:T(8,128)(2,1)S(1)} %pad_maximum_fusion.refs_4_), channel_id=1, source_target_pairs={{0,2},{2,0},{1,3},{3,1},{4,6},{6,4},{5,7},{7,5},{8,10},{10,8},{9,1... | collective-permute-start | bytes 393224 | tf_op jit(solution)/shard_map/ppermute | solution.py:359
  49.5 6.7 %collective-permute-start.7 = (bf16[2,64,512]{2,1,0:T(8,128)(2,1)S(1)}, bf16[2,64,512]{2,1,0:T(8,128)(2,1)S(1)}, u32[]{:S(2)}, u32[]{:S(2)}) collective-permute-start(bf16[2,64,512]{2,1,0:T(8,128)(2,1)S(1)} %pad_maximum_fusion.refs_4_), channel_id=1, source_target_pairs={{0,1},{1,0},{2,3},{3,2},{4,5},{5,4},{6,7},{7,6},{8,9},{9,8},{10,11... | collective-permute-start | bytes 393224 | tf_op jit(solution)/shard_map/ppermute | solution.py:359
  49.5 4.2 %collective-permute-start.9 = (bf16[1,64,512]{2,1,0:T(8,128)(2,1)S(1)}, bf16[1,64,512]{2,1,0:T(8,128)(2,1)S(1)}, u32[]{:S(2)}, u32[]{:S(2)}) collective-permute-start(bf16[1,64,512]{2,1,0:T(8,128)(2,1)S(1)} %bitcast.11), channel_id=1, source_target_pairs={{0,1},{1,0},{2,3},{3,2},{4,5},{5,4},{6,7},{7,6},{8,9},{9,8},{10,11... | collective-permute-start | bytes 196616 | tf_op jit(solution)/shard_map/ppermute | solution.py:359
  50.0 4.8 %collective-permute-start.8 = (bf16[1,64,512]{2,1,0:T(8,128)(2,1)S(1)}, bf16[1,64,512]{2,1,0:T(8,128)(2,1)S(1)}, u32[]{:S(2)}, u32[]{:S(2)}) collective-permute-start(bf16[1,64,512]{2,1,0:T(8,128)(2,1)S(1)} %bitcast.14), channel_id=1, source_target_pairs={{0,1},{1,0},{2,3},{3,2},{4,5},{5,4},{6,7},{7,6},{8,9},{9,8},{10,11... | collective-permute-start | bytes 196616 | tf_op jit(solution)/shard_map/ppermute | solution.py:359
  51.4 6.8 %collective-permute-start.6 = (bf16[2,64,512]{2,1,0:T(8,128)(2,1)S(1)}, bf16[2,64,512]{2,1,0:T(8,128)(2,1)S(1)}, u32[]{:S(2)}, u32[]{:S(2)}) collective-permute-start(bf16[2,64,512]{2,1,0:T(8,128)(2,1)S(1)} %collective-permute-done.5.refs_3_), channel_id=1, source_target_pairs={{0,1},{1,0},{2,3},{3,2},{4,5},{5,4},{6,7},{7,6},{8,9},{9,8},{10,11... | collective-permute-start | bytes 393224 | tf_op jit(solution)/shard_map/ppermute | solution.py:359
  53.7 6.6 %collective-permute-start.3 = (bf16[2,64,512]{2,1,0:T(8,128)(2,1)S(1)}, bf16[2,64,512]{2,1,0:T(8,128)(2,1)S(1)}, u32[]{:S(2)}, u32[]{:S(2)}) collective-permute-start(bf16[2,64,512]{2,1,0:T(8,128)(2,1)S(1)} %collective-permute-done.2.refs_3_), channel_id=1, source_target_pairs={{0,1},{1,0},{2,3},{3,2},{4,5},{5,4},{6,7},{7,6},{8,9},{9,8},{10,11... | collective-permute-start | bytes 393224 | tf_op jit(solution)/shard_map/ppermute | solution.py:359

commit v6 on v5

--- a/solution.py
+++ b/solution.py
@@ -175,8 +175,8 @@
     rest = product - coarse.astype(F32)
     fine = rest.astype(BF16)
     last = (rest - fine.astype(F32)).astype(BF16)
-    scores = dot32(coarse, to_head) + dot32(fine, to_head) + dot32(last, to_head)
-    scores = scores.reshape(pairs, packed, LANES) * SCORE_SCALE
+    scores = dot32(jnp.concatenate([coarse, fine, last], axis=0), to_head)
+    scores = jnp.sum(scores.reshape(3, pairs, packed, LANES), axis=0) * SCORE_SCALE
     largest = jnp.max(scores, axis=0)
     largest = jnp.maximum(largest, swap_halves(largest))
     raised = jnp.exp(scores - largest[None])
@@ -369,21 +369,24 @@
 
     direct = outer == DIRECT
     if direct:
-        far = [swap(gained, "outer", k) for k in range(1, outer)]
-        own = gained[None]
-        near, rest = jnp.stack([gained, far[0]]), jnp.stack(far[1:])
-        mid0, mid1 = swap(near, "mid"), swap(rest, "mid")
-        core = swap(own, "cores")
-        core0, core1 = swap(far[0][None], "cores"), swap(rest, "cores")
-        both0, both1 = swap(mid0, "cores"), swap(mid1, "cores")
+        blocks = [gained, swap(gained, "outer", 1), swap(gained, "outer", 2)]
+        core = swap(gained, "cores")
+        mid0 = swap(jnp.stack(blocks[:2]), "mid")
+        core1 = swap(blocks[1], "cores")
+        blocks.append(swap(blocks[2], "outer", 1))
+        mid1 = swap(blocks[2], "mid")
+        mid2 = swap(blocks[3], "mid")
+        core2 = swap(jnp.stack(blocks[2:]), "cores")
+        both0 = swap(mid0, "cores")
+        both1 = swap(jnp.stack([mid1, mid2]), "cores")
+        one = [block[None] for block in blocks]
         stages = (
-            ((own, 0, (0,)),),
-            ((core, 1, (0,)), (far[0][None], 0, (1,))),
-            ((core0, 1, (1,)), (rest, 0, (2, 3))),
-            ((core1, 1, (2, 3)),),
-            ((mid0, 2, (0, 1)),),
-            ((both0, 3, (0, 1)),),
-            ((mid1, 2, (2, 3)),),
+            ((one[0], 0, (0,)),),
+            ((core[None], 1, (0,)), (one[1], 0, (1,))),
+            ((core1[None], 1, (1,)), (one[2], 0, (2,))),
+            ((one[3], 0, (3,)), (mid0, 2, (0, 1))),
+            ((core2, 1, (2, 3)), (both0, 3, (0, 1))),
+            ((mid1[None], 2, (2,)), (mid2[None], 2, (3,))),
             ((both1, 3, (2, 3)),),
         )
     else:

time: 62.3 us -> 63.5 us (1.019)
  waiting for transfers between devices: 6.73 us -> 9.26 us
  starting transfers between devices: 5.83 us -> 5.08 us
    ppermute x10 -> x11, waiting for transfers between devices: 6.73 us -> 9.26 us  [swap(): return lax.ppermute(values, axis, pairs)]
    ppermute x10 -> x11, starting transfers between devices: 5.83 us -> 5.08 us  [swap(): return lax.ppermute(values, axis, pairs)]
    pallas_call x8 -> x7, Pallas kernels: 8.81 us -> 8.31 us  [program(): pl.pallas_call(functools.partial(final_kernel, sources) if last else func...]
  transfers between devices with their start and end apart: 10 -> 11, of which waited for: 4 -> 4; matrix products, arithmetic and copies ran while one was open for 0% -> 0% of each run, Pallas kernels for 11% -> 10%
where the time goes in v6:
time: 63.5 us; the launch traced here: 63.3 us
  blocking collectives  35.4 us (56%)
  Pallas kernels  13.1 us (21%)
  waiting for transfers between devices  9.26 us (15%)
  starting transfers between devices  5.08 us (8%)
    all_to_all x1, blocking collectives, program(): index = spread(message, axes)  14.4 us
    all_to_all x1, blocking collectives, program(): seen = spread(chosen, axes)  10.5 us
    all_to_all x1, blocking collectives, program(): token_rows = spread(encoded, axes)  10.5 us
    ppermute x11, waiting for transfers between devices, swap(): return lax.ppermute(values, axis, pairs)  9.26 us
    pallas_call x7, Pallas kernels, program(): pl.pallas_call(functools.partial(final_kernel, sources) if last else func...  8.31 us
    ppermute x11, starting transfers between devices, swap(): return lax.ppermute(values, axis, pairs)  5.08 us
    pallas_call x1, Pallas kernels, program(): pl.pallas_call(attend_kernel, out_shape=jax.ShapeDtypeStruct((frames, pac...  2.46 us
  transfers between devices with their start and end apart: 11, of which 4 were waited for; matrix products, arithmetic and copies ran while one was open for 0% of the time, Pallas kernels for 10%

profile of v6, /device:TPU:0, one launch (start us, length us, event | category | flops | bytes accessed | tf_op | source)
XLA Modules:
  0.0 63.3 jit_solution(9821656829647731953)
XLA Ops:
  0.0 1.0 %collect.1.message_ref = f32[8,128]{1,0:T(8,128)S(1)} custom-call(s32[1,2]{1,0:T(1,128)} %bitcast.30, s32[2,1,128]{2,1,0:T(1,128)} %keep_hbm.1, bf16[4,128]{1,0:T(4,128)(2,1)} %bitcast.28), custom_call_target="tpu_custom_call" | custom-call | tf_op jit(solution)/shard_map/collect/pallas_call | solution.py:307
  1.1 14.4 %all_to_all.15.index_ref.refs_0_ = f32[16,8,128]{2,1,0:T(8,128)S(1)} all-to-all(f32[16,8,128]{2,1,0:T(8,128)S(1)} %index.1), channel_id=1, replica_groups=mesh['groups'=2,'outer'=4,'mid'=2,'cores'=2] {'outer','mid','cores'}, dimensions={0} | all-to-all | bytes 131072 | tf_op jit(solution)/shard_map/all_to_all | solution.py:326
  15.5 1.0 %select.1 = bf16[16,8,512]{2,1,0:T(8,128)(2,1)S(1)} custom-call(f32[16,8,128]{2,1,0:T(8,128)S(1)} %all_to_all.15.index_ref.refs_0_, bf16[2,1,128,1024]{3,2,1,0:T(8,128)(2,1)S(1)} %copy-done.3), custom_call_target="tpu_custom_call" | custom-call | tf_op jit(solution)/shard_map/select/pallas_call | solution.py:328
  16.5 10.5 %all_to_all.16.rows_ref = bf16[16,8,512]{2,1,0:T(8,128)(2,1)S(1)} all-to-all(bf16[16,8,512]{2,1,0:T(8,128)(2,1)S(1)} %select.1), channel_id=1, replica_groups=mesh['groups'=2,'outer'=4,'mid'=2,'cores'=2] {'outer','mid','cores'}, dimensions={0} | all-to-all | bytes 262144 | tf_op jit(solution)/shard_map/all_to_all | solution.py:336
  27.0 2.5 %attend.1 = bf16[16,8,512]{2,1,0:T(8,128)(2,1)S(1)} custom-call(f32[16,8,128]{2,1,0:T(8,128)S(1)} %all_to_all.15.index_ref.refs_0_, bf16[16,8,512]{2,1,0:T(8,128)(2,1)S(1)} %all_to_all.16.rows_ref, bf16[1024,3072]{1,0:T(8,128)(2,1)S(1)} %copy-done, bf16[1024,1024]{1,0:T(8,128)(2,1)S(1)} %copy-done.1), custom_call_target="tpu_custom_call" | custom-call | tf_op jit(solution)/shard_map/attend/pallas_call | solution.py:338
  29.5 10.5 %all_to_all.17.rows_ref = bf16[16,8,512]{2,1,0:T(8,128)(2,1)S(1)} all-to-all(bf16[16,8,512]{2,1,0:T(8,128)(2,1)S(1)} %attend.1), channel_id=1, replica_groups=mesh['groups'=2,'outer'=4,'mid'=2,'cores'=2] {'outer','mid','cores'}, dimensions={0} | all-to-all | bytes 262144 | tf_op jit(solution)/shard_map/all_to_all | solution.py:346
  40.0 0.4 project.1
  40.8 0.9 %collective-permute-start.6 = (bf16[64,512]{1,0:T(8,128)(2,1)S(1)}, bf16[64,512]{1,0:T(8,128)(2,1)S(1)}, u32[]{:S(2)}, u32[]{:S(2)}) collective-permute-start(bf16[64,512]{1,0:T(8,128)(2,1)S(1)} %project.1), channel_id=1, source_target_pairs={{0,4},{4,0},{8,12},{12,8},{1,5},{5,1},{9,13},{13,9},{2,6},{6,2},{1... | collective-permute-start | bytes 196616 | tf_op jit(solution)/shard_map/ppermute | solution.py:359
  41.7 4.5 %collective-permute-done = bf16[64,512]{1,0:T(8,128)(2,1)S(1)} collective-permute-done((bf16[64,512]{1,0:T(8,128)(2,1)S(1)}, bf16[64,512]{1,0:T(8,128)(2,1)S(1)}, u32[]{:S(2)}, u32[]{:S(2)}) %collective-permute-start) | collective-permute-done | bytes 65568 | tf_op jit(solution)/shard_map/ppermute | solution.py:359
  46.2 0.7 %collective-permute-start.7 = (bf16[2,64,512]{2,1,0:T(8,128)(2,1)S(1)}, bf16[2,64,512]{2,1,0:T(8,128)(2,1)S(1)}, u32[]{:S(2)}, u32[]{:S(2)}) collective-permute-start(bf16[2,64,512]{2,1,0:T(8,128)(2,1)S(1)} %pad_maximum_fusion.2), channel_id=1, source_target_pairs={{0,2},{2,0},{1,3},{3,1},{4,6},{6,4},{5,7},{7,5},{8,10},{10,8},{9,1... | collective-permute-start | bytes 393224 | tf_op jit(solution)/shard_map/ppermute | solution.py:359
  46.9 0.5 collective-permute-start.9
  47.4 1.4 %collective-permute-start.1 = (bf16[64,512]{1,0:T(8,128)(2,1)S(1)}, bf16[64,512]{1,0:T(8,128)(2,1)S(1)}, u32[]{:S(2)}, u32[]{:S(2)}) collective-permute-start(bf16[64,512]{1,0:T(8,128)(2,1)S(1)} %collective-permute-done), channel_id=1, source_target_pairs={{0,2},{2,0},{1,3},{3,1},{4,6},{6,4},{5,7},{7,5},{8,10},{10,8},{9,1... | collective-permute-start | bytes 196616 | tf_op jit(solution)/shard_map/ppermute | solution.py:359
  48.8 1.6 %collective-permute-done.2 = bf16[64,512]{1,0:T(8,128)(2,1)S(1)} collective-permute-done((bf16[64,512]{1,0:T(8,128)(2,1)S(1)}, bf16[64,512]{1,0:T(8,128)(2,1)S(1)}, u32[]{:S(2)}, u32[]{:S(2)}) %collective-permute-start.2) | collective-permute-done | bytes 65568 | tf_op jit(solution)/shard_map/ppermute | solution.py:359
  50.4 0.6 collective-permute-start.3
  51.1 2.3 %collective-permute-done.1 = bf16[64,512]{1,0:T(8,128)(2,1)S(1)} collective-permute-done((bf16[64,512]{1,0:T(8,128)(2,1)S(1)}, bf16[64,512]{1,0:T(8,128)(2,1)S(1)}, u32[]{:S(2)}, u32[]{:S(2)}) %collective-permute-start.1) | collective-permute-done | bytes 65568 | tf_op jit(solution)/shard_map/ppermute | solution.py:359
  53.4 0.5 collective-permute-start.8
  53.9 0.8 %collective-permute-done.3 = bf16[64,512]{1,0:T(8,128)(2,1)S(1)} collective-permute-done((bf16[64,512]{1,0:T(8,128)(2,1)S(1)}, bf16[64,512]{1,0:T(8,128)(2,1)S(1)}, u32[]{:S(2)}, u32[]{:S(2)}) %collective-permute-start.3) | collective-permute-done | bytes 65568 | tf_op jit(solution)/shard_map/ppermute | solution.py:359
  54.9 0.6 part.6
  55.5 1.0 %part.7 = (f32[64,1024]{1,0:T(8,128)S(1)}, f32[64,1024]{1,0:T(8,128)S(1)}, f32[64,128]{1,0:T(8,128)S(1)}) custom-call(f32[16,8,128]{2,1,0:T(8,128)S(1)} %all_to_all.15.index_ref.refs_0_, bf16[8192,1024]{1,0:T(8,128)(2,1)S(1)} %bitcast.11, bf16[8192,1024]{1,0:T(8,128)(2,1)S(1)} %bitcast.13, bf16[1,64,512]{2,1,0:T(8,128)(2,1)S(1)} %bitcast.27, ...), custom_call_target="tpu_custom_call" | custom-call | flops 268435456 | bytes 4194304 | tf_op jit(solution)/shard_map/part/pallas_call | solution.py:403
  56.5 1.0 %part.8 = (f32[64,1024]{1,0:T(8,128)S(1)}, f32[64,1024]{1,0:T(8,128)S(1)}, f32[64,128]{1,0:T(8,128)S(1)}) custom-call(f32[16,8,128]{2,1,0:T(8,128)S(1)} %all_to_all.15.index_ref.refs_0_, bf16[8192,1024]{1,0:T(8,128)(2,1)S(1)} %bitcast.11, bf16[8192,1024]{1,0:T(8,128)(2,1)S(1)} %bitcast.13, bf16[1,64,512]{2,1,0:T(8,128)(2,1)S(1)} %bitcast.26, ...), custom_call_target="tpu_custom_call" | custom-call | flops 268435456 | bytes 4194304 | tf_op jit(solution)/shard_map/part/pallas_call | solution.py:403
  57.5 1.4 %part.9 = (f32[64,1024]{1,0:T(8,128)S(1)}, f32[64,1024]{1,0:T(8,128)S(1)}, f32[64,128]{1,0:T(8,128)S(1)}) custom-call(f32[16,8,128]{2,1,0:T(8,128)S(1)} %all_to_all.15.index_ref.refs_0_, bf16[8192,1024]{1,0:T(8,128)(2,1)S(1)} %bitcast.11, bf16[8192,1024]{1,0:T(8,128)(2,1)S(1)} %bitcast.13, bf16[1,64,512]{2,1,0:T(8,128)(2,1)S(1)} %bitcast.23, ...), custom_call_target="tpu_custom_call" | custom-call | flops 268435456 | bytes 4194304 | tf_op jit(solution)/shard_map/part/pallas_call | solution.py:403
  58.9 1.7 %part.10 = (f32[64,1024]{1,0:T(8,128)S(1)}, f32[64,1024]{1,0:T(8,128)S(1)}, f32[64,128]{1,0:T(8,128)S(1)}) custom-call(f32[16,8,128]{2,1,0:T(8,128)S(1)} %all_to_all.15.index_ref.refs_0_, bf16[8192,1024]{1,0:T(8,128)(2,1)S(1)} %bitcast.11, bf16[8192,1024]{1,0:T(8,128)(2,1)S(1)} %bitcast.13, bf16[2,64,512]{2,1,0:T(8,128)(2,1)S(1)} %collective-permute-done.5.refs_3_, ...), custom_call_target="tpu_custom_call" | custom-call | flops 268435456 | bytes 4194304 | tf_op jit(solution)/shard_map/part/pallas_call | solution.py:403
  60.6 1.0 %part.11 = (f32[64,1024]{1,0:T(8,128)S(1)}, f32[64,1024]{1,0:T(8,128)S(1)}, f32[64,128]{1,0:T(8,128)S(1)}) custom-call(f32[16,8,128]{2,1,0:T(8,128)S(1)} %all_to_all.15.index_ref.refs_0_, bf16[8192,1024]{1,0:T(8,128)(2,1)S(1)} %bitcast.11, bf16[8192,1024]{1,0:T(8,128)(2,1)S(1)} %bitcast.13, bf16[1,64,512]{2,1,0:T(8,128)(2,1)S(1)} %bitcast.17, ...), custom_call_target="tpu_custom_call" | custom-call | flops 268435456 | bytes 4194304 | tf_op jit(solution)/shard_map/part/pallas_call | solution.py:403
  61.6 1.7 %final.1 = bf16[2,32,1024]{2,1,0:T(8,128)(2,1)} custom-call(f32[16,8,128]{2,1,0:T(8,128)S(1)} %all_to_all.15.index_ref.refs_0_, bf16[8192,1024]{1,0:T(8,128)(2,1)S(1)} %bitcast.11, bf16[8192,1024]{1,0:T(8,128)(2,1)S(1)} %bitcast.13, bf16[2,64,512]{2,1,0:T(8,128)(2,1)S(1)} %collective-permute-done.4.refs_3_, f32[64,1024]{1,0:T(8,128)S(1)} %get-tuple-element.38.refs_4_, ...), custom_call_target="tpu_custom_call" | custom-call | flops 268435456 | bytes 4194304 | tf_op jit(solution)/shard_map/final/pallas_call | solution.py:403
  (44 shorter events, 0.6 us)
Async XLA Ops:
  0.0 54.8 %slice-start = ((s8[16777216]{0:T(1024)(128)(4,1)}), s8[4194304]{0:T(1024)(128)(4,1)S(1)}, s32[]{:S(2)}) async-start(s8[16777216]{0:T(1024)(128)(4,1)} %bitcast.10), calls=%async_computation.3 | async-start | bytes 8388608
  0.0 54.8 %slice-start.4 = ((s8[16777216]{0:T(1024)(128)(4,1)}), s8[4194304]{0:T(1024)(128)(4,1)S(1)}, s32[]{:S(2)}) async-start(s8[16777216]{0:T(1024)(128)(4,1)} %bitcast.12), calls=%async_computation.7 | async-start | bytes 8388608
  1.0 14.5 %copy-start.3 = (bf16[2,1,128,1024]{3,2,1,0:T(8,128)(2,1)S(1)}, bf16[2,1,128,1024]{3,2,1,0:T(8,128)(2,1)}, u32[]{:S(2)}) copy-start(bf16[2,1,128,1024]{3,2,1,0:T(8,128)(2,1)} %video_ref.1) | copy-start | bytes 1572868
  1.0 26.0 %copy-start = (bf16[1024,3072]{1,0:T(8,128)(2,1)S(1)}, bf16[1024,3072]{1,0:T(8,128)(2,1)}, u32[]{:S(2)}) copy-start(bf16[1024,3072]{1,0:T(8,128)(2,1)} %w_qkv_ref.1) | copy-start | bytes 18874372
  1.0 26.0 %copy-start.1 = (bf16[1024,1024]{1,0:T(8,128)(2,1)S(1)}, bf16[1024,1024]{1,0:T(8,128)(2,1)}, u32[]{:S(2)}) copy-start(bf16[1024,1024]{1,0:T(8,128)(2,1)} %w_out_ref.1) | copy-start | bytes 6291460
  1.0 38.9 %copy-start.2 = (bf16[1024,512]{1,0:T(8,128)(2,1)S(1)}, bf16[1024,512]{1,0:T(8,128)(2,1)}, u32[]{:S(2)}) copy-start(bf16[1024,512]{1,0:T(8,128)(2,1)} %w_proj_ref.1) | copy-start | bytes 3145732
  1.0 38.9 %copy-start.4 = (bf16[512]{0:T(512)(128)(2,1)S(1)}, bf16[512]{0:T(512)(128)(2,1)}, u32[]{:S(2)}) copy-start(bf16[512]{0:T(512)(128)(2,1)} %param.15) | copy-start | bytes 3076
  1.0 53.8 %slice-start.1 = ((s8[16777216]{0:T(1024)(128)(4,1)}), s8[4194304]{0:T(1024)(128)(4,1)S(1)}, s32[]{:S(2)}) async-start(s8[16777216]{0:T(1024)(128)(4,1)} %bitcast.10), calls=%async_computation.4 | async-start | bytes 8388608
  1.0 53.8 %slice-start.2 = ((s8[16777216]{0:T(1024)(128)(4,1)}), s8[4194304]{0:T(1024)(128)(4,1)S(1)}, s32[]{:S(2)}) async-start(s8[16777216]{0:T(1024)(128)(4,1)} %bitcast.10), calls=%async_computation.5 | async-start | bytes 8388608
  1.1 53.8 %slice-start.3 = ((s8[16777216]{0:T(1024)(128)(4,1)}), s8[4194304]{0:T(1024)(128)(4,1)S(1)}, s32[]{:S(2)}) async-start(s8[16777216]{0:T(1024)(128)(4,1)} %bitcast.10), calls=%async_computation.6 | async-start | bytes 8388608
  1.1 53.8 %slice-start.5 = ((s8[16777216]{0:T(1024)(128)(4,1)}), s8[4194304]{0:T(1024)(128)(4,1)S(1)}, s32[]{:S(2)}) async-start(s8[16777216]{0:T(1024)(128)(4,1)} %bitcast.12), calls=%async_computation.8 | async-start | bytes 8388608
  1.1 53.8 %slice-start.6 = ((s8[16777216]{0:T(1024)(128)(4,1)}), s8[4194304]{0:T(1024)(128)(4,1)S(1)}, s32[]{:S(2)}) async-start(s8[16777216]{0:T(1024)(128)(4,1)} %bitcast.12), calls=%async_computation.9 | async-start | bytes 8388608
  1.1 53.8 %slice-start.7 = ((s8[16777216]{0:T(1024)(128)(4,1)}), s8[4194304]{0:T(1024)(128)(4,1)S(1)}, s32[]{:S(2)}) async-start(s8[16777216]{0:T(1024)(128)(4,1)} %bitcast.12), calls=%async_computation.10 | async-start | bytes 8388608
  40.4 5.8 %collective-permute-start = (bf16[64,512]{1,0:T(8,128)(2,1)S(1)}, bf16[64,512]{1,0:T(8,128)(2,1)S(1)}, u32[]{:S(2)}, u32[]{:S(2)}) collective-permute-start(bf16[64,512]{1,0:T(8,128)(2,1)S(1)} %project.1), channel_id=1, source_target_pairs={{0,8},{4,12},{8,0},{12,4},{1,9},{5,13},{9,1},{13,5},{2,10},{6,14},... | collective-permute-start | bytes 196616 | tf_op jit(solution)/shard_map/ppermute | solution.py:359
  40.8 5.4 %collective-permute-start.6 = (bf16[64,512]{1,0:T(8,128)(2,1)S(1)}, bf16[64,512]{1,0:T(8,128)(2,1)S(1)}, u32[]{:S(2)}, u32[]{:S(2)}) collective-permute-start(bf16[64,512]{1,0:T(8,128)(2,1)S(1)} %project.1), channel_id=1, source_target_pairs={{0,4},{4,0},{8,12},{12,8},{1,5},{5,1},{9,13},{13,9},{2,6},{6,2},{1... | collective-permute-start | bytes 196616 | tf_op jit(solution)/shard_map/ppermute | solution.py:359
  46.2 4.3 %collective-permute-start.2 = (bf16[64,512]{1,0:T(8,128)(2,1)S(1)}, bf16[64,512]{1,0:T(8,128)(2,1)S(1)}, u32[]{:S(2)}, u32[]{:S(2)}) collective-permute-start(bf16[64,512]{1,0:T(8,128)(2,1)S(1)} %collective-permute-done), channel_id=1, source_target_pairs={{0,4},{4,0},{8,12},{12,8},{1,5},{5,1},{9,13},{13,9},{2,6},{6,2},{1... | collective-permute-start | bytes 196616 | tf_op jit(solution)/shard_map/ppermute | solution.py:359
  46.2 7.2 %collective-permute-start.7 = (bf16[2,64,512]{2,1,0:T(8,128)(2,1)S(1)}, bf16[2,64,512]{2,1,0:T(8,128)(2,1)S(1)}, u32[]{:S(2)}, u32[]{:S(2)}) collective-permute-start(bf16[2,64,512]{2,1,0:T(8,128)(2,1)S(1)} %pad_maximum_fusion.2), channel_id=1, source_target_pairs={{0,2},{2,0},{1,3},{3,1},{4,6},{6,4},{5,7},{7,5},{8,10},{10,8},{9,1... | collective-permute-start | bytes 393224 | tf_op jit(solution)/shard_map/ppermute | solution.py:359
  46.9 8.6 %collective-permute-start.10 = (bf16[64,512]{1,0:T(8,128)(2,1)S(1)}, bf16[64,512]{1,0:T(8,128)(2,1)S(1)}, u32[]{:S(2)}, u32[]{:S(2)}) collective-permute-start(bf16[64,512]{1,0:T(8,128)(2,1)S(1)} %project.1), channel_id=1, source_target_pairs={{0,1},{1,0},{2,3},{3,2},{4,5},{5,4},{6,7},{7,6},{8,9},{9,8},{10,11... | collective-permute-start | bytes 196616 | tf_op jit(solution)/shard_map/ppermute | solution.py:359
  46.9 9.6 %collective-permute-start.9 = (bf16[64,512]{1,0:T(8,128)(2,1)S(1)}, bf16[64,512]{1,0:T(8,128)(2,1)S(1)}, u32[]{:S(2)}, u32[]{:S(2)}) collective-permute-start(bf16[64,512]{1,0:T(8,128)(2,1)S(1)} %collective-permute-done.6), channel_id=1, source_target_pairs={{0,1},{1,0},{2,3},{3,2},{4,5},{5,4},{6,7},{7,6},{8,9},{9,8},{10,11... | collective-permute-start | bytes 196616 | tf_op jit(solution)/shard_map/ppermute | solution.py:359
  47.4 6.0 %collective-permute-start.1 = (bf16[64,512]{1,0:T(8,128)(2,1)S(1)}, bf16[64,512]{1,0:T(8,128)(2,1)S(1)}, u32[]{:S(2)}, u32[]{:S(2)}) collective-permute-start(bf16[64,512]{1,0:T(8,128)(2,1)S(1)} %collective-permute-done), channel_id=1, source_target_pairs={{0,2},{2,0},{1,3},{3,1},{4,6},{6,4},{5,7},{7,5},{8,10},{10,8},{9,1... | collective-permute-start | bytes 196616 | tf_op jit(solution)/shard_map/ppermute | solution.py:359
  50.4 4.3 %collective-permute-start.3 = (bf16[64,512]{1,0:T(8,128)(2,1)S(1)}, bf16[64,512]{1,0:T(8,128)(2,1)S(1)}, u32[]{:S(2)}, u32[]{:S(2)}) collective-permute-start(bf16[64,512]{1,0:T(8,128)(2,1)S(1)} %collective-permute-done.2), channel_id=1, source_target_pairs={{0,2},{2,0},{1,3},{3,1},{4,6},{6,4},{5,7},{7,5},{8,10},{10,8},{9,1... | collective-permute-start | bytes 196616 | tf_op jit(solution)/shard_map/ppermute | solution.py:359
  53.4 5.5 %collective-permute-start.5 = (bf16[2,64,512]{2,1,0:T(8,128)(2,1)S(1)}, bf16[2,64,512]{2,1,0:T(8,128)(2,1)S(1)}, u32[]{:S(2)}, u32[]{:S(2)}) collective-permute-start(bf16[2,64,512]{2,1,0:T(8,128)(2,1)S(1)} %pad_maximum_fusion.1), channel_id=1, source_target_pairs={{0,1},{1,0},{2,3},{3,2},{4,5},{5,4},{6,7},{7,6},{8,9},{9,8},{10,11... | collective-permute-start | bytes 393224 | tf_op jit(solution)/shard_map/ppermute | solution.py:359
  53.4 5.5 %collective-permute-start.8 = (bf16[2,64,512]{2,1,0:T(8,128)(2,1)S(1)}, bf16[2,64,512]{2,1,0:T(8,128)(2,1)S(1)}, u32[]{:S(2)}, u32[]{:S(2)}) collective-permute-start(bf16[2,64,512]{2,1,0:T(8,128)(2,1)S(1)} %collective-permute-done.7.refs_4_), channel_id=1, source_target_pairs={{0,1},{1,0},{2,3},{3,2},{4,5},{5,4},{6,7},{7,6},{8,9},{9,8},{10,11... | collective-permute-start | bytes 393224 | tf_op jit(solution)/shard_map/ppermute | solution.py:359
  54.7 6.9 %collective-permute-start.4 = (bf16[2,64,512]{2,1,0:T(8,128)(2,1)S(1)}, bf16[2,64,512]{2,1,0:T(8,128)(2,1)S(1)}, u32[]{:S(2)}, u32[]{:S(2)}) collective-permute-start(bf16[2,64,512]{2,1,0:T(8,128)(2,1)S(1)} %pad_maximum_fusion), channel_id=1, source_target_pairs={{0,1},{1,0},{2,3},{3,2},{4,5},{5,4},{6,7},{7,6},{8,9},{9,8},{10,11... | collective-permute-start | bytes 393224 | tf_op jit(solution)/shard_map/ppermute | solution.py:359

commit v7 on v5

--- a/solution.py
+++ b/solution.py
@@ -64,7 +64,7 @@
     spare = out_ref.shape[0] - videos - gain.shape[0]
     if spare:
         rows.append(jnp.zeros((spare, LANES), F32))
-    out_ref[...] = jnp.concatenate(rows, axis=0)
+    out_ref[...] = jnp.concatenate(rows, axis=0).astype(out_ref.dtype)
 
 
 def index_kernel(message_ref, out_ref):
@@ -72,7 +72,8 @@
     row = lax.broadcasted_iota(jnp.int32, message_ref.shape, 0)
     lane = lax.broadcasted_iota(jnp.int32, message_ref.shape, 1)
     free = jnp.logical_and(row == 0, lane == KMAX + 1)
-    out_ref[...] = jnp.where(free[None], peer, message_ref[...][None])
+    message = message_ref[...].astype(F32)
+    out_ref[...] = jnp.where(free[None], peer, message[None]).astype(out_ref.dtype)
 
 
 def select_kernel(index_ref, video_ref, out_ref):
@@ -87,7 +88,7 @@
     token = lax.broadcasted_iota(jnp.int32, (frames, seq), 1)
     patch = lax.broadcasted_iota(jnp.int32, (frames, patches), 1).astype(F32)
     for v in range(videos):
-        table = index_ref[:, v, :]
+        table = index_ref[:, v, :].astype(F32)
         count = table[:, KMAX : KMAX + 1]
         offset = dot32(before, jnp.broadcast_to(count, (frames, LANES)).astype(BF16))[:, :1]
         place = token.astype(F32) - offset
@@ -98,10 +99,10 @@
             at_patch.append(jnp.where(table[:, s : s + 1] == patch, 1.0, 0.0))
         at_token = jnp.concatenate(at_token, axis=0).astype(BF16)
         at_patch = jnp.concatenate(at_patch, axis=0).astype(BF16)
-        chosen = lax.dot_general(
-            at_token, at_patch, (((0,), (0,)), ((), ())), preferred_element_type=F32
+        kept = dot32(at_patch, video_ref[v, 0]).astype(BF16)
+        taken = lax.dot_general(
+            at_token, kept, (((0,), (0,)), ((), ())), preferred_element_type=F32
         ).astype(BF16)
-        taken = dot32(chosen, video_ref[v, 0]).astype(BF16)
         base = v * seq
         for peer in range(base // own, (base + seq) // own):
             first = peer * own - base
@@ -137,7 +138,7 @@
         part = dot32(normed, w_qkv_ref[:, start : start + width])
         return part.astype(BF16).astype(F32).reshape(pairs, packed, width)
 
-    table = index_ref[...]
+    table = index_ref[...].astype(F32)
     row = lax.broadcasted_iota(jnp.int32, (1, packed, LANES), 1)
     upper = row >= own
     me = table[:1, :1, KMAX + 1 : KMAX + 2].astype(jnp.int32)
@@ -175,8 +176,8 @@
     rest = product - coarse.astype(F32)
     fine = rest.astype(BF16)
     last = (rest - fine.astype(F32)).astype(BF16)
-    scores = dot32(coarse, to_head) + dot32(fine, to_head) + dot32(last, to_head)
-    scores = scores.reshape(pairs, packed, LANES) * SCORE_SCALE
+    scores = dot32(jnp.concatenate([coarse, fine, last], axis=0), to_head)
+    scores = jnp.sum(scores.reshape(3, pairs, packed, LANES), axis=0) * SCORE_SCALE
     largest = jnp.max(scores, axis=0)
     largest = jnp.maximum(largest, swap_halves(largest))
     raised = jnp.exp(scores - largest[None])
@@ -209,7 +210,7 @@
 
 
 def places(index_ref, sources):
-    me = jnp.max(index_ref[0, :1, KMAX + 1 : KMAX + 2]).astype(jnp.int32)
+    me = jnp.max(index_ref[0, :1, KMAX + 1 : KMAX + 2].astype(F32)).astype(jnp.int32)
     row = me // NEAR
     found = []
     for flip, steps, direct in sources:
@@ -225,7 +226,7 @@
     gain_rows = -(-columns // LANES)
     squares = jnp.zeros((tokens, LANES), F32)
     for rows_ref, i, place in blocks:
-        inverse = 1.0 / index_ref[place, videos : videos + gain_rows, :]
+        inverse = 1.0 / index_ref[place].astype(F32)[videos : videos + gain_rows]
         for r in range(gain_rows):
             piece = rows_ref[i, :, r * LANES : min((r + 1) * LANES, columns)].astype(F32)
             piece = piece * inverse[r : r + 1, : piece.shape[1]]
@@ -290,7 +291,7 @@
 
 
 def program(video, w_qkv, w_out, keep_list, kept_counts, w_proj, llm_gain, w_gate, w_up):
-    videos, _, _, width = video.shape
+    videos, _, patches, width = video.shape
     axes = ("outer", "mid", "cores")
     frames, outer = lax.axis_size(axes), lax.axis_size("outer")
     seq = frames * TOKL
@@ -303,10 +304,11 @@
     gain = llm_gain.reshape(gain_rows, -1)
 
     counts, listed = kept_counts.T, keep_list
+    kind = BF16 if max(patches, frames) <= 256 else F32
     rows = -(-(videos + gain_rows) // 8) * 8
     message = pl.pallas_call(
         collect_kernel,
-        out_shape=jax.ShapeDtypeStruct((rows, LANES), F32),
+        out_shape=jax.ShapeDtypeStruct((rows, LANES), kind),
         in_specs=[whole(pltpu.HBM)] * 3,
         out_specs=whole(),
         scratch_shapes=[pltpu.VMEM(x.shape, x.dtype) for x in (counts, listed, gain)]
@@ -316,7 +318,7 @@
     )(*(pltpu.with_memory_space_constraint(x, pltpu.HBM) for x in (counts, listed, gain)))
     message = pl.pallas_call(
         index_kernel,
-        out_shape=jax.ShapeDtypeStruct((frames, rows, LANES), F32),
+        out_shape=jax.ShapeDtypeStruct((frames, rows, LANES), kind),
         in_specs=[whole()],
         out_specs=whole(),
         compiler_params=params(2 * MIB),
@@ -369,22 +371,20 @@
 
     direct = outer == DIRECT
     if direct:
-        far = [swap(gained, "outer", k) for k in range(1, outer)]
-        own = gained[None]
-        near, rest = jnp.stack([gained, far[0]]), jnp.stack(far[1:])
+        blocks = [gained] + [swap(gained, "outer", k) for k in range(1, outer)]
+        near, rest = jnp.stack(blocks[:2]), jnp.stack(blocks[2:])
         mid0, mid1 = swap(near, "mid"), swap(rest, "mid")
-        core = swap(own, "cores")
-        core0, core1 = swap(far[0][None], "cores"), swap(rest, "cores")
+        core0, core1 = swap(near, "cores"), swap(rest, "cores")
         both0, both1 = swap(mid0, "cores"), swap(mid1, "cores")
+        first, second = (0, 1), (2, 3)
         stages = (
-            ((own, 0, (0,)),),
-            ((core, 1, (0,)), (far[0][None], 0, (1,))),
-            ((core0, 1, (1,)), (rest, 0, (2, 3))),
-            ((core1, 1, (2, 3)),),
-            ((mid0, 2, (0, 1)),),
-            ((both0, 3, (0, 1)),),
-            ((mid1, 2, (2, 3)),),
-            ((both1, 3, (2, 3)),),
+            ((near, 0, first),),
+            ((core0, 1, first),),
+            ((rest, 0, second),),
+            ((core1, 1, second), (mid0, 2, first),),
+            ((both0, 3, first),),
+            ((mid1, 2, second),),
+            ((both1, 3, second),),
         )
     else:
         line = spread(jnp.broadcast_to(gained[None], (outer,) + gained.shape), "outer")

time: 62.3 us -> 62 us (level)
  Pallas kernels: 13.7 us -> 13 us
  waiting for transfers between devices: 6.73 us -> 7.42 us
    ppermute x10 -> x9, waiting for transfers between devices: 6.73 us -> 7.42 us  [swap(): return lax.ppermute(values, axis, pairs)]
    pallas_call x8 -> x7, Pallas kernels: 8.81 us -> 8.39 us  [program(): pl.pallas_call(functools.partial(final_kernel, sources) if last else func...]
    ppermute x10 -> x9, starting transfers between devices: 5.83 us -> 5.82 us  [swap(): return lax.ppermute(values, axis, pairs)]
  transfers between devices with their start and end apart: 10 -> 9, of which waited for: 4 -> 4; matrix products, arithmetic and copies ran while one was open for 0% -> 0% of each run, Pallas kernels for 11% -> 11%
where the time goes in v7:
time: 62 us; the launch traced here: 61.8 us
  blocking collectives  35.1 us (57%)
  Pallas kernels  13 us (21%)
  waiting for transfers between devices  7.42 us (12%)
  starting transfers between devices  5.82 us (9%)
    all_to_all x1, blocking collectives, program(): index = spread(message, axes)  14.1 us
    all_to_all x1, blocking collectives, program(): seen = spread(chosen, axes)  10.5 us
    all_to_all x1, blocking collectives, program(): token_rows = spread(encoded, axes)  10.5 us
    pallas_call x7, Pallas kernels, program(): pl.pallas_call(functools.partial(final_kernel, sources) if last else func...  8.39 us
    ppermute x9, waiting for transfers between devices, swap(): return lax.ppermute(values, axis, pairs)  7.42 us
    ppermute x9, starting transfers between devices, swap(): return lax.ppermute(values, axis, pairs)  5.82 us
    pallas_call x1, Pallas kernels, program(): pl.pallas_call(attend_kernel, out_shape=jax.ShapeDtypeStruct((frames, pac...  2.48 us
  transfers between devices with their start and end apart: 9, of which 4 were waited for; matrix products, arithmetic and copies ran while one was open for 0% of the time, Pallas kernels for 11%

profile of v7, /device:TPU:0, one launch (start us, length us, event | category | flops | bytes accessed | tf_op | source)
XLA Modules:
  0.0 61.8 jit_solution(9349376968599662913)
XLA Ops:
  0.0 1.0 %collect.1.message_ref = bf16[8,128]{1,0:T(8,128)(2,1)S(1)} custom-call(s32[1,2]{1,0:T(1,128)} %bitcast.16, s32[2,1,128]{2,1,0:T(1,128)} %keep_hbm.1, bf16[4,128]{1,0:T(4,128)(2,1)} %bitcast.11), custom_call_target="tpu_custom_call" | custom-call | tf_op jit(solution)/shard_map/collect/pallas_call | solution.py:309
  1.1 14.1 %all_to_all.15.index_ref.refs_0_ = bf16[16,8,128]{2,1,0:T(8,128)(2,1)S(1)} all-to-all(bf16[16,8,128]{2,1,0:T(8,128)(2,1)S(1)} %index.1), channel_id=1, replica_groups=mesh['groups'=2,'outer'=4,'mid'=2,'cores'=2] {'outer','mid','cores'}, dimensions={0} | all-to-all | bytes 65536 | tf_op jit(solution)/shard_map/all_to_all | solution.py:328
  15.2 0.7 %select.1 = bf16[16,8,512]{2,1,0:T(8,128)(2,1)S(1)} custom-call(bf16[16,8,128]{2,1,0:T(8,128)(2,1)S(1)} %all_to_all.15.index_ref.refs_0_, bf16[2,1,128,1024]{3,2,1,0:T(8,128)(2,1)S(1)} %copy-done.3), custom_call_target="tpu_custom_call" | custom-call | tf_op jit(solution)/shard_map/select/pallas_call | solution.py:330
  16.0 10.5 %all_to_all.16.rows_ref = bf16[16,8,512]{2,1,0:T(8,128)(2,1)S(1)} all-to-all(bf16[16,8,512]{2,1,0:T(8,128)(2,1)S(1)} %select.1), channel_id=1, replica_groups=mesh['groups'=2,'outer'=4,'mid'=2,'cores'=2] {'outer','mid','cores'}, dimensions={0} | all-to-all | bytes 262144 | tf_op jit(solution)/shard_map/all_to_all | solution.py:338
  26.5 2.5 %attend.1 = bf16[16,8,512]{2,1,0:T(8,128)(2,1)S(1)} custom-call(bf16[16,8,128]{2,1,0:T(8,128)(2,1)S(1)} %all_to_all.15.index_ref.refs_0_, bf16[16,8,512]{2,1,0:T(8,128)(2,1)S(1)} %all_to_all.16.rows_ref, bf16[1024,3072]{1,0:T(8,128)(2,1)S(1)} %copy-done, bf16[1024,1024]{1,0:T(8,128)(2,1)S(1)} %copy-done.1), custom_call_target="tpu_custom_call" | custom-call | tf_op jit(solution)/shard_map/attend/pallas_call | solution.py:340
  29.0 10.5 %all_to_all.17.rows_ref = bf16[16,8,512]{2,1,0:T(8,128)(2,1)S(1)} all-to-all(bf16[16,8,512]{2,1,0:T(8,128)(2,1)S(1)} %attend.1), channel_id=1, replica_groups=mesh['groups'=2,'outer'=4,'mid'=2,'cores'=2] {'outer','mid','cores'}, dimensions={0} | all-to-all | bytes 262144 | tf_op jit(solution)/shard_map/all_to_all | solution.py:348
  39.5 0.4 project.1
  39.9 0.1 collective-permute-start.4
  40.0 1.2 %collective-permute-start = (bf16[64,512]{1,0:T(8,128)(2,1)S(1)}, bf16[64,512]{1,0:T(8,128)(2,1)S(1)}, u32[]{:S(2)}, u32[]{:S(2)}) collective-permute-start(bf16[64,512]{1,0:T(8,128)(2,1)S(1)} %project.1), channel_id=1, source_target_pairs={{0,8},{4,12},{8,0},{12,4},{1,9},{5,13},{9,1},{13,5},{2,10},{6,14},... | collective-permute-start | bytes 196616 | tf_op jit(solution)/shard_map/ppermute | solution.py:361
  41.2 3.2 %collective-permute-start.1 = (bf16[64,512]{1,0:T(8,128)(2,1)S(1)}, bf16[64,512]{1,0:T(8,128)(2,1)S(1)}, u32[]{:S(2)}, u32[]{:S(2)}) collective-permute-start(bf16[64,512]{1,0:T(8,128)(2,1)S(1)} %project.1), channel_id=1, source_target_pairs={{0,12},{4,8},{8,4},{12,0},{1,13},{5,9},{9,5},{13,1},{2,14},{6,10},... | collective-permute-start | bytes 196616 | tf_op jit(solution)/shard_map/ppermute | solution.py:361
  44.4 0.3 collective-permute-done.4
  44.7 0.1 collective-permute-start.5
  44.7 3.4 %collective-permute-done = bf16[64,512]{1,0:T(8,128)(2,1)S(1)} collective-permute-done((bf16[64,512]{1,0:T(8,128)(2,1)S(1)}, bf16[64,512]{1,0:T(8,128)(2,1)S(1)}, u32[]{:S(2)}, u32[]{:S(2)}) %collective-permute-start) | collective-permute-done | bytes 65568 | tf_op jit(solution)/shard_map/ppermute | solution.py:361
  48.2 0.8 %collective-permute-start.2 = (bf16[2,64,512]{2,1,0:T(8,128)(2,1)S(1)}, bf16[2,64,512]{2,1,0:T(8,128)(2,1)S(1)}, u32[]{:S(2)}, u32[]{:S(2)}) collective-permute-start(bf16[2,64,512]{2,1,0:T(8,128)(2,1)S(1)} %pad_maximum_fusion.refs_3_), channel_id=1, source_target_pairs={{0,2},{2,0},{1,3},{3,1},{4,6},{6,4},{5,7},{7,5},{8,10},{10,8},{9,1... | collective-permute-start | bytes 393224 | tf_op jit(solution)/shard_map/ppermute | solution.py:361
  49.0 0.5 collective-permute-start.7
  49.5 1.4 %collective-permute-done.5.refs_4_ = bf16[2,64,512]{2,1,0:T(8,128)(2,1)S(1)} collective-permute-done((bf16[2,64,512]{2,1,0:T(8,128)(2,1)S(1)}, bf16[2,64,512]{2,1,0:T(8,128)(2,1)S(1)}, u32[]{:S(2)}, u32[]{:S(2)}) %collective-permute-start.5) | collective-permute-done | bytes 131104 | tf_op jit(solution)/shard_map/ppermute | solution.py:361
  50.9 2.3 %collective-permute-done.2.refs_3_ = bf16[2,64,512]{2,1,0:T(8,128)(2,1)S(1)} collective-permute-done((bf16[2,64,512]{2,1,0:T(8,128)(2,1)S(1)}, bf16[2,64,512]{2,1,0:T(8,128)(2,1)S(1)}, u32[]{:S(2)}, u32[]{:S(2)}) %collective-permute-start.2) | collective-permute-done | bytes 131104 | tf_op jit(solution)/shard_map/ppermute | solution.py:361
  53.3 1.0 %part.6 = (f32[64,1024]{1,0:T(8,128)S(1)}, f32[64,1024]{1,0:T(8,128)S(1)}, f32[64,128]{1,0:T(8,128)S(1)}) custom-call(bf16[16,8,128]{2,1,0:T(8,128)(2,1)S(1)} %all_to_all.15.index_ref.refs_0_, bf16[8192,1024]{1,0:T(8,128)(2,1)S(1)} %bitcast.7, bf16[8192,1024]{1,0:T(8,128)(2,1)S(1)} %bitcast.9, bf16[2,64,512]{2,1,0:T(8,128)(2,1)S(1)} %pad_maximum_fusion.1.refs_3_), custom_call_target="tpu_custom_call" | custom-call | flops 268435456 | bytes 4194304 | tf_op jit(solution)/shard_map/part/pallas_call | solution.py:400
  54.3 1.0 %part.7 = (f32[64,1024]{1,0:T(8,128)S(1)}, f32[64,1024]{1,0:T(8,128)S(1)}, f32[64,128]{1,0:T(8,128)S(1)}) custom-call(bf16[16,8,128]{2,1,0:T(8,128)(2,1)S(1)} %all_to_all.15.index_ref.refs_0_, bf16[8192,1024]{1,0:T(8,128)(2,1)S(1)} %bitcast.7, bf16[8192,1024]{1,0:T(8,128)(2,1)S(1)} %bitcast.9, bf16[2,64,512]{2,1,0:T(8,128)(2,1)S(1)} %collective-permute-done.8.refs_3_, ...), custom_call_target="tpu_custom_call" | custom-call | flops 268435456 | bytes 4194304 | tf_op jit(solution)/shard_map/part/pallas_call | solution.py:400
  55.3 1.0 %part.8 = (f32[64,1024]{1,0:T(8,128)S(1)}, f32[64,1024]{1,0:T(8,128)S(1)}, f32[64,128]{1,0:T(8,128)S(1)}) custom-call(bf16[16,8,128]{2,1,0:T(8,128)(2,1)S(1)} %all_to_all.15.index_ref.refs_0_, bf16[8192,1024]{1,0:T(8,128)(2,1)S(1)} %bitcast.7, bf16[8192,1024]{1,0:T(8,128)(2,1)S(1)} %bitcast.9, bf16[2,64,512]{2,1,0:T(8,128)(2,1)S(1)} %pad_maximum_fusion.refs_3_, ...), custom_call_target="tpu_custom_call" | custom-call | flops 268435456 | bytes 4194304 | tf_op jit(solution)/shard_map/part/pallas_call | solution.py:400
  56.3 1.8 %part.9 = (f32[64,1024]{1,0:T(8,128)S(1)}, f32[64,1024]{1,0:T(8,128)S(1)}, f32[64,128]{1,0:T(8,128)S(1)}) custom-call(bf16[16,8,128]{2,1,0:T(8,128)(2,1)S(1)} %all_to_all.15.index_ref.refs_0_, bf16[8192,1024]{1,0:T(8,128)(2,1)S(1)} %bitcast.7, bf16[8192,1024]{1,0:T(8,128)(2,1)S(1)} %bitcast.9, bf16[2,64,512]{2,1,0:T(8,128)(2,1)S(1)} %collective-permute-done.7.refs_3_, ...), custom_call_target="tpu_custom_call" | custom-call | flops 268435456 | bytes 4194304 | tf_op jit(solution)/shard_map/part/pallas_call | solution.py:400
  58.1 1.0 %part.10 = (f32[64,1024]{1,0:T(8,128)S(1)}, f32[64,1024]{1,0:T(8,128)S(1)}, f32[64,128]{1,0:T(8,128)S(1)}) custom-call(bf16[16,8,128]{2,1,0:T(8,128)(2,1)S(1)} %all_to_all.15.index_ref.refs_0_, bf16[8192,1024]{1,0:T(8,128)(2,1)S(1)} %bitcast.7, bf16[8192,1024]{1,0:T(8,128)(2,1)S(1)} %bitcast.9, bf16[2,64,512]{2,1,0:T(8,128)(2,1)S(1)} %collective-permute-done.6.refs_3_, ...), custom_call_target="tpu_custom_call" | custom-call | flops 268435456 | bytes 4194304 | tf_op jit(solution)/shard_map/part/pallas_call | solution.py:400
  59.1 1.0 %part.11 = (f32[64,1024]{1,0:T(8,128)S(1)}, f32[64,1024]{1,0:T(8,128)S(1)}, f32[64,128]{1,0:T(8,128)S(1)}) custom-call(bf16[16,8,128]{2,1,0:T(8,128)(2,1)S(1)} %all_to_all.15.index_ref.refs_0_, bf16[8192,1024]{1,0:T(8,128)(2,1)S(1)} %bitcast.7, bf16[8192,1024]{1,0:T(8,128)(2,1)S(1)} %bitcast.9, bf16[2,64,512]{2,1,0:T(8,128)(2,1)S(1)} %collective-permute-done.2.refs_3_, ...), custom_call_target="tpu_custom_call" | custom-call | flops 268435456 | bytes 4194304 | tf_op jit(solution)/shard_map/part/pallas_call | solution.py:400
  60.1 1.7 %final.1 = bf16[2,32,1024]{2,1,0:T(8,128)(2,1)} custom-call(bf16[16,8,128]{2,1,0:T(8,128)(2,1)S(1)} %all_to_all.15.index_ref.refs_0_, bf16[8192,1024]{1,0:T(8,128)(2,1)S(1)} %bitcast.7, bf16[8192,1024]{1,0:T(8,128)(2,1)S(1)} %bitcast.9, bf16[2,64,512]{2,1,0:T(8,128)(2,1)S(1)} %collective-permute-done.3.refs_3_, f32[64,1024]{1,0:T(8,128)S(1)} %get-tuple-element.38.refs_4_, ...), custom_call_target="tpu_custom_call" | custom-call | flops 268435456 | bytes 4194304 | tf_op jit(solution)/shard_map/final/pallas_call | solution.py:400
  (39 shorter events, 0.1 us)
Async XLA Ops:
  0.0 53.2 %slice-start = ((s8[16777216]{0:T(1024)(128)(4,1)}), s8[4194304]{0:T(1024)(128)(4,1)S(1)}, s32[]{:S(2)}) async-start(s8[16777216]{0:T(1024)(128)(4,1)} %bitcast.6), calls=%async_computation.3 | async-start | bytes 8388608
  0.0 53.2 %slice-start.4 = ((s8[16777216]{0:T(1024)(128)(4,1)}), s8[4194304]{0:T(1024)(128)(4,1)S(1)}, s32[]{:S(2)}) async-start(s8[16777216]{0:T(1024)(128)(4,1)} %bitcast.8), calls=%async_computation.7 | async-start | bytes 8388608
  1.0 14.3 %copy-start.3 = (bf16[2,1,128,1024]{3,2,1,0:T(8,128)(2,1)S(1)}, bf16[2,1,128,1024]{3,2,1,0:T(8,128)(2,1)}, u32[]{:S(2)}) copy-start(bf16[2,1,128,1024]{3,2,1,0:T(8,128)(2,1)} %video_ref.1) | copy-start | bytes 1572868
  1.0 25.5 %copy-start = (bf16[1024,3072]{1,0:T(8,128)(2,1)S(1)}, bf16[1024,3072]{1,0:T(8,128)(2,1)}, u32[]{:S(2)}) copy-start(bf16[1024,3072]{1,0:T(8,128)(2,1)} %w_qkv_ref.1) | copy-start | bytes 18874372
  1.0 25.5 %copy-start.1 = (bf16[1024,1024]{1,0:T(8,128)(2,1)S(1)}, bf16[1024,1024]{1,0:T(8,128)(2,1)}, u32[]{:S(2)}) copy-start(bf16[1024,1024]{1,0:T(8,128)(2,1)} %w_out_ref.1) | copy-start | bytes 6291460
  1.0 38.5 %copy-start.2 = (bf16[1024,512]{1,0:T(8,128)(2,1)S(1)}, bf16[1024,512]{1,0:T(8,128)(2,1)}, u32[]{:S(2)}) copy-start(bf16[1024,512]{1,0:T(8,128)(2,1)} %w_proj_ref.1) | copy-start | bytes 3145732
  1.0 38.5 %copy-start.4 = (bf16[512]{0:T(512)(128)(2,1)S(1)}, bf16[512]{0:T(512)(128)(2,1)}, u32[]{:S(2)}) copy-start(bf16[512]{0:T(512)(128)(2,1)} %param.15) | copy-start | bytes 3076
  1.0 52.2 %slice-start.1 = ((s8[16777216]{0:T(1024)(128)(4,1)}), s8[4194304]{0:T(1024)(128)(4,1)S(1)}, s32[]{:S(2)}) async-start(s8[16777216]{0:T(1024)(128)(4,1)} %bitcast.6), calls=%async_computation.4 | async-start | bytes 8388608
  1.0 52.2 %slice-start.2 = ((s8[16777216]{0:T(1024)(128)(4,1)}), s8[4194304]{0:T(1024)(128)(4,1)S(1)}, s32[]{:S(2)}) async-start(s8[16777216]{0:T(1024)(128)(4,1)} %bitcast.6), calls=%async_computation.5 | async-start | bytes 8388608
  1.1 52.2 %slice-start.3 = ((s8[16777216]{0:T(1024)(128)(4,1)}), s8[4194304]{0:T(1024)(128)(4,1)S(1)}, s32[]{:S(2)}) async-start(s8[16777216]{0:T(1024)(128)(4,1)} %bitcast.6), calls=%async_computation.6 | async-start | bytes 8388608
  1.1 52.2 %slice-start.5 = ((s8[16777216]{0:T(1024)(128)(4,1)}), s8[4194304]{0:T(1024)(128)(4,1)S(1)}, s32[]{:S(2)}) async-start(s8[16777216]{0:T(1024)(128)(4,1)} %bitcast.8), calls=%async_computation.8 | async-start | bytes 8388608
  1.1 52.2 %slice-start.6 = ((s8[16777216]{0:T(1024)(128)(4,1)}), s8[4194304]{0:T(1024)(128)(4,1)S(1)}, s32[]{:S(2)}) async-start(s8[16777216]{0:T(1024)(128)(4,1)} %bitcast.8), calls=%async_computation.9 | async-start | bytes 8388608
  1.1 52.2 %slice-start.7 = ((s8[16777216]{0:T(1024)(128)(4,1)}), s8[4194304]{0:T(1024)(128)(4,1)S(1)}, s32[]{:S(2)}) async-start(s8[16777216]{0:T(1024)(128)(4,1)} %bitcast.8), calls=%async_computation.10 | async-start | bytes 8388608
  39.9 4.7 %collective-permute-start.4 = (bf16[64,512]{1,0:T(8,128)(2,1)S(1)}, bf16[64,512]{1,0:T(8,128)(2,1)S(1)}, u32[]{:S(2)}, u32[]{:S(2)}) collective-permute-start(bf16[64,512]{1,0:T(8,128)(2,1)S(1)} %project.1), channel_id=1, source_target_pairs={{0,4},{4,0},{8,12},{12,8},{1,5},{5,1},{9,13},{13,9},{2,6},{6,2},{1... | collective-permute-start | bytes 196616 | tf_op jit(solution)/shard_map/ppermute | solution.py:361
  40.0 8.1 %collective-permute-start = (bf16[64,512]{1,0:T(8,128)(2,1)S(1)}, bf16[64,512]{1,0:T(8,128)(2,1)S(1)}, u32[]{:S(2)}, u32[]{:S(2)}) collective-permute-start(bf16[64,512]{1,0:T(8,128)(2,1)S(1)} %project.1), channel_id=1, source_target_pairs={{0,8},{4,12},{8,0},{12,4},{1,9},{5,13},{9,1},{13,5},{2,10},{6,14},... | collective-permute-start | bytes 196616 | tf_op jit(solution)/shard_map/ppermute | solution.py:361
  41.2 7.0 %collective-permute-start.1 = (bf16[64,512]{1,0:T(8,128)(2,1)S(1)}, bf16[64,512]{1,0:T(8,128)(2,1)S(1)}, u32[]{:S(2)}, u32[]{:S(2)}) collective-permute-start(bf16[64,512]{1,0:T(8,128)(2,1)S(1)} %project.1), channel_id=1, source_target_pairs={{0,12},{4,8},{8,4},{12,0},{1,13},{5,9},{9,5},{13,1},{2,14},{6,10},... | collective-permute-start | bytes 196616 | tf_op jit(solution)/shard_map/ppermute | solution.py:361
  44.7 6.3 %collective-permute-start.5 = (bf16[2,64,512]{2,1,0:T(8,128)(2,1)S(1)}, bf16[2,64,512]{2,1,0:T(8,128)(2,1)S(1)}, u32[]{:S(2)}, u32[]{:S(2)}) collective-permute-start(bf16[2,64,512]{2,1,0:T(8,128)(2,1)S(1)} %pad_maximum_fusion.1.refs_3_), channel_id=1, source_target_pairs={{0,2},{2,0},{1,3},{3,1},{4,6},{6,4},{5,7},{7,5},{8,10},{10,8},{9,1... | collective-permute-start | bytes 393224 | tf_op jit(solution)/shard_map/ppermute | solution.py:361
  48.2 5.0 %collective-permute-start.2 = (bf16[2,64,512]{2,1,0:T(8,128)(2,1)S(1)}, bf16[2,64,512]{2,1,0:T(8,128)(2,1)S(1)}, u32[]{:S(2)}, u32[]{:S(2)}) collective-permute-start(bf16[2,64,512]{2,1,0:T(8,128)(2,1)S(1)} %pad_maximum_fusion.refs_3_), channel_id=1, source_target_pairs={{0,2},{2,0},{1,3},{3,1},{4,6},{6,4},{5,7},{7,5},{8,10},{10,8},{9,1... | collective-permute-start | bytes 393224 | tf_op jit(solution)/shard_map/ppermute | solution.py:361
  49.0 5.3 %collective-permute-start.8 = (bf16[2,64,512]{2,1,0:T(8,128)(2,1)S(1)}, bf16[2,64,512]{2,1,0:T(8,128)(2,1)S(1)}, u32[]{:S(2)}, u32[]{:S(2)}) collective-permute-start(bf16[2,64,512]{2,1,0:T(8,128)(2,1)S(1)} %pad_maximum_fusion.1.refs_3_), channel_id=1, source_target_pairs={{0,1},{1,0},{2,3},{3,2},{4,5},{5,4},{6,7},{7,6},{8,9},{9,8},{10,11... | collective-permute-start | bytes 393224 | tf_op jit(solution)/shard_map/ppermute | solution.py:361
  49.0 7.3 %collective-permute-start.7 = (bf16[2,64,512]{2,1,0:T(8,128)(2,1)S(1)}, bf16[2,64,512]{2,1,0:T(8,128)(2,1)S(1)}, u32[]{:S(2)}, u32[]{:S(2)}) collective-permute-start(bf16[2,64,512]{2,1,0:T(8,128)(2,1)S(1)} %pad_maximum_fusion.refs_3_), channel_id=1, source_target_pairs={{0,1},{1,0},{2,3},{3,2},{4,5},{5,4},{6,7},{7,6},{8,9},{9,8},{10,11... | collective-permute-start | bytes 393224 | tf_op jit(solution)/shard_map/ppermute | solution.py:361
  50.9 7.2 %collective-permute-start.6 = (bf16[2,64,512]{2,1,0:T(8,128)(2,1)S(1)}, bf16[2,64,512]{2,1,0:T(8,128)(2,1)S(1)}, u32[]{:S(2)}, u32[]{:S(2)}) collective-permute-start(bf16[2,64,512]{2,1,0:T(8,128)(2,1)S(1)} %collective-permute-done.5.refs_4_), channel_id=1, source_target_pairs={{0,1},{1,0},{2,3},{3,2},{4,5},{5,4},{6,7},{7,6},{8,9},{9,8},{10,11... | collective-permute-start | bytes 393224 | tf_op jit(solution)/shard_map/ppermute | solution.py:361
  53.2 6.9 %collective-permute-start.3 = (bf16[2,64,512]{2,1,0:T(8,128)(2,1)S(1)}, bf16[2,64,512]{2,1,0:T(8,128)(2,1)S(1)}, u32[]{:S(2)}, u32[]{:S(2)}) collective-permute-start(bf16[2,64,512]{2,1,0:T(8,128)(2,1)S(1)} %collective-permute-done.2.refs_3_), channel_id=1, source_target_pairs={{0,1},{1,0},{2,3},{3,2},{4,5},{5,4},{6,7},{7,6},{8,9},{9,8},{10,11... | collective-permute-start | bytes 393224 | tf_op jit(solution)/shard_map/ppermute | solution.py:361

commit v8 on v7

--- a/solution.py
+++ b/solution.py
@@ -16,6 +16,8 @@
 SCORE_SCALE = 0.125
 DIRECT = 4
 NEAR = 4
+BLOCK = 256
+WIDE = 1024
 MIB = 1 << 20
 COVER_FLOPS = 20_000_000_000
 F32 = jnp.float32
@@ -238,10 +240,10 @@
     return squares
 
 
-def products(blocks, w_gate_ref, w_up_ref, begun, emit):
+def products(blocks, w_gate_ref, w_up_ref, begun, emit, limit):
     columns = blocks[0][0].shape[2]
     width = w_gate_ref.shape[1]
-    block = min(width, 256)
+    block = min(width, limit)
     for first in range(0, width, block):
         sums = []
         for i, w_ref in enumerate((w_gate_ref, w_up_ref)):
@@ -272,22 +274,32 @@
 
     squares = square_sums(blocks, videos, index_ref)
     squares_ref[...] = squares + begun[2][...] if begun else squares
-    products(blocks, w_gate_ref, w_up_ref, begun, emit)
+    products(blocks, w_gate_ref, w_up_ref, begun, emit, WIDE)
 
 
 def final_kernel(sources, *refs):
+    refs, (hidden_ref, sems) = refs[:-2], refs[-2:]
     index_ref, w_gate_ref, w_up_ref, blocks, rest = split_refs(sources, refs)
-    begun, out_ref = rest[:3], rest[3]
-    videos = out_ref.shape[0]
+    begun, out_hbm = rest[:3], rest[3]
+    videos = hidden_ref.shape[0]
     squares = begun[2][...] + square_sums(blocks, videos, index_ref)
     mean = jnp.sum(squares, axis=1, keepdims=True) / w_gate_ref.shape[0]
     scale = lax.rsqrt(mean + NORM_EPS)
+    copies = []
 
     def emit(first, block, gate, up):
         hidden = (jax.nn.silu(gate * scale) * (up * scale)).astype(BF16)
-        out_ref[:, :, first : first + block] = hidden.reshape(videos, -1, block)
-
-    products(blocks, w_gate_ref, w_up_ref, begun, emit)
+        units = slice(first, first + block)
+        hidden_ref[:, :, units] = hidden.reshape(videos, -1, block)
+        copy = pltpu.make_async_copy(
+            hidden_ref.at[:, :, units], out_hbm.at[:, :, units], sems.at[len(copies)]
+        )
+        copy.start()
+        copies.append(copy)
+
+    products(blocks, w_gate_ref, w_up_ref, begun, emit, BLOCK)
+    for copy in copies:
+        copy.wait()
 
 
 def program(video, w_qkv, w_out, keep_list, kept_counts, w_proj, llm_gain, w_gate, w_up):
@@ -403,7 +415,13 @@
             else functools.partial(partial_kernel, sources, videos),
             out_shape=jax.ShapeDtypeStruct((videos, seq, units), BF16) if last else sums,
             in_specs=[whole()] * (3 + len(stage) + len(begun)),
-            out_specs=whole() if last else (whole(),) * 3,
+            out_specs=whole(pl.ANY) if last else (whole(),) * 3,
+            scratch_shapes=[
+                pltpu.VMEM((videos, seq, units), BF16),
+                pltpu.SemaphoreType.DMA((-(-units // BLOCK),)),
+            ]
+            if last
+            else [],
             compiler_params=params(3 * MIB + 20 * tokens * units),
             cost_estimate=work,
             name="final" if last else "part",

time: 62 us -> 61.9 us (level)
  no operation moved by 1% of the time
where the time goes in v8:
time: 61.9 us; the launch traced here: 61.7 us
  blocking collectives  35.1 us (57%)
  Pallas kernels  12.9 us (21%)
  waiting for transfers between devices  7.42 us (12%)
  starting transfers between devices  5.82 us (9%)
    all_to_all x1, blocking collectives, program(): index = spread(message, axes)  14.1 us
    all_to_all x1, blocking collectives, program(): seen = spread(chosen, axes)  10.5 us
    all_to_all x1, blocking collectives, program(): token_rows = spread(encoded, axes)  10.5 us
    pallas_call x7, Pallas kernels, program(): pl.pallas_call(functools.partial(final_kernel, sources) if last else func...  8.31 us
    ppermute x9, waiting for transfers between devices, swap(): return lax.ppermute(values, axis, pairs)  7.42 us
    ppermute x9, starting transfers between devices, swap(): return lax.ppermute(values, axis, pairs)  5.82 us
    pallas_call x1, Pallas kernels, program(): pl.pallas_call(attend_kernel, out_shape=jax.ShapeDtypeStruct((frames, pac...  2.48 us
  transfers between devices with their start and end apart: 9, of which 4 were waited for; matrix products, arithmetic and copies ran while one was open for 0% of the time, Pallas kernels for 11%

profile of v8, /device:TPU:0, one launch (start us, length us, event | category | flops | bytes accessed | tf_op | source)
XLA Modules:
  0.0 61.7 jit_solution(14895824392695303233)
XLA Ops:
  0.0 1.0 %collect.1.message_ref = bf16[8,128]{1,0:T(8,128)(2,1)S(1)} custom-call(s32[1,2]{1,0:T(1,128)} %bitcast.16, s32[2,1,128]{2,1,0:T(1,128)} %keep_hbm.1, bf16[4,128]{1,0:T(4,128)(2,1)} %bitcast.11), custom_call_target="tpu_custom_call" | custom-call | tf_op jit(solution)/shard_map/collect/pallas_call | solution.py:321
  1.1 14.1 %all_to_all.15.index_ref.refs_0_ = bf16[16,8,128]{2,1,0:T(8,128)(2,1)S(1)} all-to-all(bf16[16,8,128]{2,1,0:T(8,128)(2,1)S(1)} %index.1), channel_id=1, replica_groups=mesh['groups'=2,'outer'=4,'mid'=2,'cores'=2] {'outer','mid','cores'}, dimensions={0} | all-to-all | bytes 65536 | tf_op jit(solution)/shard_map/all_to_all | solution.py:340
  15.2 0.7 %select.1 = bf16[16,8,512]{2,1,0:T(8,128)(2,1)S(1)} custom-call(bf16[16,8,128]{2,1,0:T(8,128)(2,1)S(1)} %all_to_all.15.index_ref.refs_0_, bf16[2,1,128,1024]{3,2,1,0:T(8,128)(2,1)S(1)} %copy-done.3), custom_call_target="tpu_custom_call" | custom-call | tf_op jit(solution)/shard_map/select/pallas_call | solution.py:342
  16.0 10.5 %all_to_all.16.rows_ref = bf16[16,8,512]{2,1,0:T(8,128)(2,1)S(1)} all-to-all(bf16[16,8,512]{2,1,0:T(8,128)(2,1)S(1)} %select.1), channel_id=1, replica_groups=mesh['groups'=2,'outer'=4,'mid'=2,'cores'=2] {'outer','mid','cores'}, dimensions={0} | all-to-all | bytes 262144 | tf_op jit(solution)/shard_map/all_to_all | solution.py:350
  26.5 2.5 %attend.1 = bf16[16,8,512]{2,1,0:T(8,128)(2,1)S(1)} custom-call(bf16[16,8,128]{2,1,0:T(8,128)(2,1)S(1)} %all_to_all.15.index_ref.refs_0_, bf16[16,8,512]{2,1,0:T(8,128)(2,1)S(1)} %all_to_all.16.rows_ref, bf16[1024,3072]{1,0:T(8,128)(2,1)S(1)} %copy-done, bf16[1024,1024]{1,0:T(8,128)(2,1)S(1)} %copy-done.1), custom_call_target="tpu_custom_call" | custom-call | tf_op jit(solution)/shard_map/attend/pallas_call | solution.py:352
  29.0 10.5 %all_to_all.17.rows_ref = bf16[16,8,512]{2,1,0:T(8,128)(2,1)S(1)} all-to-all(bf16[16,8,512]{2,1,0:T(8,128)(2,1)S(1)} %attend.1), channel_id=1, replica_groups=mesh['groups'=2,'outer'=4,'mid'=2,'cores'=2] {'outer','mid','cores'}, dimensions={0} | all-to-all | bytes 262144 | tf_op jit(solution)/shard_map/all_to_all | solution.py:360
  39.5 0.4 project.1
  39.9 0.1 collective-permute-start.4
  40.0 1.2 %collective-permute-start = (bf16[64,512]{1,0:T(8,128)(2,1)S(1)}, bf16[64,512]{1,0:T(8,128)(2,1)S(1)}, u32[]{:S(2)}, u32[]{:S(2)}) collective-permute-start(bf16[64,512]{1,0:T(8,128)(2,1)S(1)} %project.1), channel_id=1, source_target_pairs={{0,8},{4,12},{8,0},{12,4},{1,9},{5,13},{9,1},{13,5},{2,10},{6,14},... | collective-permute-start | bytes 196616 | tf_op jit(solution)/shard_map/ppermute | solution.py:373
  41.2 3.2 %collective-permute-start.1 = (bf16[64,512]{1,0:T(8,128)(2,1)S(1)}, bf16[64,512]{1,0:T(8,128)(2,1)S(1)}, u32[]{:S(2)}, u32[]{:S(2)}) collective-permute-start(bf16[64,512]{1,0:T(8,128)(2,1)S(1)} %project.1), channel_id=1, source_target_pairs={{0,12},{4,8},{8,4},{12,0},{1,13},{5,9},{9,5},{13,1},{2,14},{6,10},... | collective-permute-start | bytes 196616 | tf_op jit(solution)/shard_map/ppermute | solution.py:373
  44.4 0.3 collective-permute-done.4
  44.7 0.1 collective-permute-start.5
  44.7 3.4 %collective-permute-done = bf16[64,512]{1,0:T(8,128)(2,1)S(1)} collective-permute-done((bf16[64,512]{1,0:T(8,128)(2,1)S(1)}, bf16[64,512]{1,0:T(8,128)(2,1)S(1)}, u32[]{:S(2)}, u32[]{:S(2)}) %collective-permute-start) | collective-permute-done | bytes 65568 | tf_op jit(solution)/shard_map/ppermute | solution.py:373
  48.2 0.8 %collective-permute-start.2 = (bf16[2,64,512]{2,1,0:T(8,128)(2,1)S(1)}, bf16[2,64,512]{2,1,0:T(8,128)(2,1)S(1)}, u32[]{:S(2)}, u32[]{:S(2)}) collective-permute-start(bf16[2,64,512]{2,1,0:T(8,128)(2,1)S(1)} %pad_maximum_fusion.refs_3_), channel_id=1, source_target_pairs={{0,2},{2,0},{1,3},{3,1},{4,6},{6,4},{5,7},{7,5},{8,10},{10,8},{9,1... | collective-permute-start | bytes 393224 | tf_op jit(solution)/shard_map/ppermute | solution.py:373
  49.0 0.5 collective-permute-start.7
  49.5 1.4 %collective-permute-done.5.refs_4_ = bf16[2,64,512]{2,1,0:T(8,128)(2,1)S(1)} collective-permute-done((bf16[2,64,512]{2,1,0:T(8,128)(2,1)S(1)}, bf16[2,64,512]{2,1,0:T(8,128)(2,1)S(1)}, u32[]{:S(2)}, u32[]{:S(2)}) %collective-permute-start.5) | collective-permute-done | bytes 131104 | tf_op jit(solution)/shard_map/ppermute | solution.py:373
  50.9 2.3 %collective-permute-done.2.refs_3_ = bf16[2,64,512]{2,1,0:T(8,128)(2,1)S(1)} collective-permute-done((bf16[2,64,512]{2,1,0:T(8,128)(2,1)S(1)}, bf16[2,64,512]{2,1,0:T(8,128)(2,1)S(1)}, u32[]{:S(2)}, u32[]{:S(2)}) %collective-permute-start.2) | collective-permute-done | bytes 131104 | tf_op jit(solution)/shard_map/ppermute | solution.py:373
  53.3 1.0 %part.6 = (f32[64,1024]{1,0:T(8,128)S(1)}, f32[64,1024]{1,0:T(8,128)S(1)}, f32[64,128]{1,0:T(8,128)S(1)}) custom-call(bf16[16,8,128]{2,1,0:T(8,128)(2,1)S(1)} %all_to_all.15.index_ref.refs_0_, bf16[8192,1024]{1,0:T(8,128)(2,1)S(1)} %bitcast.7, bf16[8192,1024]{1,0:T(8,128)(2,1)S(1)} %bitcast.9, bf16[2,64,512]{2,1,0:T(8,128)(2,1)S(1)} %pad_maximum_fusion.1.refs_3_), custom_call_target="tpu_custom_call" | custom-call | flops 268435456 | bytes 4194304 | tf_op jit(solution)/shard_map/part/pallas_call | solution.py:412
  54.3 1.0 %part.7 = (f32[64,1024]{1,0:T(8,128)S(1)}, f32[64,1024]{1,0:T(8,128)S(1)}, f32[64,128]{1,0:T(8,128)S(1)}) custom-call(bf16[16,8,128]{2,1,0:T(8,128)(2,1)S(1)} %all_to_all.15.index_ref.refs_0_, bf16[8192,1024]{1,0:T(8,128)(2,1)S(1)} %bitcast.7, bf16[8192,1024]{1,0:T(8,128)(2,1)S(1)} %bitcast.9, bf16[2,64,512]{2,1,0:T(8,128)(2,1)S(1)} %collective-permute-done.8.refs_3_, ...), custom_call_target="tpu_custom_call" | custom-call | flops 268435456 | bytes 4194304 | tf_op jit(solution)/shard_map/part/pallas_call | solution.py:412
  55.3 1.0 %part.8 = (f32[64,1024]{1,0:T(8,128)S(1)}, f32[64,1024]{1,0:T(8,128)S(1)}, f32[64,128]{1,0:T(8,128)S(1)}) custom-call(bf16[16,8,128]{2,1,0:T(8,128)(2,1)S(1)} %all_to_all.15.index_ref.refs_0_, bf16[8192,1024]{1,0:T(8,128)(2,1)S(1)} %bitcast.7, bf16[8192,1024]{1,0:T(8,128)(2,1)S(1)} %bitcast.9, bf16[2,64,512]{2,1,0:T(8,128)(2,1)S(1)} %pad_maximum_fusion.refs_3_, ...), custom_call_target="tpu_custom_call" | custom-call | flops 268435456 | bytes 4194304 | tf_op jit(solution)/shard_map/part/pallas_call | solution.py:412
  56.3 1.7 %part.9 = (f32[64,1024]{1,0:T(8,128)S(1)}, f32[64,1024]{1,0:T(8,128)S(1)}, f32[64,128]{1,0:T(8,128)S(1)}) custom-call(bf16[16,8,128]{2,1,0:T(8,128)(2,1)S(1)} %all_to_all.15.index_ref.refs_0_, bf16[8192,1024]{1,0:T(8,128)(2,1)S(1)} %bitcast.7, bf16[8192,1024]{1,0:T(8,128)(2,1)S(1)} %bitcast.9, bf16[2,64,512]{2,1,0:T(8,128)(2,1)S(1)} %collective-permute-done.7.refs_3_, ...), custom_call_target="tpu_custom_call" | custom-call | flops 268435456 | bytes 4194304 | tf_op jit(solution)/shard_map/part/pallas_call | solution.py:412
  58.0 1.0 %part.10 = (f32[64,1024]{1,0:T(8,128)S(1)}, f32[64,1024]{1,0:T(8,128)S(1)}, f32[64,128]{1,0:T(8,128)S(1)}) custom-call(bf16[16,8,128]{2,1,0:T(8,128)(2,1)S(1)} %all_to_all.15.index_ref.refs_0_, bf16[8192,1024]{1,0:T(8,128)(2,1)S(1)} %bitcast.7, bf16[8192,1024]{1,0:T(8,128)(2,1)S(1)} %bitcast.9, bf16[2,64,512]{2,1,0:T(8,128)(2,1)S(1)} %collective-permute-done.6.refs_3_, ...), custom_call_target="tpu_custom_call" | custom-call | flops 268435456 | bytes 4194304 | tf_op jit(solution)/shard_map/part/pallas_call | solution.py:412
  59.0 1.0 %part.11 = (f32[64,1024]{1,0:T(8,128)S(1)}, f32[64,1024]{1,0:T(8,128)S(1)}, f32[64,128]{1,0:T(8,128)S(1)}) custom-call(bf16[16,8,128]{2,1,0:T(8,128)(2,1)S(1)} %all_to_all.15.index_ref.refs_0_, bf16[8192,1024]{1,0:T(8,128)(2,1)S(1)} %bitcast.7, bf16[8192,1024]{1,0:T(8,128)(2,1)S(1)} %bitcast.9, bf16[2,64,512]{2,1,0:T(8,128)(2,1)S(1)} %collective-permute-done.2.refs_3_, ...), custom_call_target="tpu_custom_call" | custom-call | flops 268435456 | bytes 4194304 | tf_op jit(solution)/shard_map/part/pallas_call | solution.py:412
  60.0 1.7 %final.1 = bf16[2,32,1024]{2,1,0:T(8,128)(2,1)} custom-call(bf16[16,8,128]{2,1,0:T(8,128)(2,1)S(1)} %all_to_all.15.index_ref.refs_0_, bf16[8192,1024]{1,0:T(8,128)(2,1)S(1)} %bitcast.7, bf16[8192,1024]{1,0:T(8,128)(2,1)S(1)} %bitcast.9, bf16[2,64,512]{2,1,0:T(8,128)(2,1)S(1)} %collective-permute-done.3.refs_3_, f32[64,1024]{1,0:T(8,128)S(1)} %get-tuple-element.38.refs_4_, ...), custom_call_target="tpu_custom_call" | custom-call | flops 268435456 | bytes 4194304 | tf_op jit(solution)/shard_map/final/pallas_call | solution.py:412
  (39 shorter events, 0.1 us)
Async XLA Ops:
  0.0 53.2 %slice-start = ((s8[16777216]{0:T(1024)(128)(4,1)}), s8[4194304]{0:T(1024)(128)(4,1)S(1)}, s32[]{:S(2)}) async-start(s8[16777216]{0:T(1024)(128)(4,1)} %bitcast.6), calls=%async_computation.3 | async-start | bytes 8388608
  0.0 53.2 %slice-start.4 = ((s8[16777216]{0:T(1024)(128)(4,1)}), s8[4194304]{0:T(1024)(128)(4,1)S(1)}, s32[]{:S(2)}) async-start(s8[16777216]{0:T(1024)(128)(4,1)} %bitcast.8), calls=%async_computation.7 | async-start | bytes 8388608
  1.0 14.3 %copy-start.3 = (bf16[2,1,128,1024]{3,2,1,0:T(8,128)(2,1)S(1)}, bf16[2,1,128,1024]{3,2,1,0:T(8,128)(2,1)}, u32[]{:S(2)}) copy-start(bf16[2,1,128,1024]{3,2,1,0:T(8,128)(2,1)} %video_ref.1) | copy-start | bytes 1572868
  1.0 25.5 %copy-start = (bf16[1024,3072]{1,0:T(8,128)(2,1)S(1)}, bf16[1024,3072]{1,0:T(8,128)(2,1)}, u32[]{:S(2)}) copy-start(bf16[1024,3072]{1,0:T(8,128)(2,1)} %w_qkv_ref.1) | copy-start | bytes 18874372
  1.0 25.5 %copy-start.1 = (bf16[1024,1024]{1,0:T(8,128)(2,1)S(1)}, bf16[1024,1024]{1,0:T(8,128)(2,1)}, u32[]{:S(2)}) copy-start(bf16[1024,1024]{1,0:T(8,128)(2,1)} %w_out_ref.1) | copy-start | bytes 6291460
  1.0 38.5 %copy-start.2 = (bf16[1024,512]{1,0:T(8,128)(2,1)S(1)}, bf16[1024,512]{1,0:T(8,128)(2,1)}, u32[]{:S(2)}) copy-start(bf16[1024,512]{1,0:T(8,128)(2,1)} %w_proj_ref.1) | copy-start | bytes 3145732
  1.0 38.5 %copy-start.4 = (bf16[512]{0:T(512)(128)(2,1)S(1)}, bf16[512]{0:T(512)(128)(2,1)}, u32[]{:S(2)}) copy-start(bf16[512]{0:T(512)(128)(2,1)} %param.15) | copy-start | bytes 3076
  1.0 52.2 %slice-start.1 = ((s8[16777216]{0:T(1024)(128)(4,1)}), s8[4194304]{0:T(1024)(128)(4,1)S(1)}, s32[]{:S(2)}) async-start(s8[16777216]{0:T(1024)(128)(4,1)} %bitcast.6), calls=%async_computation.4 | async-start | bytes 8388608
  1.0 52.2 %slice-start.2 = ((s8[16777216]{0:T(1024)(128)(4,1)}), s8[4194304]{0:T(1024)(128)(4,1)S(1)}, s32[]{:S(2)}) async-start(s8[16777216]{0:T(1024)(128)(4,1)} %bitcast.6), calls=%async_computation.5 | async-start | bytes 8388608
  1.1 52.2 %slice-start.3 = ((s8[16777216]{0:T(1024)(128)(4,1)}), s8[4194304]{0:T(1024)(128)(4,1)S(1)}, s32[]{:S(2)}) async-start(s8[16777216]{0:T(1024)(128)(4,1)} %bitcast.6), calls=%async_computation.6 | async-start | bytes 8388608
  1.1 52.2 %slice-start.5 = ((s8[16777216]{0:T(1024)(128)(4,1)}), s8[4194304]{0:T(1024)(128)(4,1)S(1)}, s32[]{:S(2)}) async-start(s8[16777216]{0:T(1024)(128)(4,1)} %bitcast.8), calls=%async_computation.8 | async-start | bytes 8388608
  1.1 52.2 %slice-start.6 = ((s8[16777216]{0:T(1024)(128)(4,1)}), s8[4194304]{0:T(1024)(128)(4,1)S(1)}, s32[]{:S(2)}) async-start(s8[16777216]{0:T(1024)(128)(4,1)} %bitcast.8), calls=%async_computation.9 | async-start | bytes 8388608
  1.1 52.2 %slice-start.7 = ((s8[16777216]{0:T(1024)(128)(4,1)}), s8[4194304]{0:T(1024)(128)(4,1)S(1)}, s32[]{:S(2)}) async-start(s8[16777216]{0:T(1024)(128)(4,1)} %bitcast.8), calls=%async_computation.10 | async-start | bytes 8388608
  39.9 4.7 %collective-permute-start.4 = (bf16[64,512]{1,0:T(8,128)(2,1)S(1)}, bf16[64,512]{1,0:T(8,128)(2,1)S(1)}, u32[]{:S(2)}, u32[]{:S(2)}) collective-permute-start(bf16[64,512]{1,0:T(8,128)(2,1)S(1)} %project.1), channel_id=1, source_target_pairs={{0,4},{4,0},{8,12},{12,8},{1,5},{5,1},{9,13},{13,9},{2,6},{6,2},{1... | collective-permute-start | bytes 196616 | tf_op jit(solution)/shard_map/ppermute | solution.py:373
  40.0 8.1 %collective-permute-start = (bf16[64,512]{1,0:T(8,128)(2,1)S(1)}, bf16[64,512]{1,0:T(8,128)(2,1)S(1)}, u32[]{:S(2)}, u32[]{:S(2)}) collective-permute-start(bf16[64,512]{1,0:T(8,128)(2,1)S(1)} %project.1), channel_id=1, source_target_pairs={{0,8},{4,12},{8,0},{12,4},{1,9},{5,13},{9,1},{13,5},{2,10},{6,14},... | collective-permute-start | bytes 196616 | tf_op jit(solution)/shard_map/ppermute | solution.py:373
  41.2 7.0 %collective-permute-start.1 = (bf16[64,512]{1,0:T(8,128)(2,1)S(1)}, bf16[64,512]{1,0:T(8,128)(2,1)S(1)}, u32[]{:S(2)}, u32[]{:S(2)}) collective-permute-start(bf16[64,512]{1,0:T(8,128)(2,1)S(1)} %project.1), channel_id=1, source_target_pairs={{0,12},{4,8},{8,4},{12,0},{1,13},{5,9},{9,5},{13,1},{2,14},{6,10},... | collective-permute-start | bytes 196616 | tf_op jit(solution)/shard_map/ppermute | solution.py:373
  44.7 6.3 %collective-permute-start.5 = (bf16[2,64,512]{2,1,0:T(8,128)(2,1)S(1)}, bf16[2,64,512]{2,1,0:T(8,128)(2,1)S(1)}, u32[]{:S(2)}, u32[]{:S(2)}) collective-permute-start(bf16[2,64,512]{2,1,0:T(8,128)(2,1)S(1)} %pad_maximum_fusion.1.refs_3_), channel_id=1, source_target_pairs={{0,2},{2,0},{1,3},{3,1},{4,6},{6,4},{5,7},{7,5},{8,10},{10,8},{9,1... | collective-permute-start | bytes 393224 | tf_op jit(solution)/shard_map/ppermute | solution.py:373
  48.2 5.0 %collective-permute-start.2 = (bf16[2,64,512]{2,1,0:T(8,128)(2,1)S(1)}, bf16[2,64,512]{2,1,0:T(8,128)(2,1)S(1)}, u32[]{:S(2)}, u32[]{:S(2)}) collective-permute-start(bf16[2,64,512]{2,1,0:T(8,128)(2,1)S(1)} %pad_maximum_fusion.refs_3_), channel_id=1, source_target_pairs={{0,2},{2,0},{1,3},{3,1},{4,6},{6,4},{5,7},{7,5},{8,10},{10,8},{9,1... | collective-permute-start | bytes 393224 | tf_op jit(solution)/shard_map/ppermute | solution.py:373
  49.0 5.3 %collective-permute-start.8 = (bf16[2,64,512]{2,1,0:T(8,128)(2,1)S(1)}, bf16[2,64,512]{2,1,0:T(8,128)(2,1)S(1)}, u32[]{:S(2)}, u32[]{:S(2)}) collective-permute-start(bf16[2,64,512]{2,1,0:T(8,128)(2,1)S(1)} %pad_maximum_fusion.1.refs_3_), channel_id=1, source_target_pairs={{0,1},{1,0},{2,3},{3,2},{4,5},{5,4},{6,7},{7,6},{8,9},{9,8},{10,11... | collective-permute-start | bytes 393224 | tf_op jit(solution)/shard_map/ppermute | solution.py:373
  49.0 7.3 %collective-permute-start.7 = (bf16[2,64,512]{2,1,0:T(8,128)(2,1)S(1)}, bf16[2,64,512]{2,1,0:T(8,128)(2,1)S(1)}, u32[]{:S(2)}, u32[]{:S(2)}) collective-permute-start(bf16[2,64,512]{2,1,0:T(8,128)(2,1)S(1)} %pad_maximum_fusion.refs_3_), channel_id=1, source_target_pairs={{0,1},{1,0},{2,3},{3,2},{4,5},{5,4},{6,7},{7,6},{8,9},{9,8},{10,11... | collective-permute-start | bytes 393224 | tf_op jit(solution)/shard_map/ppermute | solution.py:373
  50.9 7.1 %collective-permute-start.6 = (bf16[2,64,512]{2,1,0:T(8,128)(2,1)S(1)}, bf16[2,64,512]{2,1,0:T(8,128)(2,1)S(1)}, u32[]{:S(2)}, u32[]{:S(2)}) collective-permute-start(bf16[2,64,512]{2,1,0:T(8,128)(2,1)S(1)} %collective-permute-done.5.refs_4_), channel_id=1, source_target_pairs={{0,1},{1,0},{2,3},{3,2},{4,5},{5,4},{6,7},{7,6},{8,9},{9,8},{10,11... | collective-permute-start | bytes 393224 | tf_op jit(solution)/shard_map/ppermute | solution.py:373
  53.2 6.8 %collective-permute-start.3 = (bf16[2,64,512]{2,1,0:T(8,128)(2,1)S(1)}, bf16[2,64,512]{2,1,0:T(8,128)(2,1)S(1)}, u32[]{:S(2)}, u32[]{:S(2)}) collective-permute-start(bf16[2,64,512]{2,1,0:T(8,128)(2,1)S(1)} %collective-permute-done.2.refs_3_), channel_id=1, source_target_pairs={{0,1},{1,0},{2,3},{3,2},{4,5},{5,4},{6,7},{7,6},{8,9},{9,8},{10,11... | collective-permute-start | bytes 393224 | tf_op jit(solution)/shard_map/ppermute | solution.py:373

commit v9 on v8

--- a/solution.py
+++ b/solution.py
@@ -41,7 +41,7 @@
     return pltpu.CompilerParams(vmem_limit_bytes=int(limit))
 
 
-def collect_kernel(counts_hbm, keep_hbm, gain_hbm, out_ref, counts_ref, keep_ref, gain_ref, sems):
+def index_kernel(counts_hbm, keep_hbm, gain_hbm, out_ref, counts_ref, keep_ref, gain_ref, sems):
     arrays = ((counts_hbm, counts_ref), (keep_hbm, keep_ref), (gain_hbm, gain_ref))
     copies = [
         pltpu.make_async_copy(source, target, sems.at[i])
@@ -52,6 +52,7 @@
     for copy in copies:
         copy.wait()
     videos = keep_ref.shape[0]
+    peers, height, _ = out_ref.shape
     lane = lax.broadcasted_iota(jnp.int32, (1, LANES), 1)
     counts = counts_ref[...].astype(F32)
     rows = []
@@ -63,18 +64,14 @@
         fill = jnp.ones((gain.shape[0], LANES - gain.shape[1]), F32)
         gain = jnp.concatenate([gain, fill], axis=1)
     rows.append(gain)
-    spare = out_ref.shape[0] - videos - gain.shape[0]
+    spare = height - videos - gain.shape[0]
     if spare:
         rows.append(jnp.zeros((spare, LANES), F32))
-    out_ref[...] = jnp.concatenate(rows, axis=0).astype(out_ref.dtype)
-
-
-def index_kernel(message_ref, out_ref):
-    peer = lax.broadcasted_iota(jnp.int32, (out_ref.shape[0], 1, LANES), 0).astype(F32)
-    row = lax.broadcasted_iota(jnp.int32, message_ref.shape, 0)
-    lane = lax.broadcasted_iota(jnp.int32, message_ref.shape, 1)
+    message = jnp.concatenate(rows, axis=0)
+    peer = lax.broadcasted_iota(jnp.int32, (peers, 1, LANES), 0).astype(F32)
+    row = lax.broadcasted_iota(jnp.int32, (height, LANES), 0)
+    lane = lax.broadcasted_iota(jnp.int32, (height, LANES), 1)
     free = jnp.logical_and(row == 0, lane == KMAX + 1)
-    message = message_ref[...].astype(F32)
     out_ref[...] = jnp.where(free[None], peer, message[None]).astype(out_ref.dtype)
 
 
@@ -319,24 +316,16 @@
     kind = BF16 if max(patches, frames) <= 256 else F32
     rows = -(-(videos + gain_rows) // 8) * 8
     message = pl.pallas_call(
-        collect_kernel,
-        out_shape=jax.ShapeDtypeStruct((rows, LANES), kind),
+        index_kernel,
+        out_shape=jax.ShapeDtypeStruct((frames, rows, LANES), kind),
         in_specs=[whole(pltpu.HBM)] * 3,
         out_specs=whole(),
         scratch_shapes=[pltpu.VMEM(x.shape, x.dtype) for x in (counts, listed, gain)]
         + [pltpu.SemaphoreType.DMA((3,))],
         compiler_params=params(2 * MIB),
-        name="collect",
-    )(*(pltpu.with_memory_space_constraint(x, pltpu.HBM) for x in (counts, listed, gain)))
-    message = pl.pallas_call(
-        index_kernel,
-        out_shape=jax.ShapeDtypeStruct((frames, rows, LANES), kind),
-        in_specs=[whole()],
-        out_specs=whole(),
-        compiler_params=params(2 * MIB),
         cost_estimate=pl.CostEstimate(flops=COVER_FLOPS, bytes_accessed=65536, transcendentals=0),
         name="index",
-    )(message)
+    )(*(pltpu.with_memory_space_constraint(x, pltpu.HBM) for x in (counts, listed, gain)))
     index = spread(message, axes)
 
     chosen = pl.pallas_call(

time: 61.9 us -> 61.9 us (level)
    pallas_call x1 -> x0, Pallas kernels: 0.96 us -> none  [program(): pl.pallas_call(collect_kernel, out_shape=jax.ShapeDtypeStruct((rows, LANE...]
    pallas_call x1, Pallas kernels: 0.01 us -> 0.94 us  [program(): pl.pallas_call(index_kernel, out_shape=jax.ShapeDtypeStruct((frames, rows...]
where the time goes in v9:
time: 61.9 us; the launch traced here: 61.6 us
  blocking collectives  35.1 us (57%)
  Pallas kernels  12.9 us (21%)
  waiting for transfers between devices  7.42 us (12%)
  starting transfers between devices  5.82 us (9%)
    all_to_all x1, blocking collectives, program(): index = spread(message, axes)  14.1 us
    all_to_all x1, blocking collectives, program(): seen = spread(chosen, axes)  10.5 us
    all_to_all x1, blocking collectives, program(): token_rows = spread(encoded, axes)  10.5 us
    pallas_call x7, Pallas kernels, program(): pl.pallas_call(functools.partial(final_kernel, sources) if last else func...  8.31 us
    ppermute x9, waiting for transfers between devices, swap(): return lax.ppermute(values, axis, pairs)  7.42 us
    ppermute x9, starting transfers between devices, swap(): return lax.ppermute(values, axis, pairs)  5.82 us
    pallas_call x1, Pallas kernels, program(): pl.pallas_call(attend_kernel, out_shape=jax.ShapeDtypeStruct((frames, pac...  2.48 us
  transfers between devices with their start and end apart: 9, of which 4 were waited for; matrix products, arithmetic and copies ran while one was open for 0% of the time, Pallas kernels for 11%

profile of v9, /device:TPU:0, one launch (start us, length us, event | category | flops | bytes accessed | tf_op | source)
XLA Modules:
  0.0 61.6 jit_solution(3405612614510666472)
XLA Ops:
  0.1 0.9 %index.1 = bf16[16,8,128]{2,1,0:T(8,128)(2,1)S(1)} custom-call(s32[1,2]{1,0:T(1,128)} %bitcast.16, s32[2,1,128]{2,1,0:T(1,128)} %keep_hbm.1, bf16[4,128]{1,0:T(4,128)(2,1)} %bitcast.11), custom_call_target="tpu_custom_call" | custom-call | flops 20000000000 | bytes 65536 | tf_op jit(solution)/shard_map/index/pallas_call | solution.py:318
  1.0 14.1 %all_to_all.15.index_ref.refs_0_ = bf16[16,8,128]{2,1,0:T(8,128)(2,1)S(1)} all-to-all(bf16[16,8,128]{2,1,0:T(8,128)(2,1)S(1)} %index.1), channel_id=1, replica_groups=mesh['groups'=2,'outer'=4,'mid'=2,'cores'=2] {'outer','mid','cores'}, dimensions={0} | all-to-all | bytes 65536 | tf_op jit(solution)/shard_map/all_to_all | solution.py:329
  15.2 0.8 %select.1 = bf16[16,8,512]{2,1,0:T(8,128)(2,1)S(1)} custom-call(bf16[16,8,128]{2,1,0:T(8,128)(2,1)S(1)} %all_to_all.15.index_ref.refs_0_, bf16[2,1,128,1024]{3,2,1,0:T(8,128)(2,1)S(1)} %copy-done.3), custom_call_target="tpu_custom_call" | custom-call | tf_op jit(solution)/shard_map/select/pallas_call | solution.py:331
  15.9 10.5 %all_to_all.16.rows_ref = bf16[16,8,512]{2,1,0:T(8,128)(2,1)S(1)} all-to-all(bf16[16,8,512]{2,1,0:T(8,128)(2,1)S(1)} %select.1), channel_id=1, replica_groups=mesh['groups'=2,'outer'=4,'mid'=2,'cores'=2] {'outer','mid','cores'}, dimensions={0} | all-to-all | bytes 262144 | tf_op jit(solution)/shard_map/all_to_all | solution.py:339
  26.4 2.5 %attend.1 = bf16[16,8,512]{2,1,0:T(8,128)(2,1)S(1)} custom-call(bf16[16,8,128]{2,1,0:T(8,128)(2,1)S(1)} %all_to_all.15.index_ref.refs_0_, bf16[16,8,512]{2,1,0:T(8,128)(2,1)S(1)} %all_to_all.16.rows_ref, bf16[1024,3072]{1,0:T(8,128)(2,1)S(1)} %copy-done, bf16[1024,1024]{1,0:T(8,128)(2,1)S(1)} %copy-done.1), custom_call_target="tpu_custom_call" | custom-call | tf_op jit(solution)/shard_map/attend/pallas_call | solution.py:341
  28.9 10.5 %all_to_all.17.rows_ref = bf16[16,8,512]{2,1,0:T(8,128)(2,1)S(1)} all-to-all(bf16[16,8,512]{2,1,0:T(8,128)(2,1)S(1)} %attend.1), channel_id=1, replica_groups=mesh['groups'=2,'outer'=4,'mid'=2,'cores'=2] {'outer','mid','cores'}, dimensions={0} | all-to-all | bytes 262144 | tf_op jit(solution)/shard_map/all_to_all | solution.py:349
  39.4 0.4 project.1
  39.9 0.1 collective-permute-start.4
  39.9 1.2 %collective-permute-start = (bf16[64,512]{1,0:T(8,128)(2,1)S(1)}, bf16[64,512]{1,0:T(8,128)(2,1)S(1)}, u32[]{:S(2)}, u32[]{:S(2)}) collective-permute-start(bf16[64,512]{1,0:T(8,128)(2,1)S(1)} %project.1), channel_id=1, source_target_pairs={{0,8},{4,12},{8,0},{12,4},{1,9},{5,13},{9,1},{13,5},{2,10},{6,14},... | collective-permute-start | bytes 196616 | tf_op jit(solution)/shard_map/ppermute | solution.py:362
  41.1 3.2 %collective-permute-start.1 = (bf16[64,512]{1,0:T(8,128)(2,1)S(1)}, bf16[64,512]{1,0:T(8,128)(2,1)S(1)}, u32[]{:S(2)}, u32[]{:S(2)}) collective-permute-start(bf16[64,512]{1,0:T(8,128)(2,1)S(1)} %project.1), channel_id=1, source_target_pairs={{0,12},{4,8},{8,4},{12,0},{1,13},{5,9},{9,5},{13,1},{2,14},{6,10},... | collective-permute-start | bytes 196616 | tf_op jit(solution)/shard_map/ppermute | solution.py:362
  44.3 0.3 collective-permute-done.4
  44.6 0.1 collective-permute-start.5
  44.7 3.4 %collective-permute-done = bf16[64,512]{1,0:T(8,128)(2,1)S(1)} collective-permute-done((bf16[64,512]{1,0:T(8,128)(2,1)S(1)}, bf16[64,512]{1,0:T(8,128)(2,1)S(1)}, u32[]{:S(2)}, u32[]{:S(2)}) %collective-permute-start) | collective-permute-done | bytes 65568 | tf_op jit(solution)/shard_map/ppermute | solution.py:362
  48.1 0.8 %collective-permute-start.2 = (bf16[2,64,512]{2,1,0:T(8,128)(2,1)S(1)}, bf16[2,64,512]{2,1,0:T(8,128)(2,1)S(1)}, u32[]{:S(2)}, u32[]{:S(2)}) collective-permute-start(bf16[2,64,512]{2,1,0:T(8,128)(2,1)S(1)} %pad_maximum_fusion.refs_3_), channel_id=1, source_target_pairs={{0,2},{2,0},{1,3},{3,1},{4,6},{6,4},{5,7},{7,5},{8,10},{10,8},{9,1... | collective-permute-start | bytes 393224 | tf_op jit(solution)/shard_map/ppermute | solution.py:362
  48.9 0.5 collective-permute-start.7
  49.4 1.4 %collective-permute-done.5.refs_4_ = bf16[2,64,512]{2,1,0:T(8,128)(2,1)S(1)} collective-permute-done((bf16[2,64,512]{2,1,0:T(8,128)(2,1)S(1)}, bf16[2,64,512]{2,1,0:T(8,128)(2,1)S(1)}, u32[]{:S(2)}, u32[]{:S(2)}) %collective-permute-start.5) | collective-permute-done | bytes 131104 | tf_op jit(solution)/shard_map/ppermute | solution.py:362
  50.8 2.3 %collective-permute-done.2.refs_3_ = bf16[2,64,512]{2,1,0:T(8,128)(2,1)S(1)} collective-permute-done((bf16[2,64,512]{2,1,0:T(8,128)(2,1)S(1)}, bf16[2,64,512]{2,1,0:T(8,128)(2,1)S(1)}, u32[]{:S(2)}, u32[]{:S(2)}) %collective-permute-start.2) | collective-permute-done | bytes 131104 | tf_op jit(solution)/shard_map/ppermute | solution.py:362
  53.2 1.0 %part.6 = (f32[64,1024]{1,0:T(8,128)S(1)}, f32[64,1024]{1,0:T(8,128)S(1)}, f32[64,128]{1,0:T(8,128)S(1)}) custom-call(bf16[16,8,128]{2,1,0:T(8,128)(2,1)S(1)} %all_to_all.15.index_ref.refs_0_, bf16[8192,1024]{1,0:T(8,128)(2,1)S(1)} %bitcast.7, bf16[8192,1024]{1,0:T(8,128)(2,1)S(1)} %bitcast.9, bf16[2,64,512]{2,1,0:T(8,128)(2,1)S(1)} %pad_maximum_fusion.1.refs_3_), custom_call_target="tpu_custom_call" | custom-call | flops 268435456 | bytes 4194304 | tf_op jit(solution)/shard_map/part/pallas_call | solution.py:401
  54.2 1.0 %part.7 = (f32[64,1024]{1,0:T(8,128)S(1)}, f32[64,1024]{1,0:T(8,128)S(1)}, f32[64,128]{1,0:T(8,128)S(1)}) custom-call(bf16[16,8,128]{2,1,0:T(8,128)(2,1)S(1)} %all_to_all.15.index_ref.refs_0_, bf16[8192,1024]{1,0:T(8,128)(2,1)S(1)} %bitcast.7, bf16[8192,1024]{1,0:T(8,128)(2,1)S(1)} %bitcast.9, bf16[2,64,512]{2,1,0:T(8,128)(2,1)S(1)} %collective-permute-done.8.refs_3_, ...), custom_call_target="tpu_custom_call" | custom-call | flops 268435456 | bytes 4194304 | tf_op jit(solution)/shard_map/part/pallas_call | solution.py:401
  55.2 1.0 %part.8 = (f32[64,1024]{1,0:T(8,128)S(1)}, f32[64,1024]{1,0:T(8,128)S(1)}, f32[64,128]{1,0:T(8,128)S(1)}) custom-call(bf16[16,8,128]{2,1,0:T(8,128)(2,1)S(1)} %all_to_all.15.index_ref.refs_0_, bf16[8192,1024]{1,0:T(8,128)(2,1)S(1)} %bitcast.7, bf16[8192,1024]{1,0:T(8,128)(2,1)S(1)} %bitcast.9, bf16[2,64,512]{2,1,0:T(8,128)(2,1)S(1)} %pad_maximum_fusion.refs_3_, ...), custom_call_target="tpu_custom_call" | custom-call | flops 268435456 | bytes 4194304 | tf_op jit(solution)/shard_map/part/pallas_call | solution.py:401
  56.2 1.7 %part.9 = (f32[64,1024]{1,0:T(8,128)S(1)}, f32[64,1024]{1,0:T(8,128)S(1)}, f32[64,128]{1,0:T(8,128)S(1)}) custom-call(bf16[16,8,128]{2,1,0:T(8,128)(2,1)S(1)} %all_to_all.15.index_ref.refs_0_, bf16[8192,1024]{1,0:T(8,128)(2,1)S(1)} %bitcast.7, bf16[8192,1024]{1,0:T(8,128)(2,1)S(1)} %bitcast.9, bf16[2,64,512]{2,1,0:T(8,128)(2,1)S(1)} %collective-permute-done.7.refs_3_, ...), custom_call_target="tpu_custom_call" | custom-call | flops 268435456 | bytes 4194304 | tf_op jit(solution)/shard_map/part/pallas_call | solution.py:401
  58.0 1.0 %part.10 = (f32[64,1024]{1,0:T(8,128)S(1)}, f32[64,1024]{1,0:T(8,128)S(1)}, f32[64,128]{1,0:T(8,128)S(1)}) custom-call(bf16[16,8,128]{2,1,0:T(8,128)(2,1)S(1)} %all_to_all.15.index_ref.refs_0_, bf16[8192,1024]{1,0:T(8,128)(2,1)S(1)} %bitcast.7, bf16[8192,1024]{1,0:T(8,128)(2,1)S(1)} %bitcast.9, bf16[2,64,512]{2,1,0:T(8,128)(2,1)S(1)} %collective-permute-done.6.refs_3_, ...), custom_call_target="tpu_custom_call" | custom-call | flops 268435456 | bytes 4194304 | tf_op jit(solution)/shard_map/part/pallas_call | solution.py:401
  59.0 1.0 %part.11 = (f32[64,1024]{1,0:T(8,128)S(1)}, f32[64,1024]{1,0:T(8,128)S(1)}, f32[64,128]{1,0:T(8,128)S(1)}) custom-call(bf16[16,8,128]{2,1,0:T(8,128)(2,1)S(1)} %all_to_all.15.index_ref.refs_0_, bf16[8192,1024]{1,0:T(8,128)(2,1)S(1)} %bitcast.7, bf16[8192,1024]{1,0:T(8,128)(2,1)S(1)} %bitcast.9, bf16[2,64,512]{2,1,0:T(8,128)(2,1)S(1)} %collective-permute-done.2.refs_3_, ...), custom_call_target="tpu_custom_call" | custom-call | flops 268435456 | bytes 4194304 | tf_op jit(solution)/shard_map/part/pallas_call | solution.py:401
  60.0 1.7 %final.1 = bf16[2,32,1024]{2,1,0:T(8,128)(2,1)} custom-call(bf16[16,8,128]{2,1,0:T(8,128)(2,1)S(1)} %all_to_all.15.index_ref.refs_0_, bf16[8192,1024]{1,0:T(8,128)(2,1)S(1)} %bitcast.7, bf16[8192,1024]{1,0:T(8,128)(2,1)S(1)} %bitcast.9, bf16[2,64,512]{2,1,0:T(8,128)(2,1)S(1)} %collective-permute-done.3.refs_3_, f32[64,1024]{1,0:T(8,128)S(1)} %get-tuple-element.38.refs_4_, ...), custom_call_target="tpu_custom_call" | custom-call | flops 268435456 | bytes 4194304 | tf_op jit(solution)/shard_map/final/pallas_call | solution.py:401
  (38 shorter events, 0.1 us)
Async XLA Ops:
  0.0 53.1 %slice-start = ((s8[16777216]{0:T(1024)(128)(4,1)}), s8[4194304]{0:T(1024)(128)(4,1)S(1)}, s32[]{:S(2)}) async-start(s8[16777216]{0:T(1024)(128)(4,1)} %bitcast.6), calls=%async_computation.3 | async-start | bytes 8388608
  0.0 53.1 %slice-start.4 = ((s8[16777216]{0:T(1024)(128)(4,1)}), s8[4194304]{0:T(1024)(128)(4,1)S(1)}, s32[]{:S(2)}) async-start(s8[16777216]{0:T(1024)(128)(4,1)} %bitcast.8), calls=%async_computation.7 | async-start | bytes 8388608
  0.0 15.2 %copy-start.3 = (bf16[2,1,128,1024]{3,2,1,0:T(8,128)(2,1)S(1)}, bf16[2,1,128,1024]{3,2,1,0:T(8,128)(2,1)}, u32[]{:S(2)}) copy-start(bf16[2,1,128,1024]{3,2,1,0:T(8,128)(2,1)} %video_ref.1) | copy-start | bytes 1572868
  0.0 26.4 %copy-start = (bf16[1024,3072]{1,0:T(8,128)(2,1)S(1)}, bf16[1024,3072]{1,0:T(8,128)(2,1)}, u32[]{:S(2)}) copy-start(bf16[1024,3072]{1,0:T(8,128)(2,1)} %w_qkv_ref.1) | copy-start | bytes 18874372
  0.0 26.4 %copy-start.1 = (bf16[1024,1024]{1,0:T(8,128)(2,1)S(1)}, bf16[1024,1024]{1,0:T(8,128)(2,1)}, u32[]{:S(2)}) copy-start(bf16[1024,1024]{1,0:T(8,128)(2,1)} %w_out_ref.1) | copy-start | bytes 6291460
  0.0 39.4 %copy-start.2 = (bf16[1024,512]{1,0:T(8,128)(2,1)S(1)}, bf16[1024,512]{1,0:T(8,128)(2,1)}, u32[]{:S(2)}) copy-start(bf16[1024,512]{1,0:T(8,128)(2,1)} %w_proj_ref.1) | copy-start | bytes 3145732
  0.0 39.4 %copy-start.4 = (bf16[512]{0:T(512)(128)(2,1)S(1)}, bf16[512]{0:T(512)(128)(2,1)}, u32[]{:S(2)}) copy-start(bf16[512]{0:T(512)(128)(2,1)} %param.15) | copy-start | bytes 3076
  0.0 53.1 %slice-start.1 = ((s8[16777216]{0:T(1024)(128)(4,1)}), s8[4194304]{0:T(1024)(128)(4,1)S(1)}, s32[]{:S(2)}) async-start(s8[16777216]{0:T(1024)(128)(4,1)} %bitcast.6), calls=%async_computation.4 | async-start | bytes 8388608
  0.0 53.1 %slice-start.2 = ((s8[16777216]{0:T(1024)(128)(4,1)}), s8[4194304]{0:T(1024)(128)(4,1)S(1)}, s32[]{:S(2)}) async-start(s8[16777216]{0:T(1024)(128)(4,1)} %bitcast.6), calls=%async_computation.5 | async-start | bytes 8388608
  0.1 53.1 %slice-start.3 = ((s8[16777216]{0:T(1024)(128)(4,1)}), s8[4194304]{0:T(1024)(128)(4,1)S(1)}, s32[]{:S(2)}) async-start(s8[16777216]{0:T(1024)(128)(4,1)} %bitcast.6), calls=%async_computation.6 | async-start | bytes 8388608
  0.1 53.1 %slice-start.5 = ((s8[16777216]{0:T(1024)(128)(4,1)}), s8[4194304]{0:T(1024)(128)(4,1)S(1)}, s32[]{:S(2)}) async-start(s8[16777216]{0:T(1024)(128)(4,1)} %bitcast.8), calls=%async_computation.8 | async-start | bytes 8388608
  0.1 53.1 %slice-start.6 = ((s8[16777216]{0:T(1024)(128)(4,1)}), s8[4194304]{0:T(1024)(128)(4,1)S(1)}, s32[]{:S(2)}) async-start(s8[16777216]{0:T(1024)(128)(4,1)} %bitcast.8), calls=%async_computation.9 | async-start | bytes 8388608
  0.1 53.1 %slice-start.7 = ((s8[16777216]{0:T(1024)(128)(4,1)}), s8[4194304]{0:T(1024)(128)(4,1)S(1)}, s32[]{:S(2)}) async-start(s8[16777216]{0:T(1024)(128)(4,1)} %bitcast.8), calls=%async_computation.10 | async-start | bytes 8388608
  39.9 4.7 %collective-permute-start.4 = (bf16[64,512]{1,0:T(8,128)(2,1)S(1)}, bf16[64,512]{1,0:T(8,128)(2,1)S(1)}, u32[]{:S(2)}, u32[]{:S(2)}) collective-permute-start(bf16[64,512]{1,0:T(8,128)(2,1)S(1)} %project.1), channel_id=1, source_target_pairs={{0,4},{4,0},{8,12},{12,8},{1,5},{5,1},{9,13},{13,9},{2,6},{6,2},{1... | collective-permute-start | bytes 196616 | tf_op jit(solution)/shard_map/ppermute | solution.py:362
  39.9 8.1 %collective-permute-start = (bf16[64,512]{1,0:T(8,128)(2,1)S(1)}, bf16[64,512]{1,0:T(8,128)(2,1)S(1)}, u32[]{:S(2)}, u32[]{:S(2)}) collective-permute-start(bf16[64,512]{1,0:T(8,128)(2,1)S(1)} %project.1), channel_id=1, source_target_pairs={{0,8},{4,12},{8,0},{12,4},{1,9},{5,13},{9,1},{13,5},{2,10},{6,14},... | collective-permute-start | bytes 196616 | tf_op jit(solution)/shard_map/ppermute | solution.py:362
  41.1 7.0 %collective-permute-start.1 = (bf16[64,512]{1,0:T(8,128)(2,1)S(1)}, bf16[64,512]{1,0:T(8,128)(2,1)S(1)}, u32[]{:S(2)}, u32[]{:S(2)}) collective-permute-start(bf16[64,512]{1,0:T(8,128)(2,1)S(1)} %project.1), channel_id=1, source_target_pairs={{0,12},{4,8},{8,4},{12,0},{1,13},{5,9},{9,5},{13,1},{2,14},{6,10},... | collective-permute-start | bytes 196616 | tf_op jit(solution)/shard_map/ppermute | solution.py:362
  44.6 6.3 %collective-permute-start.5 = (bf16[2,64,512]{2,1,0:T(8,128)(2,1)S(1)}, bf16[2,64,512]{2,1,0:T(8,128)(2,1)S(1)}, u32[]{:S(2)}, u32[]{:S(2)}) collective-permute-start(bf16[2,64,512]{2,1,0:T(8,128)(2,1)S(1)} %pad_maximum_fusion.1.refs_3_), channel_id=1, source_target_pairs={{0,2},{2,0},{1,3},{3,1},{4,6},{6,4},{5,7},{7,5},{8,10},{10,8},{9,1... | collective-permute-start | bytes 393224 | tf_op jit(solution)/shard_map/ppermute | solution.py:362
  48.1 5.0 %collective-permute-start.2 = (bf16[2,64,512]{2,1,0:T(8,128)(2,1)S(1)}, bf16[2,64,512]{2,1,0:T(8,128)(2,1)S(1)}, u32[]{:S(2)}, u32[]{:S(2)}) collective-permute-start(bf16[2,64,512]{2,1,0:T(8,128)(2,1)S(1)} %pad_maximum_fusion.refs_3_), channel_id=1, source_target_pairs={{0,2},{2,0},{1,3},{3,1},{4,6},{6,4},{5,7},{7,5},{8,10},{10,8},{9,1... | collective-permute-start | bytes 393224 | tf_op jit(solution)/shard_map/ppermute | solution.py:362
  48.9 5.3 %collective-permute-start.8 = (bf16[2,64,512]{2,1,0:T(8,128)(2,1)S(1)}, bf16[2,64,512]{2,1,0:T(8,128)(2,1)S(1)}, u32[]{:S(2)}, u32[]{:S(2)}) collective-permute-start(bf16[2,64,512]{2,1,0:T(8,128)(2,1)S(1)} %pad_maximum_fusion.1.refs_3_), channel_id=1, source_target_pairs={{0,1},{1,0},{2,3},{3,2},{4,5},{5,4},{6,7},{7,6},{8,9},{9,8},{10,11... | collective-permute-start | bytes 393224 | tf_op jit(solution)/shard_map/ppermute | solution.py:362
  48.9 7.3 %collective-permute-start.7 = (bf16[2,64,512]{2,1,0:T(8,128)(2,1)S(1)}, bf16[2,64,512]{2,1,0:T(8,128)(2,1)S(1)}, u32[]{:S(2)}, u32[]{:S(2)}) collective-permute-start(bf16[2,64,512]{2,1,0:T(8,128)(2,1)S(1)} %pad_maximum_fusion.refs_3_), channel_id=1, source_target_pairs={{0,1},{1,0},{2,3},{3,2},{4,5},{5,4},{6,7},{7,6},{8,9},{9,8},{10,11... | collective-permute-start | bytes 393224 | tf_op jit(solution)/shard_map/ppermute | solution.py:362
  50.8 7.1 %collective-permute-start.6 = (bf16[2,64,512]{2,1,0:T(8,128)(2,1)S(1)}, bf16[2,64,512]{2,1,0:T(8,128)(2,1)S(1)}, u32[]{:S(2)}, u32[]{:S(2)}) collective-permute-start(bf16[2,64,512]{2,1,0:T(8,128)(2,1)S(1)} %collective-permute-done.5.refs_4_), channel_id=1, source_target_pairs={{0,1},{1,0},{2,3},{3,2},{4,5},{5,4},{6,7},{7,6},{8,9},{9,8},{10,11... | collective-permute-start | bytes 393224 | tf_op jit(solution)/shard_map/ppermute | solution.py:362
  53.1 6.8 %collective-permute-start.3 = (bf16[2,64,512]{2,1,0:T(8,128)(2,1)S(1)}, bf16[2,64,512]{2,1,0:T(8,128)(2,1)S(1)}, u32[]{:S(2)}, u32[]{:S(2)}) collective-permute-start(bf16[2,64,512]{2,1,0:T(8,128)(2,1)S(1)} %collective-permute-done.2.refs_3_), channel_id=1, source_target_pairs={{0,1},{1,0},{2,3},{3,2},{4,5},{5,4},{6,7},{7,6},{8,9},{9,8},{10,11... | collective-permute-start | bytes 393224 | tf_op jit(solution)/shard_map/ppermute | solution.py:362
